TPU v7x, 256 devices: a whole 4x4x8 slice. The times are simulated.
256 devices in a mesh: doc: 32 (over z, y_lo, core), head: 8 (over y_hi, x).
Axes of the slice: x: 4, y: 4 (y_hi: 2, y_lo: 2; y = y_hi * 2 + y_lo), z: 8, core: 2. Of those that a mesh axis runs over, the one named last changes fastest.
Arguments:
- queries: bfloat16 [16384, 4096], P('doc', 'head'), may hold values from -6 to 6
- local_keys: bfloat16 [16384, 4096], P('doc', 'head'), may hold values from -6 to 6
- local_values: bfloat16 [16384, 4096], P('doc', 'head'), may hold values from -6 to 6
- mem_keys: bfloat16 [32768, 4096], P('doc', 'head'), may hold values from -6 to 6
- mem_values: bfloat16 [32768, 4096], P('doc', 'head'), may hold values from -6 to 6
- offsets: int32 [32, 4], P('doc'), may hold values from 1 to 4
- mem_lengths: int32 [32], replicated, may hold values from 1 to 1024
- out_weight: bfloat16 [4096, 2048], P('head'), may hold values from -0.09375 to 0.09375
Outputs:
- mixed: bfloat16 [16384, 2048], P(('doc', 'head'))
All inputs are finite; a program needn't handle non-finite values.
Results may differ from a plain program's by a relative error of at most 0.015.
Values may be sent and summed in bfloat16 or wider, within the bound.
No kernel may reach another device: no remote copies, remote signals or barrier semaphores. Data moves between devices by JAX's collectives and lax.ppermute only.
A program may use at most 128 MiB of HBM per device.

v0:
```python
import math

import jax
import jax.numpy as jnp
from jax import lax
from jax.sharding import Mesh
from jax.sharding import PartitionSpec as P

DH = 128
HEAD = ("head_0", "head_1")
DOC_HEAD = ("doc", "head_0", "head_1")


def shifted(value, axis, steps):
    count = lax.axis_size(axis)
    pairs = [(source, (source + steps) % count) for source in range(count)]
    return lax.ppermute(value, axis, pairs)


def own_block(tiles, axes, sequence):
    inside = tiles.shape[1:]
    tiles = tiles.reshape(*(lax.axis_size(a) for a in axes), *inside)
    tiles = jnp.moveaxis(tiles, sequence, range(len(axes))).reshape(-1, *inside)
    for k in sequence:
        tiles = lax.psum_scatter(tiles, axes[k], scatter_dimension=0, tiled=True)
    return tiles[0]


def cut_along(x, dim, length):
    before, after = (x.shape[:dim], x.shape[dim + 1 :])
    return jnp.moveaxis(x.reshape(*before, length, -1, *after), dim, 0)


def sum_by_axis(x, axes, sequence, dim):
    length = lax.axis_size(axes)
    return own_block(cut_along(x, dim, length), axes, sequence)


def split_heads(rows, local_heads):
    return rows.reshape(rows.shape[0], local_heads, DH).transpose(1, 0, 2)


def per_device(
    queries, local_keys, local_values, mem_keys, mem_values, offsets, mem_lengths, out_weight
):
    doc_count = lax.axis_size("doc")
    document = lax.axis_index("doc")
    local_heads = queries.shape[1] // DH
    query_count = queries.shape[0]
    memory_rows = mem_keys.shape[0]
    slot_count = offsets.shape[1]
    score_scale = 1.0 / math.sqrt(DH)
    table_index = jnp.arange(mem_lengths.shape[0])
    causal = jnp.arange(query_count)[:, None] >= jnp.arange(query_count)[None, :]
    fetched = []
    carried_keys, carried_values = (mem_keys, mem_values)
    for step_index in range(slot_count):
        carried_keys, carried_values = shifted((carried_keys, carried_values), "doc", 1)
        fetched.append((carried_keys, carried_values))
    key_stack = jnp.stack([entry[0] for entry in fetched])
    value_stack = jnp.stack([entry[1] for entry in fetched])
    key_parts = [local_keys, mem_keys]
    value_parts = [local_values, mem_values]
    for slot in range(slot_count):
        chosen = offsets[0, slot] - 1
        key_parts.append(lax.dynamic_index_in_dim(key_stack, chosen, 0, keepdims=False))
        value_parts.append(lax.dynamic_index_in_dim(value_stack, chosen, 0, keepdims=False))
    key_all = jnp.concatenate(key_parts, axis=0)
    value_all = jnp.concatenate(value_parts, axis=0)
    owners = jnp.concatenate([document[None], (document - offsets[0]) % doc_count])
    owner_lengths = jnp.sum(
        jnp.where(owners[:, None] == table_index[None, :], mem_lengths[None, :], 0), axis=1
    )
    live_rows = (jnp.arange(memory_rows)[None, :] < owner_lengths[:, None]).reshape(1, -1)
    live_mask = jnp.concatenate(
        [causal, jnp.broadcast_to(live_rows, (query_count, live_rows.shape[1]))], axis=1
    )
    query_heads = split_heads(queries, local_heads)
    key_heads = split_heads(key_all, local_heads)
    value_heads = split_heads(value_all, local_heads)

    def one_head(operands):
        query_head, key_head, value_head = operands
        scores = (
            jnp.einsum("qd,kd->qk", query_head, key_head, preferred_element_type=jnp.float32)
            * score_scale
        )
        scores = jnp.where(live_mask, scores, -1e30)
        row_max = jnp.max(scores, axis=-1, keepdims=True)
        exponent = jnp.where(live_mask, jnp.exp(scores - row_max), 0.0)
        weights = (exponent / jnp.sum(exponent, axis=-1, keepdims=True)).astype(jnp.bfloat16)
        return jnp.einsum(
            "qk,kd->qd", weights, value_head, preferred_element_type=jnp.float32
        ).astype(jnp.bfloat16)

    head_out = lax.map(one_head, (query_heads, key_heads, value_heads))
    attended = head_out.transpose(1, 0, 2).reshape(query_count, local_heads * DH)
    mixed = sum_by_axis(
        jnp.dot(attended, out_weight, preferred_element_type=jnp.float32).astype(jnp.bfloat16),
        HEAD,
        (1, 0),
        0,
    ).astype(jnp.float32)
    return mixed.astype(jnp.bfloat16)


def solution(mesh):
    split = Mesh(mesh.devices.reshape(mesh.shape["doc"], 2, 4), ("doc", "head_0", "head_1"))
    placed = (
        P("doc", HEAD),
        P("doc", HEAD),
        P("doc", HEAD),
        P("doc", HEAD),
        P("doc", HEAD),
        P("doc", None),
        P(),
        P(HEAD, None),
    )
    return jax.shard_map(
        per_device, mesh=split, in_specs=placed, out_specs=P(DOC_HEAD, None), check_vma=False
    )
```

profile of v0, /device:TPU:1, one launch (start us, length us, event | category | flops | bytes accessed | tf_op | source)
XLA Modules:
  0.0 246.1 jit_solution(4670913972901156844)
XLA Ops:
  6.5 1.6 copy.24
  8.2 2.8 %collective-permute-start = (bf16[1024,512]{0,1:T(8,128)(2,1)S(1)}, bf16[1024,512]{0,1:T(8,128)(2,1)}, u32[]{:S(2)}, u32[]{:S(2)}) collective-permute-start(bf16[1024,512]{0,1:T(8,128)(2,1)S(1)} %copy.24), channel_id=1, source_target_pairs={{0,8},{8,16},{16,24},{24,32},{32,40},{40,48},{48,56},{56,64},{64,7... | collective-permute-start | bytes 3145736 | tf_op jit(solution)/shard_map/ppermute | solution.py:17
  10.9 2.3 copy.27
  13.2 9.4 %collective-permute-done = bf16[1024,512]{0,1:T(8,128)(2,1)} collective-permute-done((bf16[1024,512]{0,1:T(8,128)(2,1)S(1)}, bf16[1024,512]{0,1:T(8,128)(2,1)}, u32[]{:S(2)}, u32[]{:S(2)}) %collective-permute-start) | collective-permute-done | bytes 1048608 | tf_op jit(solution)/shard_map/ppermute | solution.py:17
  22.7 2.6 %collective-permute-start.1 = (bf16[1024,512]{0,1:T(8,128)(2,1)}, bf16[1024,512]{0,1:T(8,128)(2,1)}, u32[]{:S(2)}, u32[]{:S(2)}) collective-permute-start(bf16[1024,512]{0,1:T(8,128)(2,1)} %collective-permute-done), channel_id=1, source_target_pairs={{0,8},{8,16},{16,24},{24,32},{32,40},{40,48},{48,56},{56,64},{64,7... | collective-permute-start | bytes 3145736 | tf_op jit(solution)/shard_map/ppermute | solution.py:17
  25.3 8.8 %collective-permute-done.4 = bf16[1024,512]{0,1:T(8,128)(2,1)S(1)} collective-permute-done((bf16[1024,512]{0,1:T(8,128)(2,1)}, bf16[1024,512]{0,1:T(8,128)(2,1)S(1)}, u32[]{:S(2)}, u32[]{:S(2)}) %collective-permute-start.4) | collective-permute-done | bytes 1048608 | tf_op jit(solution)/shard_map/ppermute | solution.py:17
  34.0 1.0 copy-done.4
  35.0 2.4 collective-permute-start.5
  37.4 7.9 %collective-permute-done.1 = bf16[1024,512]{0,1:T(8,128)(2,1)} collective-permute-done((bf16[1024,512]{0,1:T(8,128)(2,1)}, bf16[1024,512]{0,1:T(8,128)(2,1)}, u32[]{:S(2)}, u32[]{:S(2)}) %collective-permute-start.1) | collective-permute-done | bytes 1048608 | tf_op jit(solution)/shard_map/ppermute | solution.py:17
  45.3 2.5 %collective-permute-start.2 = (bf16[1024,512]{0,1:T(8,128)(2,1)}, bf16[1024,512]{0,1:T(8,128)(2,1)}, u32[]{:S(2)}, u32[]{:S(2)}) collective-permute-start(bf16[1024,512]{0,1:T(8,128)(2,1)} %collective-permute-done.1), channel_id=1, source_target_pairs={{0,8},{8,16},{16,24},{24,32},{32,40},{40,48},{48,56},{56,64},{64,7... | collective-permute-start | bytes 3145736 | tf_op jit(solution)/shard_map/ppermute | solution.py:17
  47.7 8.6 %collective-permute-done.5 = bf16[1024,512]{0,1:T(8,128)(2,1)} collective-permute-done((bf16[1024,512]{0,1:T(8,128)(2,1)S(1)}, bf16[1024,512]{0,1:T(8,128)(2,1)}, u32[]{:S(2)}, u32[]{:S(2)}) %collective-permute-start.5) | collective-permute-done | bytes 1048608 | tf_op jit(solution)/shard_map/ppermute | solution.py:17
  56.4 2.6 %collective-permute-start.6 = (bf16[1024,512]{0,1:T(8,128)(2,1)}, bf16[1024,512]{0,1:T(8,128)(2,1)}, u32[]{:S(2)}, u32[]{:S(2)}) collective-permute-start(bf16[1024,512]{0,1:T(8,128)(2,1)} %collective-permute-done.5), channel_id=1, source_target_pairs={{0,8},{8,16},{16,24},{24,32},{32,40},{40,48},{48,56},{56,64},{64,7... | collective-permute-start | bytes 3145736 | tf_op jit(solution)/shard_map/ppermute | solution.py:17
  59.0 0.7 and_select_fusion
  59.6 0.1 pad_add_fusion.1
  59.7 0.8 select_reduce_fusion
  60.6 0.1 iota_compare_fusion.1
  60.7 0.1 iota_compare_fusion
  60.8 7.0 %collective-permute-done.2 = bf16[1024,512]{0,1:T(8,128)(2,1)} collective-permute-done((bf16[1024,512]{0,1:T(8,128)(2,1)}, bf16[1024,512]{0,1:T(8,128)(2,1)}, u32[]{:S(2)}, u32[]{:S(2)}) %collective-permute-start.2) | collective-permute-done | bytes 1048608 | tf_op jit(solution)/shard_map/ppermute | solution.py:17
  67.7 2.5 %collective-permute-start.3 = (bf16[1024,512]{0,1:T(8,128)(2,1)}, bf16[1024,512]{0,1:T(8,128)(2,1)}, u32[]{:S(2)}, u32[]{:S(2)}) collective-permute-start(bf16[1024,512]{0,1:T(8,128)(2,1)} %collective-permute-done.2), channel_id=1, source_target_pairs={{0,8},{8,16},{16,24},{24,32},{32,40},{40,48},{48,56},{56,64},{64,7... | collective-permute-start | bytes 3145736 | tf_op jit(solution)/shard_map/ppermute | solution.py:17
  70.2 8.8 %collective-permute-done.6 = bf16[1024,512]{0,1:T(8,128)(2,1)} collective-permute-done((bf16[1024,512]{0,1:T(8,128)(2,1)}, bf16[1024,512]{0,1:T(8,128)(2,1)}, u32[]{:S(2)}, u32[]{:S(2)}) %collective-permute-start.6) | collective-permute-done | bytes 1048608 | tf_op jit(solution)/shard_map/ppermute | solution.py:17
  79.0 2.5 %collective-permute-start.7 = (bf16[1024,512]{0,1:T(8,128)(2,1)}, bf16[1024,512]{0,1:T(8,128)(2,1)}, u32[]{:S(2)}, u32[]{:S(2)}) collective-permute-start(bf16[1024,512]{0,1:T(8,128)(2,1)} %collective-permute-done.6), channel_id=1, source_target_pairs={{0,8},{8,16},{16,24},{24,32},{32,40},{40,48},{48,56},{56,64},{64,7... | collective-permute-start | bytes 3145736 | tf_op jit(solution)/shard_map/ppermute | solution.py:17
  81.5 2.5 %pad_add_fusion = pred[512,5632]{1,0:T(32,128)(4,1)} fusion(pred[512,512]{1,0:T(32,128)(4,1)S(1)} %iota_compare_fusion, pred[5632]{0:T(1024)(128)(4,1)S(1)} %pad.5.clone), kind=kLoop, calls=%fused_computation.21 | loop fusion | flops 2883584 | bytes 3151360 | tf_op jit(solution)/shard_map/concatenate | solution.py:75
  83.9 0.6 fusion.22
  89.7 2.0 copy.26
  91.7 2.1 copy.23
  93.8 2.0 copy.22
  95.9 2.0 constant_dynamic-update-slice_fusion.12
  97.8 1.1 constant_dynamic-update-slice_fusion.6
  98.9 2.3 constant_dynamic-update-slice_fusion.11
  101.2 0.1 constant_dynamic-update-slice_fusion.5
  101.3 2.7 %pad_maximum_fusion = bf16[4,1024,512]{1,2,0:T(8,128)(2,1)S(1)} fusion(bf16[1,1024,512]{1,2,0:T(8,128)(2,1)} %bitcast.11, bf16[1,1024,512]{1,2,0:T(8,128)(2,1)} %bitcast.10, bf16[1,1024,512]{1,2,0:T(8,128)(2,1)} %bitcast.9, bf16[1,1024,512]{1,2,0:T(8,128)(2,1)} %bitcast.8), kind=kLoop, calls=%fused_computation.22 | loop fusion | flops 6291456 | bytes 8388608 | tf_op jit(solution)/shard_map/stack | solution.py:60
  104.0 2.1 pad_maximum_fusion.1
  106.1 2.7 %constant_dynamic-slice_fusion = (bf16[1,1024,512]{1,2,0:T(8,128)(2,1)}, bf16[1,1024,512]{1,2,0:T(8,128)(2,1)}, bf16[1,1024,512]{1,2,0:T(8,128)(2,1)}, bf16[1,10...) fusion(bf16[4,1024,512]{1,2,0:T(8,128)(2,1)S(1)} %pad_maximum_f, ...), kind=kLoop, calls=%fused_computation.43 | loop fusion | bytes 16777232 | tf_op jit(solution)/shard_map/jit(dynamic_index_in_dim)/dynamic_slice | solution.py:67
  108.8 2.4 constant_dynamic-update-slice_fusion.10
  111.2 2.3 constant_dynamic-update-slice_fusion.9
  113.5 2.3 constant_dynamic-update-slice_fusion.8
  115.8 1.1 constant_dynamic-update-slice_fusion.7
  116.9 0.1 constant_dynamic-update-slice_fusion.4
  117.0 0.1 constant_dynamic-update-slice_fusion.3
  117.1 0.1 constant_dynamic-update-slice_fusion.2
  117.1 0.1 constant_dynamic-update-slice_fusion.1
  117.2 2.5 %copy-done.2 = bf16[5632,4,128]{0,2,1:T(8,128)(2,1)} copy-done((bf16[5632,4,128]{0,2,1:T(8,128)(2,1)}, bf16[5632,4,128]{0,2,1:T(8,128)(2,1)S(1)}, u32[]{:S(2)}) %copy-start.2) | copy-done | bytes 5767192
  119.7 57.5 %while.10 = (s32[]{:T(128)}, bf16[4,512,128]{1,2,0:T(8,128)(2,1)S(1)}, bf16[4,512,128]{1,2,0:T(8,128)(2,1)}, bf16[4,5632,128]{1,2,0:T(8,128)(2,1)}, pred[512,563...) while((s32[]{:T(128)}, bf16[4,512,128]{1,2,0:T(8,128)(2,1)S(1)}, ...), condition=%wide.region_4.5_spmd, body=%wide.region_1.4_spmd.sunk | while | flops 1516829696 | bytes 58469996 | solution.py:96
  119.7 5.2 %fusion.30 = (f32[512]{0:T(512)S(1)}, f32[512,5632]{1,0:T(8,128)S(1)}) fusion(pred[512,5632]{1,0:T(32,128)(4,1)} %get-tuple-element.139, bf16[4,5632,128]{1,2,0:T(8,128)(2,1)} %get-tuple-element.138, s32[]{:T(128)} %get-tuple-element.128, bf16[4,512,128]{1,2,0:T(8,128)(2,1)} %get-tuple-element.137), kind=kOutput, calls=%fused_computation.3.clone.1 | convolution fusion | flops 746847744 | bytes 15993856 | tf_op jit(solution)/shard_map/while/body/eval_jaxpr/qd,kd->qk/dot_general | solution.py:85
  124.9 3.8 %fusion.31 = f32[512]{0:T(512)S(1)} fusion(pred[512,5632]{1,0:T(32,128)(4,1)S(1)} %copy-done.1, f32[512,5632]{1,0:T(8,128)S(1)} %get-tuple-element.119, f32[512]{0:T(512)S(1)} %get-tuple-element.120), kind=kLoop, calls=%fused_computation.4.clone.1 | loop fusion | flops 14417408 | bytes 14422016 | tf_op jit(solution)/shard_map/while/body/eval_jaxpr/reduce_sum | solution.py:91
  128.8 5.1 %fusion.32 = bf16[1,512,128]{2,1,0:T(8,128)(2,1)S(1)} fusion(bf16[4,5632,128]{1,2,0:T(8,128)(2,1)} %get-tuple-element.140, s32[]{:T(128)} %get-tuple-element.128, pred[512,5632]{1,0:T(32,128)(4,1)S(1)} %copy-done.1, f32[512,5632]{1,0:T(8,128)S(1)} %get-tuple-element.119, f32[512]{0:T(512)S(1)} %fusion.31, f32[512]{0:T(512)S(1)} %get-tuple-element.120), kind=kOutput, calls=%fused_computation.12.clone.1 | convolution fusion | flops 755564544 | bytes 15995392 | tf_op jit(solution)/shard_map/while/body/eval_jaxpr/qk,kd->qd/dot_general | solution.py:92
  133.9 0.1 copy.40
  134.1 5.2 %fusion.30 = (f32[512]{0:T(512)S(1)}, f32[512,5632]{1,0:T(8,128)S(1)}) fusion(pred[512,5632]{1,0:T(32,128)(4,1)} %get-tuple-element.139, bf16[4,5632,128]{1,2,0:T(8,128)(2,1)} %get-tuple-element.138, s32[]{:T(128)} %get-tuple-element.128, bf16[4,512,128]{1,2,0:T(8,128)(2,1)} %get-tuple-element.137), kind=kOutput, calls=%fused_computation.3.clone.1 | convolution fusion | flops 746847744 | bytes 15993856 | tf_op jit(solution)/shard_map/while/body/eval_jaxpr/qd,kd->qk/dot_general | solution.py:85
  139.3 3.8 %fusion.31 = f32[512]{0:T(512)S(1)} fusion(pred[512,5632]{1,0:T(32,128)(4,1)S(1)} %copy-done.1, f32[512,5632]{1,0:T(8,128)S(1)} %get-tuple-element.119, f32[512]{0:T(512)S(1)} %get-tuple-element.120), kind=kLoop, calls=%fused_computation.4.clone.1 | loop fusion | flops 14417408 | bytes 14422016 | tf_op jit(solution)/shard_map/while/body/eval_jaxpr/reduce_sum | solution.py:91
  143.1 5.1 %fusion.32 = bf16[1,512,128]{2,1,0:T(8,128)(2,1)S(1)} fusion(bf16[4,5632,128]{1,2,0:T(8,128)(2,1)} %get-tuple-element.140, s32[]{:T(128)} %get-tuple-element.128, pred[512,5632]{1,0:T(32,128)(4,1)S(1)} %copy-done.1, f32[512,5632]{1,0:T(8,128)S(1)} %get-tuple-element.119, f32[512]{0:T(512)S(1)} %fusion.31, f32[512]{0:T(512)S(1)} %get-tuple-element.120), kind=kOutput, calls=%fused_computation.12.clone.1 | convolution fusion | flops 755564544 | bytes 15995392 | tf_op jit(solution)/shard_map/while/body/eval_jaxpr/qk,kd->qd/dot_general | solution.py:92
  148.3 0.1 copy.40
  148.5 5.2 %fusion.30 = (f32[512]{0:T(512)S(1)}, f32[512,5632]{1,0:T(8,128)S(1)}) fusion(pred[512,5632]{1,0:T(32,128)(4,1)} %get-tuple-element.139, bf16[4,5632,128]{1,2,0:T(8,128)(2,1)} %get-tuple-element.138, s32[]{:T(128)} %get-tuple-element.128, bf16[4,512,128]{1,2,0:T(8,128)(2,1)} %get-tuple-element.137), kind=kOutput, calls=%fused_computation.3.clone.1 | convolution fusion | flops 746847744 | bytes 15993856 | tf_op jit(solution)/shard_map/while/body/eval_jaxpr/qd,kd->qk/dot_general | solution.py:85
  153.7 3.8 %fusion.31 = f32[512]{0:T(512)S(1)} fusion(pred[512,5632]{1,0:T(32,128)(4,1)S(1)} %copy-done.1, f32[512,5632]{1,0:T(8,128)S(1)} %get-tuple-element.119, f32[512]{0:T(512)S(1)} %get-tuple-element.120), kind=kLoop, calls=%fused_computation.4.clone.1 | loop fusion | flops 14417408 | bytes 14422016 | tf_op jit(solution)/shard_map/while/body/eval_jaxpr/reduce_sum | solution.py:91
  157.5 5.1 %fusion.32 = bf16[1,512,128]{2,1,0:T(8,128)(2,1)S(1)} fusion(bf16[4,5632,128]{1,2,0:T(8,128)(2,1)} %get-tuple-element.140, s32[]{:T(128)} %get-tuple-element.128, pred[512,5632]{1,0:T(32,128)(4,1)S(1)} %copy-done.1, f32[512,5632]{1,0:T(8,128)S(1)} %get-tuple-element.119, f32[512]{0:T(512)S(1)} %fusion.31, f32[512]{0:T(512)S(1)} %get-tuple-element.120), kind=kOutput, calls=%fused_computation.12.clone.1 | convolution fusion | flops 755564544 | bytes 15995392 | tf_op jit(solution)/shard_map/while/body/eval_jaxpr/qk,kd->qd/dot_general | solution.py:92
  162.7 0.1 copy.40
  162.8 5.2 %fusion.30 = (f32[512]{0:T(512)S(1)}, f32[512,5632]{1,0:T(8,128)S(1)}) fusion(pred[512,5632]{1,0:T(32,128)(4,1)} %get-tuple-element.139, bf16[4,5632,128]{1,2,0:T(8,128)(2,1)} %get-tuple-element.138, s32[]{:T(128)} %get-tuple-element.128, bf16[4,512,128]{1,2,0:T(8,128)(2,1)} %get-tuple-element.137), kind=kOutput, calls=%fused_computation.3.clone.1 | convolution fusion | flops 746847744 | bytes 15993856 | tf_op jit(solution)/shard_map/while/body/eval_jaxpr/qd,kd->qk/dot_general | solution.py:85
  168.1 3.8 %fusion.31 = f32[512]{0:T(512)S(1)} fusion(pred[512,5632]{1,0:T(32,128)(4,1)S(1)} %copy-done.1, f32[512,5632]{1,0:T(8,128)S(1)} %get-tuple-element.119, f32[512]{0:T(512)S(1)} %get-tuple-element.120), kind=kLoop, calls=%fused_computation.4.clone.1 | loop fusion | flops 14417408 | bytes 14422016 | tf_op jit(solution)/shard_map/while/body/eval_jaxpr/reduce_sum | solution.py:91
  171.9 5.1 %fusion.32 = bf16[1,512,128]{2,1,0:T(8,128)(2,1)S(1)} fusion(bf16[4,5632,128]{1,2,0:T(8,128)(2,1)} %get-tuple-element.140, s32[]{:T(128)} %get-tuple-element.128, pred[512,5632]{1,0:T(32,128)(4,1)S(1)} %copy-done.1, f32[512,5632]{1,0:T(8,128)S(1)} %get-tuple-element.119, f32[512]{0:T(512)S(1)} %fusion.31, f32[512]{0:T(512)S(1)} %get-tuple-element.120), kind=kOutput, calls=%fused_computation.12.clone.1 | convolution fusion | flops 755564544 | bytes 15995392 | tf_op jit(solution)/shard_map/while/body/eval_jaxpr/qk,kd->qd/dot_general | solution.py:92
  177.0 0.1 copy.40
  177.2 1.3 convolution_convert_fusion
  178.5 1.5 copy.33
  180.0 0.0 reduce-scatter.5.cloned.1.call-start
  180.0 35.8 %reduce-scatter.3.cloned.1.call-done = bf16[2,64,2048]{2,1,0:T(8,128)(2,1)} async-done(((bf16[8,64,2048]{2,1,0:T(8,128)(2,1)}), bf16[2,64,2048]{2,1,0:T(8,128)(2,1)}) %reduce-scatter.3.cloned.1.call-update) | async-done | bytes 524304 | tf_op jit(solution)/shard_map/reduce_scatter | solution.py:25
  215.8 23.4 %reduce-scatter.5.cloned.1.call-done = bf16[1,64,2048]{2,1,0:T(8,128)(2,1)} async-done(((bf16[2,64,2048]{2,1,0:T(8,128)(2,1)}), bf16[1,64,2048]{2,1,0:T(8,128)(2,1)}) %reduce-scatter.5.cloned.1.call-update) | async-done | bytes 262160 | tf_op jit(solution)/shard_map/reduce_scatter | solution.py:25
  (33 shorter events, 0.2 us)
Async XLA Ops:
  6.5 170.7 %copy-start = (bf16[512,2048]{1,0:T(8,128)(2,1)S(1)}, bf16[512,2048]{1,0:T(8,128)(2,1)}, u32[]{:S(2)}) copy-start(bf16[512,2048]{1,0:T(8,128)(2,1)} %param.17) | copy-start | bytes 6291460
  6.5 77.4 %copy-start.6 = (s32[1,4]{1,0:T(1,128)S(1)}, s32[1,4]{1,0:T(1,128)}, u32[]{:S(2)}) copy-start(s32[1,4]{1,0:T(1,128)} %param.15) | copy-start | bytes 52
  6.5 209.3 %reduce-scatter.3.cloned.1.call-start = ((), (), s32[]{:S(2)}) async-start(), calls=%async_computation.2 | async-start | bytes 2621440 | tf_op jit(solution)/shard_map/reduce_scatter | solution.py:25
  8.2 14.5 %collective-permute-start = (bf16[1024,512]{0,1:T(8,128)(2,1)S(1)}, bf16[1024,512]{0,1:T(8,128)(2,1)}, u32[]{:S(2)}, u32[]{:S(2)}) collective-permute-start(bf16[1024,512]{0,1:T(8,128)(2,1)S(1)} %copy.24), channel_id=1, source_target_pairs={{0,8},{8,16},{16,24},{24,32},{32,40},{40,48},{48,56},{56,64},{64,7... | collective-permute-start | bytes 3145736 | tf_op jit(solution)/shard_map/ppermute | solution.py:17
  13.2 20.8 %collective-permute-start.4 = (bf16[1024,512]{0,1:T(8,128)(2,1)}, bf16[1024,512]{0,1:T(8,128)(2,1)S(1)}, u32[]{:S(2)}, u32[]{:S(2)}) collective-permute-start(bf16[1024,512]{0,1:T(8,128)(2,1)} %copy.27), channel_id=1, source_target_pairs={{0,8},{8,16},{16,24},{24,32},{32,40},{40,48},{48,56},{56,64},{64,7... | collective-permute-start | bytes 3145736 | tf_op jit(solution)/shard_map/ppermute | solution.py:17
  22.7 22.6 %collective-permute-start.1 = (bf16[1024,512]{0,1:T(8,128)(2,1)}, bf16[1024,512]{0,1:T(8,128)(2,1)}, u32[]{:S(2)}, u32[]{:S(2)}) collective-permute-start(bf16[1024,512]{0,1:T(8,128)(2,1)} %collective-permute-done), channel_id=1, source_target_pairs={{0,8},{8,16},{16,24},{24,32},{32,40},{40,48},{48,56},{56,64},{64,7... | collective-permute-start | bytes 3145736 | tf_op jit(solution)/shard_map/ppermute | solution.py:17
  34.0 1.0 copy-start.4
  35.0 21.4 %collective-permute-start.5 = (bf16[1024,512]{0,1:T(8,128)(2,1)S(1)}, bf16[1024,512]{0,1:T(8,128)(2,1)}, u32[]{:S(2)}, u32[]{:S(2)}) collective-permute-start(bf16[1024,512]{0,1:T(8,128)(2,1)S(1)} %collective-permute-done.4), channel_id=1, source_target_pairs={{0,8},{8,16},{16,24},{24,32},{32,40},{40,48},{48,56},{56,64},{64,7... | collective-permute-start | bytes 3145736 | tf_op jit(solution)/shard_map/ppermute | solution.py:17
  45.3 22.5 %collective-permute-start.2 = (bf16[1024,512]{0,1:T(8,128)(2,1)}, bf16[1024,512]{0,1:T(8,128)(2,1)}, u32[]{:S(2)}, u32[]{:S(2)}) collective-permute-start(bf16[1024,512]{0,1:T(8,128)(2,1)} %collective-permute-done.1), channel_id=1, source_target_pairs={{0,8},{8,16},{16,24},{24,32},{32,40},{40,48},{48,56},{56,64},{64,7... | collective-permute-start | bytes 3145736 | tf_op jit(solution)/shard_map/ppermute | solution.py:17
  56.4 22.6 %collective-permute-start.6 = (bf16[1024,512]{0,1:T(8,128)(2,1)}, bf16[1024,512]{0,1:T(8,128)(2,1)}, u32[]{:S(2)}, u32[]{:S(2)}) collective-permute-start(bf16[1024,512]{0,1:T(8,128)(2,1)} %collective-permute-done.5), channel_id=1, source_target_pairs={{0,8},{8,16},{16,24},{24,32},{32,40},{40,48},{48,56},{56,64},{64,7... | collective-permute-start | bytes 3145736 | tf_op jit(solution)/shard_map/ppermute | solution.py:17
  67.7 33.5 %collective-permute-start.3 = (bf16[1024,512]{0,1:T(8,128)(2,1)}, bf16[1024,512]{0,1:T(8,128)(2,1)}, u32[]{:S(2)}, u32[]{:S(2)}) collective-permute-start(bf16[1024,512]{0,1:T(8,128)(2,1)} %collective-permute-done.2), channel_id=1, source_target_pairs={{0,8},{8,16},{16,24},{24,32},{32,40},{40,48},{48,56},{56,64},{64,7... | collective-permute-start | bytes 3145736 | tf_op jit(solution)/shard_map/ppermute | solution.py:17
  79.0 25.0 %collective-permute-start.7 = (bf16[1024,512]{0,1:T(8,128)(2,1)}, bf16[1024,512]{0,1:T(8,128)(2,1)}, u32[]{:S(2)}, u32[]{:S(2)}) collective-permute-start(bf16[1024,512]{0,1:T(8,128)(2,1)} %collective-permute-done.6), channel_id=1, source_target_pairs={{0,8},{8,16},{16,24},{24,32},{32,40},{40,48},{48,56},{56,64},{64,7... | collective-permute-start | bytes 3145736 | tf_op jit(solution)/shard_map/ppermute | solution.py:17
  101.2 2.8 %copy-start.5 = (bf16[1024,512]{0,1:T(8,128)(2,1)S(1)}, bf16[1024,512]{0,1:T(8,128)(2,1)}, u32[]{:S(2)}) copy-start(bf16[1024,512]{0,1:T(8,128)(2,1)} %copy-done.4) | copy-start | bytes 3145732
  108.8 7.0 %copy-start.3 = (bf16[1,1024,512]{1,2,0:T(8,128)(2,1)S(1)}, bf16[1,1024,512]{1,2,0:T(8,128)(2,1)}, u32[]{:S(2)}) copy-start(bf16[1,1024,512]{1,2,0:T(8,128)(2,1)} %get-tuple-element.64) | copy-start | bytes 3145732
  115.8 3.9 %copy-start.7 = (bf16[4,512,128]{1,2,0:T(8,128)(2,1)S(1)}, bf16[4,512,128]{1,2,0:T(8,128)(2,1)}, u32[]{:S(2)}) copy-start(bf16[4,512,128]{1,2,0:T(8,128)(2,1)} %custom-call.2) | copy-start | bytes 1572868
  117.2 2.5 %copy-start.2 = (bf16[5632,4,128]{0,2,1:T(8,128)(2,1)}, bf16[5632,4,128]{0,2,1:T(8,128)(2,1)S(1)}, u32[]{:S(2)}) copy-start(bf16[5632,4,128]{0,2,1:T(8,128)(2,1)S(1)} %constant_dynamic-update-slice_fusion.1) | copy-start | bytes 17301508
  119.7 5.2 %copy-start.1 = (pred[512,5632]{1,0:T(32,128)(4,1)S(1)}, pred[512,5632]{1,0:T(32,128)(4,1)}, u32[]{:S(2)}) copy-start(pred[512,5632]{1,0:T(32,128)(4,1)} %get-tuple-element.139) | copy-start | bytes 8650756 | tf_op jit(solution)/shard_map/while
  134.1 5.2 %copy-start.1 = (pred[512,5632]{1,0:T(32,128)(4,1)S(1)}, pred[512,5632]{1,0:T(32,128)(4,1)}, u32[]{:S(2)}) copy-start(pred[512,5632]{1,0:T(32,128)(4,1)} %get-tuple-element.139) | copy-start | bytes 8650756 | tf_op jit(solution)/shard_map/while
  148.5 5.2 %copy-start.1 = (pred[512,5632]{1,0:T(32,128)(4,1)S(1)}, pred[512,5632]{1,0:T(32,128)(4,1)}, u32[]{:S(2)}) copy-start(pred[512,5632]{1,0:T(32,128)(4,1)} %get-tuple-element.139) | copy-start | bytes 8650756 | tf_op jit(solution)/shard_map/while
  162.8 5.2 %copy-start.1 = (pred[512,5632]{1,0:T(32,128)(4,1)S(1)}, pred[512,5632]{1,0:T(32,128)(4,1)}, u32[]{:S(2)}) copy-start(pred[512,5632]{1,0:T(32,128)(4,1)} %get-tuple-element.139) | copy-start | bytes 8650756 | tf_op jit(solution)/shard_map/while
  180.0 59.3 %reduce-scatter.5.cloned.1.call-start = ((), (), s32[]{:S(2)}) async-start(), calls=%async_computation.3 | async-start | bytes 786432 | tf_op jit(solution)/shard_map/reduce_scatter | solution.py:25
Sparse Core Ops, SparseCore 0:
  180.1 35.6 reduce-scatter.2
  218.3 20.9 reduce-scatter.4
where the time goes:
time: 247 us; the launch traced here: 246 us
  waiting for transfers between devices  110 us (45%)
  matrix products  42.7 us (17%)
  local copies, waits for them, and re-layouts  32.8 us (13%)
  other arithmetic  24.3 us (10%)
  between operations  18.7 us (8%)
  starting transfers between devices  17.8 us (7%)
    reduce_scatter x2, waiting for transfers between devices, own_block(): tiles = lax.psum_scatter(tiles, axes[k], scatter_dimension=0, tiled=True)  59.2 us
    ppermute x8, waiting for transfers between devices, shifted(): return lax.ppermute(value, axis, pairs)  50.4 us
    unnamed x29, local copies, waits for them, and re-layouts  26.2 us
    dot_general x4, matrix products, one_head(): jnp.einsum('qd,kd->qk', query_head, key_head, preferred_element_type=jnp....  20.8 us
    dot_general x4, matrix products, one_head(): jnp.einsum('qk,kd->qd', weights, value_head, preferred_element_type=jnp.f...  20.6 us
    ppermute x8, starting transfers between devices, shifted(): return lax.ppermute(value, axis, pairs)  17.8 us
    reduce_sum x4, other arithmetic, one_head(): jnp.sum(exponent, axis=-1, keepdims=True)  15.4 us
  transfers between devices with their start and end apart: 10, of which 8 were waited for; matrix products, arithmetic and copies ran while one was open for 9% of the time, Pallas kernels for 0%

commit v1 on v0

v1 whole, which is shorter than its diff:
```python
import math

import jax
import jax.numpy as jnp
from jax import lax
from jax.experimental import pallas as pl
from jax.experimental.pallas import tpu as pltpu
from jax.sharding import Mesh
from jax.sharding import PartitionSpec as P

DH = 128
DOC = ("z", "yl", "core")
HEAD = ("yh", "x")
NEG = -1e30
KEY_CHUNK = 512
TAIL = 16
SCALE = math.log2(math.e) / math.sqrt(DH)


def shift(value, axis, steps):
    count = lax.axis_size(axis)
    return lax.ppermute(value, axis, [(i, (i + steps) % count) for i in range(count)])


def swap(value, axis):
    return lax.ppermute(value, axis, [(0, 1), (1, 0)])


def part_ways(value):
    count = lax.axis_size("x")
    up = [(i, (i + 1) % count) for i in range(count)]
    down = [(count + i, count + (i - 1) % count) for i in range(count)]
    return lax.ppermute(value, ("core", "x"), up + down)


def lanes(x, width):
    return jnp.concatenate([x] * (width // DH), axis=1)


def scores_of(q, k):
    return lax.dot_general(q, k, (((1,), (1,)), ((), ())), preferred_element_type=jnp.float32) * SCALE


def with_ones(v):
    return jnp.concatenate([v, jnp.ones(v.shape, v.dtype)], axis=1)


def absorb(s, v, m_ref, acc_ref):
    m_old = m_ref[...]
    m_new = jnp.maximum(m_old, jnp.max(s, axis=1, keepdims=True))
    p = jnp.exp2(s - lanes(m_new, s.shape[1])).astype(jnp.bfloat16)
    pv = jnp.dot(p, with_ones(v), preferred_element_type=jnp.float32)
    acc_ref[...] = acc_ref[...] * lanes(jnp.exp2(m_old - m_new), 2 * DH) + pv
    m_ref[...] = m_new


def reset(m_ref, acc_ref):
    m_ref[...] = jnp.full(m_ref.shape, NEG, jnp.float32)
    acc_ref[...] = jnp.zeros(acc_ref.shape, jnp.float32)


def log2_count(count):
    return jnp.where(count >= 4, 2.0, jnp.where(count >= 3, math.log2(3), jnp.where(count >= 2, 1.0, 0.0)))


class Memory:
    def __init__(self, keys, values, buffers, sems, length, count):
        self.keys, self.values, self.buffers, self.sems = keys, values, buffers, sems
        self.length, self.bias = jnp.where(count > 0, length, 0), log2_count(count)
        self.chunks = range(0, keys.shape[0], KEY_CHUNK)

    def copies(self, h, j):
        rows, cols = pl.ds(self.chunks[j], KEY_CHUNK), pl.ds(pl.multiple_of(h * DH, DH), DH)
        return [
            pltpu.make_async_copy(src.at[rows, cols], self.buffers.at[i, h, rows, :], self.sems.at[i, h, j])
            for i, src in enumerate((self.keys, self.values))
        ]

    def fetch(self, h):
        for j, start in enumerate(self.chunks):

            @pl.when(self.length > start)
            def _(j=j):
                for copy in self.copies(h, j):
                    copy.start()

    def use(self, h, q, m_ref, acc_ref):
        for j, start in enumerate(self.chunks):

            @pl.when(self.length > start)
            def _(j=j, start=start):
                for copy in self.copies(h, j):
                    copy.wait()
                row = lax.broadcasted_iota(jnp.int32, (1, KEY_CHUNK), 1) + start
                bias = jnp.where(row < self.length, self.bias, NEG)
                rows = pl.ds(start, KEY_CHUNK)
                absorb(scores_of(q, self.buffers[0, h, rows, :]) + bias, self.buffers[1, h, rows, :], m_ref, acc_ref)


def finish(h, rows, put, level_ref, m_ref, acc_ref):
    total = acc_ref[:, DH:]
    seen = total > 0
    safe = jnp.where(seen, total, 1.0)
    put((acc_ref[:, :DH] / safe).astype(jnp.bfloat16))
    rest = jnp.where(seen, m_ref[...] + jnp.log2(safe), NEG).T[:1, :]
    for i in range(3):
        term = rest.astype(jnp.bfloat16).astype(jnp.float32)
        level_ref[pl.ds(3 * h + i, 1), :rows] = term
        rest = rest - term


def home_kernel(offsets, lengths, q_ref, lk_ref, lv_ref, *refs, partner):
    k0, v0, k1, v1, out_ref, m_ref, acc_ref, level_ref, buf0, buf1, sem0, sem1 = refs
    heads = q_ref.shape[1] // DH
    core, document, yh = lax.axis_index("core"), lax.axis_index(DOC), lax.axis_index("yh")
    rows = q_ref.shape[0] // 2
    first = (1 - yh if partner else yh) * rows
    count = sum(jnp.where((offsets[0, i] == 1) & (core == 1), 1, 0) for i in range(offsets.shape[1]))
    memories = [
        Memory(k0, v0, buf0, sem0, lengths[document], jnp.int32(1)),
        Memory(k1, v1, buf1, sem1, lengths[document + 1 - 2 * core], count),
    ]
    for h in range(heads):
        for memory in memories:
            memory.fetch(h)
    level_ref[...] = jnp.zeros(level_ref.shape, jnp.float32)

    def one_head(h, carry):
        cols = pl.ds(pl.multiple_of(h * DH, DH), DH)
        reset(m_ref, acc_ref)
        q = q_ref[pl.ds(pl.multiple_of(first, rows), rows), cols]
        s = scores_of(q, lk_ref[:, cols])
        row = lax.broadcasted_iota(jnp.int32, s.shape, 0) + first
        s = jnp.where(row >= lax.broadcasted_iota(jnp.int32, s.shape, 1), s, NEG)
        absorb(s, lv_ref[:, cols], m_ref, acc_ref)
        for memory in memories:
            memory.use(h, q, m_ref, acc_ref)

        def put(o):
            out_ref[pl.ds(0, rows), cols] = o

        finish(h, rows, put, level_ref, m_ref, acc_ref)
        return carry

    lax.fori_loop(0, heads, one_head, 0)
    out_ref[pl.ds(rows, TAIL), :] = level_ref[...].astype(jnp.bfloat16)


def guest_kernel(lengths, q_ref, k0, v0, k1, v1, out_ref, m_ref, acc_ref, level_ref, buf0, buf1, sem0, sem1, *, back):
    heads, rows = q_ref.shape[1] // DH, q_ref.shape[0] - TAIL
    core, document = lax.axis_index("core"), lax.axis_index(DOC)
    table = q_ref[pl.ds(rows, TAIL), pl.ds(0, DH)].astype(jnp.float32)
    own = jnp.sum(jnp.where(table == back, 1.0, 0.0)).astype(jnp.int32)
    wanted = (back - 1 + 2 * core).astype(jnp.float32)
    other = jnp.sum(jnp.where(table == wanted, 1.0, 0.0)).astype(jnp.int32)
    memories = [
        Memory(k0, v0, buf0, sem0, lengths[document], own),
        Memory(k1, v1, buf1, sem1, lengths[document + 1 - 2 * core], other),
    ]
    for h in range(heads):
        for memory in memories:
            memory.fetch(h)
    level_ref[...] = jnp.zeros(level_ref.shape, jnp.float32)

    def one_head(h, carry):
        cols = pl.ds(pl.multiple_of(h * DH, DH), DH)
        reset(m_ref, acc_ref)
        q = q_ref[pl.ds(0, rows), cols]
        for memory in memories:
            memory.use(h, q, m_ref, acc_ref)

        def put(o):
            out_ref[pl.ds(0, rows), cols] = o

        finish(h, rows, put, level_ref, m_ref, acc_ref)
        return carry

    lax.fori_loop(0, heads, one_head, 0)
    out_ref[pl.ds(rows, TAIL), :] = level_ref[...].astype(jnp.bfloat16)


def whole(shape):
    return pl.BlockSpec(shape, lambda *_: (0,) * len(shape))


def anywhere():
    return pl.BlockSpec(memory_space=pl.ANY)


def attention(kernel, scalars, blocks, memory, rows, out_shape):
    heads = blocks[0].shape[1] // DH
    mem_rows, width = memory[0].shape
    buffer = pltpu.VMEM((2, heads, mem_rows, DH), jnp.bfloat16)
    sems = pltpu.SemaphoreType.DMA((2, heads, mem_rows // KEY_CHUNK))
    return pl.pallas_call(
        kernel,
        grid_spec=pltpu.PrefetchScalarGridSpec(
            num_scalar_prefetch=len(scalars),
            grid=(1,),
            in_specs=[whole(a.shape) for a in blocks] + [anywhere()] * 4,
            out_specs=whole(out_shape),
            scratch_shapes=[
                pltpu.VMEM((rows, DH), jnp.float32),
                pltpu.VMEM((rows, 2 * DH), jnp.float32),
                pltpu.VMEM((TAIL, width), jnp.float32),
                buffer,
                buffer,
                sems,
                sems,
            ],
        ),
        out_shape=jax.ShapeDtypeStruct(out_shape, jnp.bfloat16),
    )(*scalars, *blocks, *memory)


def merge_kernel(home_ref, far_ref, near_ref, out_ref, share_ref):
    rows, width = out_ref.shape
    heads = width // DH
    parts = [home_ref[...], far_ref[...], near_ref[...]]
    tails = [part[rows:, :rows].astype(jnp.float32) for part in parts]
    for h in range(heads):
        levels = [tail[3 * h : 3 * h + 1] + tail[3 * h + 1 : 3 * h + 2] + tail[3 * h + 2 : 3 * h + 3] for tail in tails]
        top = jnp.maximum(jnp.maximum(levels[0], levels[1]), levels[2])
        shares = [jnp.exp2(level - top) for level in levels]
        total = shares[0] + shares[1] + shares[2]
        for i, share in enumerate(shares):
            share_ref[pl.ds(3 * h + i, 1), :] = share / total
    columns = share_ref[...].T
    for h in range(heads):
        cols = slice(h * DH, (h + 1) * DH)
        mixed = sum(columns[:, 3 * h + i : 3 * h + i + 1] * part[:rows, cols].astype(jnp.float32) for i, part in enumerate(parts))
        out_ref[:, cols] = mixed.astype(out_ref.dtype)


def merge(home, far, near):
    rows, width = far.shape[0] - TAIL, far.shape[1]
    return pl.pallas_call(
        merge_kernel,
        grid=(1,),
        in_specs=[whole(home.shape), whole(far.shape), whole(near.shape)],
        out_specs=whole((rows, width)),
        out_shape=jax.ShapeDtypeStruct((rows, width), jnp.bfloat16),
        scratch_shapes=[pltpu.VMEM((DH, rows), jnp.float32)],
        name="merge",
    )(home, far, near)


def project_kernel(a_ref, own, near, near_other, far, far_other, *rest):
    *extra, out_ref, w_ref, sems = rest
    count, depth = a_ref.shape[0], own.shape[0]
    half = depth // 2
    x, core = lax.axis_index("x"), lax.axis_index("core")
    side = (x + count - 1 + 2 * core) % count
    other_side = (x + 1 + count - 2 * core) % count
    opposite = (x + 2) % count
    copies = []
    for n, src in enumerate((own, near, near_other)):
        for i in range(2):
            rows = pl.ds(i * half, half)
            copies.append((src.at[rows, :], w_ref.at[2 * n + i]))
    copies.append((far, w_ref.at[6 + core]))
    copies.append((far_other, w_ref.at[7 - core]))
    copies = [pltpu.make_async_copy(src, dst, sems.at[i]) for i, (src, dst) in enumerate(copies)]
    for copy in copies:
        copy.start()
    acc = jnp.zeros(out_ref.shape, jnp.float32)
    for n, index in enumerate((x, side, other_side, opposite)):
        for i in range(2):
            if n < 3:
                copies[2 * n + i].wait()
            elif i == 0:
                copies[6].wait()
                copies[7].wait()
            a = a_ref[index, :, i * half : (i + 1) * half]
            acc = acc + jnp.dot(a, w_ref[2 * n + i], preferred_element_type=jnp.float32)
    for ref in extra:
        acc = acc + ref[...].astype(jnp.float32)
    out_ref[...] = acc.astype(out_ref.dtype)


def project(gathered, weights, extra):
    count, rows, depth = gathered.shape
    width = weights[0].shape[1]
    return pl.pallas_call(
        project_kernel,
        grid=(1,),
        in_specs=[whole(gathered.shape)] + [anywhere()] * len(weights) + [whole(e.shape) for e in extra],
        out_specs=whole((rows, width)),
        scratch_shapes=[pltpu.VMEM((2 * count, depth // 2, width), jnp.bfloat16), pltpu.SemaphoreType.DMA((8,))],
        out_shape=jax.ShapeDtypeStruct((rows, width), jnp.bfloat16),
    )(gathered, *weights, *extra)


def after(value, *others):
    return lax.optimization_barrier((value, *others))[0]


def step(queries, local_keys, local_values, mem_keys, mem_values, offsets, mem_lengths, out_weight):
    core = lax.axis_index("core")
    yh = lax.axis_index("yh")
    rows = queries.shape[0] // 2
    width = queries.shape[1]

    tail = jnp.pad(offsets.astype(jnp.bfloat16), ((0, TAIL - 1), (0, width - offsets.shape[1])))
    loads = [
        jnp.concatenate([lax.dynamic_slice_in_dim(queries, half * rows, rows, 0), tail], axis=0) for half in (1 - yh, yh)
    ]
    guests = [[shift(load, DOC, -back) for back in (4, 2)] for load in loads]
    other = [swap(a, "core") for a in (mem_keys, mem_values)]
    memory = (mem_keys, mem_values, *other)
    near = part_ways(after(out_weight, *loads))

    def at_home(queries, partner):
        def kernel(*refs):
            home_kernel(*refs, partner=partner)

        blocks = (queries, local_keys, local_values)
        return attention(kernel, (offsets, mem_lengths), blocks, memory, rows, (rows + TAIL, width))

    def guest(load, back):
        def kernel(*refs):
            guest_kernel(*refs, back=back)

        out = attention(kernel, (mem_lengths,), (load,), memory, rows, load.shape)
        return out, shift(out, DOC, back)

    home0 = at_home(queries, True)
    far0, from_far0 = guest(after(guests[0][0], home0), 4)
    near0, from_near0 = guest(after(guests[0][1], far0), 2)
    far1, from_far1 = guest(after(guests[1][0], near0), 4)
    near1, from_near1 = guest(after(guests[1][1], far1), 2)

    half_depth = out_weight.shape[0] // 2
    near = after(near, far1)
    far = part_ways(lax.dynamic_slice_in_dim(near, core * half_depth, half_depth, 0))
    weights = [out_weight, near, swap(near, "core"), far, swap(far, "core")]

    home1 = at_home(after(queries, near1), False)

    count = lax.axis_size("x")

    def attended(home, far, near):
        merged = merge(home, far, near)
        return lax.all_to_all(merged.reshape(count, rows // count, width), "x", 0, 0)

    given = project(attended(home0, from_far0, from_near0), weights, ())
    kept = attended(home1, from_far1, from_near1)
    return project(kept, weights, (swap(given, "yh"),))


def solution(mesh):
    split = Mesh(mesh.devices.reshape(-1, 2, 2, 2, 4), (*DOC, *HEAD))
    placed = (
        P(DOC, HEAD),
        P(DOC, HEAD),
        P(DOC, HEAD),
        P(DOC, HEAD),
        P(DOC, HEAD),
        P(DOC, None),
        P(),
        P(HEAD, None),
    )
    return jax.shard_map(step, mesh=split, in_specs=placed, out_specs=P((*DOC, *HEAD), None), check_vma=False)
```

time: 247 us -> 170 us (0.69)
  waiting for transfers between devices: 110 us -> 12.3 us
  Pallas kernels: 0 us -> 79.3 us
  matrix products: 42.7 us -> 0 us
  starting transfers between devices: 17.8 us -> 49.8 us
  local copies, waits for them, and re-layouts: 32.8 us -> 6.08 us
  other arithmetic: 24.3 us -> 1.69 us
  blocking collectives: 0 us -> 19.3 us
  between operations: 18.7 us -> 0.35 us
    pallas_call x0 -> x10, Pallas kernels: none -> 79.3 us  [the longest x6 63.2 us: attention(): pl.pallas_call(kernel, grid_spec=pltpu.PrefetchScalarGridSpec(num_scalar_...]
    reduce_scatter x2 -> x0, waiting for transfers between devices: 59.2 us -> none  [own_block(): tiles = lax.psum_scatter(tiles, axes[k], scatter_dimension=0, tiled=True)]
    dot_general x9 -> x0, matrix products: 42.7 us -> none  [the longest x4 20.8 us: one_head(): jnp.einsum('qd,kd->qk', query_head, key_head, preferred_element_type=jnp....]
    ppermute x8 -> x15, waiting for transfers between devices: 50.4 us -> 12.3 us  [the longest x8 12.3 us: shift(): lax.ppermute(value, axis, [(i, (i + steps) % count) for i in range(count)])]
    ppermute x8 -> x15, starting transfers between devices: 17.8 us -> 49.8 us  [the longest x5 34.4 us: swap(): return lax.ppermute(value, axis, [(0, 1), (1, 0)])]
    unnamed x29 -> x18, local copies, waits for them, and re-layouts: 26.2 us -> 3.72 us
    all_to_all x0 -> x2, blocking collectives: none -> 19.3 us  [attended(): lax.all_to_all(merged.reshape(count, rows // count, width), 'x', 0, 0)]
    reduce_sum x5 -> x0, other arithmetic: 16.2 us -> none  [the longest x4 15.4 us: one_head(): jnp.sum(exponent, axis=-1, keepdims=True)]
  transfers between devices with their start and end apart: 10 -> 15, of which waited for: 8 -> 1; matrix products, arithmetic and copies ran while one was open for 9% -> 0% of each run, Pallas kernels for 0% -> 44%
where the time goes in v1:
time: 170 us; the launch traced here: 169 us
  Pallas kernels  79.3 us (47%)
  starting transfers between devices  49.8 us (29%)
  blocking collectives  19.3 us (11%)
  waiting for transfers between devices  12.3 us (7%)
  local copies, waits for them, and re-layouts  6.08 us (4%)
    pallas_call x6, Pallas kernels, attention(): pl.pallas_call(kernel, grid_spec=pltpu.PrefetchScalarGridSpec(num_scalar_...  63.2 us
    ppermute x5, starting transfers between devices, swap(): return lax.ppermute(value, axis, [(0, 1), (1, 0)])  34.4 us
    all_to_all x2, blocking collectives, attended(): lax.all_to_all(merged.reshape(count, rows // count, width), 'x', 0, 0)  19.3 us
    ppermute x8, waiting for transfers between devices, shift(): lax.ppermute(value, axis, [(i, (i + steps) % count) for i in range(count)])  12.3 us
    pallas_call x2, Pallas kernels, project(): pl.pallas_call(project_kernel, grid=(1,), in_specs=[whole(gathered.shape)...  11.3 us
    ppermute x8, starting transfers between devices, shift(): lax.ppermute(value, axis, [(i, (i + steps) % count) for i in range(count)])  11.2 us
    pallas_call x2, Pallas kernels, merge(): pl.pallas_call(merge_kernel, grid=(1,), in_specs=[whole(home.shape), whol...  4.89 us
    ppermute x2, starting transfers between devices, part_ways(): return lax.ppermute(value, ('core', 'x'), up + down)  4.29 us
  transfers between devices with their start and end apart: 15, of which 1 were waited for; matrix products, arithmetic and copies ran while one was open for 0% of the time, Pallas kernels for 44%

profile of v1, /device:TPU:1, one launch (start us, length us, event | category | flops | bytes accessed | tf_op | source)
XLA Modules:
  0.0 168.9 jit_solution(5996938543769562951)
XLA Ops:
  0.0 0.0 copy-start
  0.0 0.0 copy-start.1
  0.0 0.8 convert_element_type.5
  0.8 1.1 constant_dynamic-slice_fusion.1
  1.9 0.9 fusion.2
  2.8 3.3 %collective-permute-start.8 = (bf16[512,2048]{1,0:T(8,128)(2,1)}, bf16[512,2048]{1,0:T(8,128)(2,1)}, u32[]{:S(2)}, u32[]{:S(2)}) collective-permute-start(bf16[512,2048]{1,0:T(8,128)(2,1)} %own.3), channel_id=1, source_target_pairs={{0,1},{1,2},{2,3},{3,0},{8,11},{9,8},{10,9},{11,10},{4,5},{5,6},{6... | collective-permute-start | bytes 6291464 | tf_op jit(solution)/shard_map/ppermute | solution.py:33
  6.1 0.0 copy-done
  6.1 0.0 collective-permute-start.4
  6.1 0.0 copy-done.1
  6.1 0.5 collective-permute-start.5
  6.6 5.6 %collective-permute-start.3 = (bf16[272,512]{1,0:T(8,128)(2,1)}, bf16[272,512]{1,0:T(8,128)(2,1)}, u32[]{:S(2)}, u32[]{:S(2)}) collective-permute-start(bf16[272,512]{1,0:T(8,128)(2,1)} %get-tuple-element.21), channel_id=1, source_target_pairs={{0,224},{8,232},{16,240},{24,248},{32,0},{40,8},{48,16},{56,24},{6... | collective-permute-start | bytes 835592 | tf_op jit(solution)/shard_map/ppermute | solution.py:22
  12.2 1.7 %collective-permute-start.2 = (bf16[272,512]{1,0:T(8,128)(2,1)}, bf16[272,512]{1,0:T(8,128)(2,1)S(1)}, u32[]{:S(2)}, u32[]{:S(2)}) collective-permute-start(bf16[272,512]{1,0:T(8,128)(2,1)} %get-tuple-element.21), channel_id=1, source_target_pairs={{0,240},{8,248},{16,0},{24,8},{32,16},{40,24},{48,32},{56,40},{64,... | collective-permute-start | bytes 835592 | tf_op jit(solution)/shard_map/ppermute | solution.py:22
  13.9 0.0 collective-permute-done.4.refs_7_.refs_4_
  13.9 0.0 copy-start.2
  13.9 0.7 collective-permute-start.1
  14.6 0.0 collective-permute-done.5.refs_8_.refs_5_
  14.6 0.3 copy-done.2
  14.9 15.1 %shard_map.82.home_ref = bf16[272,512]{1,0:T(8,128)(2,1)} custom-call(s32[1,4]{1,0:T(1,128)} %refs_0_.11, s32[32]{0:T(128)} %refs_1_.3, bf16[512,512]{1,0:T(8,128)(2,1)} %refs_2_.10, bf16[512,512]{1,0:T(8,128)(2,1)} %refs_3_.11, bf16[512,512]{1,0:T(8,128)(2,1)} %refs_4_.3, bf16[1024,512]{1,0:T(8,128)(2,1)} %refs_5_.3, bf16[1024,512]{1,0:T(8,128)(2,1)} %refs_6_.3, ...), custom_call_target="tpu_custom_call" | custom-call | tf_op jit(solution)/shard_map/pallas_call | solution.py:195
  30.0 0.0 collective-permute-done.3.refs_1_
  30.0 3.3 %shard_map.83 = bf16[272,512]{1,0:T(8,128)(2,1)} custom-call(s32[32]{0:T(128)} %refs_1_.3, bf16[272,512]{1,0:T(8,128)(2,1)} %collective-permute-done.3.refs_1_, bf16[1024,512]{1,0:T(8,128)(2,1)} %refs_5_.3, bf16[1024,512]{1,0:T(8,128)(2,1)} %refs_6_.3, bf16[1024,512]{1,0:T(8,128)(2,1)} %copy-done.2, bf16[1024,512]{1,0:T(8,128)(2,1)} %collective-permute-done.5.refs_8_.refs_5_), custom_call_target="tpu_custom_call" | custom-call | tf_op jit(solution)/shard_map/pallas_call | solution.py:195
  33.3 0.0 collective-permute-done.2.refs_1_
  33.3 0.0 copy-start.6
  33.3 0.7 copy-done.6
  34.0 13.2 %shard_map.84 = bf16[272,512]{1,0:T(8,128)(2,1)} custom-call(s32[32]{0:T(128)} %refs_1_.3, bf16[272,512]{1,0:T(8,128)(2,1)} %copy-done.6, bf16[1024,512]{1,0:T(8,128)(2,1)} %refs_5_.3, bf16[1024,512]{1,0:T(8,128)(2,1)} %refs_6_.3, bf16[1024,512]{1,0:T(8,128)(2,1)} %copy-done.2, bf16[1024,512]{1,0:T(8,128)(2,1)} %collective-permute-done.5.refs_8_.refs_5_), custom_call_target="tpu_custom_call" | custom-call | tf_op jit(solution)/shard_map/pallas_call | solution.py:195
  47.2 0.0 collective-permute-done.1.refs_1_
  47.2 0.0 copy-start.7
  47.3 0.7 copy-done.7
  48.0 3.3 %shard_map.85 = bf16[272,512]{1,0:T(8,128)(2,1)} custom-call(s32[32]{0:T(128)} %refs_1_.3, bf16[272,512]{1,0:T(8,128)(2,1)} %copy-done.7, bf16[1024,512]{1,0:T(8,128)(2,1)} %refs_5_.3, bf16[1024,512]{1,0:T(8,128)(2,1)} %refs_6_.3, bf16[1024,512]{1,0:T(8,128)(2,1)} %copy-done.2, bf16[1024,512]{1,0:T(8,128)(2,1)} %collective-permute-done.5.refs_8_.refs_5_), custom_call_target="tpu_custom_call" | custom-call | tf_op jit(solution)/shard_map/pallas_call | solution.py:195
  51.3 0.0 collective-permute-done.8.near
  51.3 1.3 constant_dynamic-slice_fusion
  52.6 0.0 copy-start.5
  52.6 1.0 collective-permute-start.10
  53.6 16.3 %collective-permute-start.9 = (bf16[512,2048]{1,0:T(8,128)(2,1)}, bf16[512,2048]{1,0:T(8,128)(2,1)S(1)}, u32[]{:S(2)}, u32[]{:S(2)}) collective-permute-start(bf16[512,2048]{1,0:T(8,128)(2,1)} %collective-permute-done.8.near), channel_id=1, source_target_pairs={{0,8},{8,0},{1,9},{9,1},{2,10},{10,2},{3,11},{11,3},{4,12},{12,4},... | collective-permute-start | bytes 6291464 | tf_op jit(solution)/shard_map/ppermute | solution.py:26
  69.9 0.0 collective-permute-done.10.far
  69.9 0.0 copy-start.4
  69.9 14.9 %collective-permute-start.11 = (bf16[256,2048]{1,0:T(8,128)(2,1)S(1)}, bf16[256,2048]{1,0:T(8,128)(2,1)}, u32[]{:S(2)}, u32[]{:S(2)}) collective-permute-start(bf16[256,2048]{1,0:T(8,128)(2,1)S(1)} %collective-permute-done.10.far), channel_id=1, source_target_pairs={{0,8},{8,0},{1,9},{9,1},{2,10},{10,2},{3,11},{11,3},{4,12},{12,4},... | collective-permute-start | bytes 3145736 | tf_op jit(solution)/shard_map/ppermute | solution.py:26
  84.8 0.0 collective-permute-start
  84.8 1.5 collective-permute-start.13
  86.3 0.7 collective-permute-start.12
  87.0 12.3 %collective-permute-done.refs_1_ = bf16[272,512]{1,0:T(8,128)(2,1)} collective-permute-done((bf16[272,512]{1,0:T(8,128)(2,1)}, bf16[272,512]{1,0:T(8,128)(2,1)}, u32[]{:S(2)}, u32[]{:S(2)}) %collective-permute-start) | collective-permute-done | bytes 278560 | tf_op jit(solution)/shard_map/ppermute | solution.py:22
  99.3 13.2 %shard_map.86 = bf16[272,512]{1,0:T(8,128)(2,1)} custom-call(s32[32]{0:T(128)} %refs_1_.3, bf16[272,512]{1,0:T(8,128)(2,1)} %collective-permute-done.refs_1_, bf16[1024,512]{1,0:T(8,128)(2,1)} %refs_5_.3, bf16[1024,512]{1,0:T(8,128)(2,1)} %refs_6_.3, bf16[1024,512]{1,0:T(8,128)(2,1)} %copy-done.2, bf16[1024,512]{1,0:T(8,128)(2,1)} %collective-permute-done.5.refs_8_.refs_5_), custom_call_target="tpu_custom_call" | custom-call | tf_op jit(solution)/shard_map/pallas_call | solution.py:195
  112.5 0.0 copy-done.4
  112.5 0.1 collective-permute-start.7
  112.6 0.0 collective-permute-done.13.near_ref
  112.6 0.0 copy-done.5
  112.6 0.8 collective-permute-start.6
  113.4 0.0 collective-permute-done.12.far_ref
  113.4 2.4 %merge.3 = bf16[256,512]{1,0:T(8,128)(2,1)} custom-call(bf16[272,512]{1,0:T(8,128)(2,1)} %shard_map.82.home_ref, bf16[272,512]{1,0:T(8,128)(2,1)} %collective-permute-done.12.far_ref, bf16[272,512]{1,0:T(8,128)(2,1)} %collective-permute-done.13.near_ref), custom_call_target="tpu_custom_call" | custom-call | tf_op jit(solution)/shard_map/merge/pallas_call | solution.py:237
  115.9 9.6 %all_to_all.10.a_ref = bf16[4,64,512]{2,1,0:T(8,128)(2,1)} all-to-all(bf16[4,64,512]{2,1,0:T(8,128)(2,1)} %bitcast.2), channel_id=1, replica_groups=mesh['z'=8,'yl'=2,'core'=2,'yh'=2,'x'=4] {'x'}, dimensions={0} | all-to-all | bytes 524288 | tf_op jit(solution)/shard_map/all_to_all | solution.py:344
  125.5 0.0 collective-permute-done.11.far_other
  125.5 0.0 collective-permute-done.9.near_other
  125.5 0.0 copy-start.3
  125.5 1.3 copy-done.3
  126.8 5.6 %shard_map.88 = bf16[64,2048]{1,0:T(8,128)(2,1)} custom-call(bf16[4,64,512]{2,1,0:T(8,128)(2,1)} %all_to_all.10.a_ref, bf16[512,2048]{1,0:T(8,128)(2,1)} %own.3, bf16[512,2048]{1,0:T(8,128)(2,1)} %collective-permute-done.8.near, bf16[512,2048]{1,0:T(8,128)(2,1)} %copy-done.3, bf16[256,2048]{1,0:T(8,128)(2,1)} %copy-done.4, ...), custom_call_target="tpu_custom_call" | custom-call | tf_op jit(solution)/shard_map/pallas_call | solution.py:284
  132.4 2.7 %collective-permute-start.14 = (bf16[64,2048]{1,0:T(8,128)(2,1)}, bf16[64,2048]{1,0:T(8,128)(2,1)S(1)}, u32[]{:S(2)}, u32[]{:S(2)}) collective-permute-start(bf16[64,2048]{1,0:T(8,128)(2,1)} %shard_map.88), channel_id=1, source_target_pairs={{0,4},{4,0},{1,5},{5,1},{2,6},{6,2},{3,7},{7,3},{8,12},{12,8},{9,1... | collective-permute-start | bytes 786440 | tf_op jit(solution)/shard_map/ppermute | solution.py:26
  135.2 15.1 %shard_map.87.home_ref = bf16[272,512]{1,0:T(8,128)(2,1)} custom-call(s32[1,4]{1,0:T(1,128)} %refs_0_.11, s32[32]{0:T(128)} %refs_1_.3, bf16[512,512]{1,0:T(8,128)(2,1)} %refs_2_.10, bf16[512,512]{1,0:T(8,128)(2,1)} %refs_3_.11, bf16[512,512]{1,0:T(8,128)(2,1)} %refs_4_.3, bf16[1024,512]{1,0:T(8,128)(2,1)} %refs_5_.3, bf16[1024,512]{1,0:T(8,128)(2,1)} %refs_6_.3, ...), custom_call_target="tpu_custom_call" | custom-call | tf_op jit(solution)/shard_map/pallas_call | solution.py:195
  150.2 0.0 collective-permute-done.7.near_ref
  150.2 0.0 collective-permute-done.6.far_ref
  150.3 2.4 %merge.2 = bf16[256,512]{1,0:T(8,128)(2,1)} custom-call(bf16[272,512]{1,0:T(8,128)(2,1)} %shard_map.87.home_ref, bf16[272,512]{1,0:T(8,128)(2,1)} %collective-permute-done.6.far_ref, bf16[272,512]{1,0:T(8,128)(2,1)} %collective-permute-done.7.near_ref), custom_call_target="tpu_custom_call" | custom-call | tf_op jit(solution)/shard_map/merge/pallas_call | solution.py:237
  152.7 9.6 %all_to_all.11.a_ref = bf16[4,64,512]{2,1,0:T(8,128)(2,1)} all-to-all(bf16[4,64,512]{2,1,0:T(8,128)(2,1)} %bitcast.3), channel_id=1, replica_groups=mesh['z'=8,'yl'=2,'core'=2,'yh'=2,'x'=4] {'x'}, dimensions={0} | all-to-all | bytes 524288 | tf_op jit(solution)/shard_map/all_to_all | solution.py:344
  162.3 0.0 collective-permute-done.14.rest_0_
  162.3 0.0 copy-start.8
  162.3 0.7 copy-done.8
  163.1 5.7 %shard_map.89 = bf16[64,2048]{1,0:T(8,128)(2,1)} custom-call(bf16[4,64,512]{2,1,0:T(8,128)(2,1)} %all_to_all.11.a_ref, bf16[512,2048]{1,0:T(8,128)(2,1)} %own.3, bf16[512,2048]{1,0:T(8,128)(2,1)} %collective-permute-done.8.near, bf16[512,2048]{1,0:T(8,128)(2,1)} %copy-done.3, bf16[256,2048]{1,0:T(8,128)(2,1)} %copy-done.4, ...), custom_call_target="tpu_custom_call" | custom-call | tf_op jit(solution)/shard_map/pallas_call | solution.py:284
Async XLA Ops:
  0.0 6.1 %copy-start = (bf16[1024,512]{1,0:T(8,128)(2,1)S(1)}, bf16[1024,512]{1,0:T(8,128)(2,1)}, u32[]{:S(2)}) copy-start(bf16[1024,512]{1,0:T(8,128)(2,1)} %refs_5_.3) | copy-start | bytes 3145732
  0.0 6.1 %copy-start.1 = (bf16[1024,512]{1,0:T(8,128)(2,1)S(1)}, bf16[1024,512]{1,0:T(8,128)(2,1)}, u32[]{:S(2)}) copy-start(bf16[1024,512]{1,0:T(8,128)(2,1)} %refs_6_.3) | copy-start | bytes 3145732
  2.8 48.5 %collective-permute-start.8 = (bf16[512,2048]{1,0:T(8,128)(2,1)}, bf16[512,2048]{1,0:T(8,128)(2,1)}, u32[]{:S(2)}, u32[]{:S(2)}) collective-permute-start(bf16[512,2048]{1,0:T(8,128)(2,1)} %own.3), channel_id=1, source_target_pairs={{0,1},{1,2},{2,3},{3,0},{8,11},{9,8},{10,9},{11,10},{4,5},{5,6},{6... | collective-permute-start | bytes 6291464 | tf_op jit(solution)/shard_map/ppermute | solution.py:33
  6.1 7.8 %collective-permute-start.4 = (bf16[1024,512]{1,0:T(8,128)(2,1)S(1)}, bf16[1024,512]{1,0:T(8,128)(2,1)S(1)}, u32[]{:S(2)}, u32[]{:S(2)}) collective-permute-start(bf16[1024,512]{1,0:T(8,128)(2,1)S(1)} %copy-done), channel_id=1, source_target_pairs={{0,8},{8,0},{1,9},{9,1},{2,10},{10,2},{3,11},{11,3},{4,12},{12,4},... | collective-permute-start | bytes 3145736 | tf_op jit(solution)/shard_map/ppermute | solution.py:26
  6.1 8.6 %collective-permute-start.5 = (bf16[1024,512]{1,0:T(8,128)(2,1)S(1)}, bf16[1024,512]{1,0:T(8,128)(2,1)}, u32[]{:S(2)}, u32[]{:S(2)}) collective-permute-start(bf16[1024,512]{1,0:T(8,128)(2,1)S(1)} %copy-done.1), channel_id=1, source_target_pairs={{0,8},{8,0},{1,9},{9,1},{2,10},{10,2},{3,11},{11,3},{4,12},{12,4},... | collective-permute-start | bytes 3145736 | tf_op jit(solution)/shard_map/ppermute | solution.py:26
  6.6 23.4 %collective-permute-start.3 = (bf16[272,512]{1,0:T(8,128)(2,1)}, bf16[272,512]{1,0:T(8,128)(2,1)}, u32[]{:S(2)}, u32[]{:S(2)}) collective-permute-start(bf16[272,512]{1,0:T(8,128)(2,1)} %get-tuple-element.21), channel_id=1, source_target_pairs={{0,224},{8,232},{16,240},{24,248},{32,0},{40,8},{48,16},{56,24},{6... | collective-permute-start | bytes 835592 | tf_op jit(solution)/shard_map/ppermute | solution.py:22
  12.2 21.2 %collective-permute-start.2 = (bf16[272,512]{1,0:T(8,128)(2,1)}, bf16[272,512]{1,0:T(8,128)(2,1)S(1)}, u32[]{:S(2)}, u32[]{:S(2)}) collective-permute-start(bf16[272,512]{1,0:T(8,128)(2,1)} %get-tuple-element.21), channel_id=1, source_target_pairs={{0,240},{8,248},{16,0},{24,8},{32,16},{40,24},{48,32},{56,40},{64,... | collective-permute-start | bytes 835592 | tf_op jit(solution)/shard_map/ppermute | solution.py:22
  13.9 1.0 copy-start.2
  13.9 33.3 %collective-permute-start.1 = (bf16[272,512]{1,0:T(8,128)(2,1)}, bf16[272,512]{1,0:T(8,128)(2,1)S(1)}, u32[]{:S(2)}, u32[]{:S(2)}) collective-permute-start(bf16[272,512]{1,0:T(8,128)(2,1)} %get-tuple-element.22), channel_id=1, source_target_pairs={{0,224},{8,232},{16,240},{24,248},{32,0},{40,8},{48,16},{56,24},{6... | collective-permute-start | bytes 835592 | tf_op jit(solution)/shard_map/ppermute | solution.py:22
  33.3 0.7 copy-start.6
  47.2 0.7 copy-start.7
  52.6 60.0 %copy-start.5 = (bf16[272,512]{1,0:T(8,128)(2,1)S(1)}, bf16[272,512]{1,0:T(8,128)(2,1)}, u32[]{:S(2)}) copy-start(bf16[272,512]{1,0:T(8,128)(2,1)} %shard_map.85) | copy-start | bytes 835588
  52.6 17.3 %collective-permute-start.10 = (bf16[256,2048]{1,0:T(8,128)(2,1)S(1)}, bf16[256,2048]{1,0:T(8,128)(2,1)S(1)}, u32[]{:S(2)}, u32[]{:S(2)}) collective-permute-start(bf16[256,2048]{1,0:T(8,128)(2,1)S(1)} %constant_dynamic-slice_fusion), channel_id=1, source_target_pairs={{0,1},{1,2},{2,3},{3,0},{8,11},{9,8},{10,9},{11,10},{4,5},{5,6},{6... | collective-permute-start | bytes 3145736 | tf_op jit(solution)/shard_map/ppermute | solution.py:33
  53.6 71.9 %collective-permute-start.9 = (bf16[512,2048]{1,0:T(8,128)(2,1)}, bf16[512,2048]{1,0:T(8,128)(2,1)S(1)}, u32[]{:S(2)}, u32[]{:S(2)}) collective-permute-start(bf16[512,2048]{1,0:T(8,128)(2,1)} %collective-permute-done.8.near), channel_id=1, source_target_pairs={{0,8},{8,0},{1,9},{9,1},{2,10},{10,2},{3,11},{11,3},{4,12},{12,4},... | collective-permute-start | bytes 6291464 | tf_op jit(solution)/shard_map/ppermute | solution.py:26
  69.9 42.6 %copy-start.4 = (bf16[256,2048]{1,0:T(8,128)(2,1)}, bf16[256,2048]{1,0:T(8,128)(2,1)S(1)}, u32[]{:S(2)}) copy-start(bf16[256,2048]{1,0:T(8,128)(2,1)S(1)} %collective-permute-done.10.far) | copy-start | bytes 3145732
  69.9 55.6 %collective-permute-start.11 = (bf16[256,2048]{1,0:T(8,128)(2,1)S(1)}, bf16[256,2048]{1,0:T(8,128)(2,1)}, u32[]{:S(2)}, u32[]{:S(2)}) collective-permute-start(bf16[256,2048]{1,0:T(8,128)(2,1)S(1)} %collective-permute-done.10.far), channel_id=1, source_target_pairs={{0,8},{8,0},{1,9},{9,1},{2,10},{10,2},{3,11},{11,3},{4,12},{12,4},... | collective-permute-start | bytes 3145736 | tf_op jit(solution)/shard_map/ppermute | solution.py:26
  84.8 14.5 %collective-permute-start = (bf16[272,512]{1,0:T(8,128)(2,1)}, bf16[272,512]{1,0:T(8,128)(2,1)}, u32[]{:S(2)}, u32[]{:S(2)}) collective-permute-start(bf16[272,512]{1,0:T(8,128)(2,1)} %get-tuple-element.22), channel_id=1, source_target_pairs={{0,240},{8,248},{16,0},{24,8},{32,16},{40,24},{48,32},{56,40},{64,... | collective-permute-start | bytes 835592 | tf_op jit(solution)/shard_map/ppermute | solution.py:22
  84.8 27.8 %collective-permute-start.13 = (bf16[272,512]{1,0:T(8,128)(2,1)}, bf16[272,512]{1,0:T(8,128)(2,1)}, u32[]{:S(2)}, u32[]{:S(2)}) collective-permute-start(bf16[272,512]{1,0:T(8,128)(2,1)} %shard_map.84), channel_id=1, source_target_pairs={{0,16},{8,24},{16,32},{24,40},{32,48},{40,56},{48,64},{56,72},{64,... | collective-permute-start | bytes 835592 | tf_op jit(solution)/shard_map/ppermute | solution.py:22
  86.3 27.2 %collective-permute-start.12 = (bf16[272,512]{1,0:T(8,128)(2,1)}, bf16[272,512]{1,0:T(8,128)(2,1)}, u32[]{:S(2)}, u32[]{:S(2)}) collective-permute-start(bf16[272,512]{1,0:T(8,128)(2,1)} %shard_map.83), channel_id=1, source_target_pairs={{0,32},{8,40},{16,48},{24,56},{32,64},{40,72},{48,80},{56,88},{64,... | collective-permute-start | bytes 835592 | tf_op jit(solution)/shard_map/ppermute | solution.py:22
  112.5 37.7 %collective-permute-start.7 = (bf16[272,512]{1,0:T(8,128)(2,1)}, bf16[272,512]{1,0:T(8,128)(2,1)}, u32[]{:S(2)}, u32[]{:S(2)}) collective-permute-start(bf16[272,512]{1,0:T(8,128)(2,1)} %shard_map.86), channel_id=1, source_target_pairs={{0,16},{8,24},{16,32},{24,40},{32,48},{40,56},{48,64},{56,72},{64,... | collective-permute-start | bytes 835592 | tf_op jit(solution)/shard_map/ppermute | solution.py:22
  112.6 37.6 %collective-permute-start.6 = (bf16[272,512]{1,0:T(8,128)(2,1)S(1)}, bf16[272,512]{1,0:T(8,128)(2,1)}, u32[]{:S(2)}, u32[]{:S(2)}) collective-permute-start(bf16[272,512]{1,0:T(8,128)(2,1)S(1)} %copy-done.5), channel_id=1, source_target_pairs={{0,32},{8,40},{16,48},{24,56},{32,64},{40,72},{48,80},{56,88},{64,... | collective-permute-start | bytes 835592 | tf_op jit(solution)/shard_map/ppermute | solution.py:22
  125.5 1.3 copy-start.3
  132.4 29.9 %collective-permute-start.14 = (bf16[64,2048]{1,0:T(8,128)(2,1)}, bf16[64,2048]{1,0:T(8,128)(2,1)S(1)}, u32[]{:S(2)}, u32[]{:S(2)}) collective-permute-start(bf16[64,2048]{1,0:T(8,128)(2,1)} %shard_map.88), channel_id=1, source_target_pairs={{0,4},{4,0},{1,5},{5,1},{2,6},{6,2},{3,7},{7,3},{8,12},{12,8},{9,1... | collective-permute-start | bytes 786440 | tf_op jit(solution)/shard_map/ppermute | solution.py:26
  162.3 0.7 copy-start.8

commit v2 on v1

v2 whole, which is shorter than its diff:
```python
import math

import jax
import jax.numpy as jnp
from jax import lax
from jax.experimental import pallas as pl
from jax.experimental.pallas import tpu as pltpu
from jax.sharding import Mesh
from jax.sharding import PartitionSpec as P

DH = 128
DOC = ("z", "yl", "core")
HEAD = ("yh", "x")
NEG = -1e30
KEY_CHUNK = 512
TAIL = 16
SCALE = math.log2(math.e) / math.sqrt(DH)


def shift(value, axis, steps):
    count = lax.axis_size(axis)
    return lax.ppermute(value, axis, [(i, (i + steps) % count) for i in range(count)])


def swap(value, axis):
    return lax.ppermute(value, axis, [(0, 1), (1, 0)])


def part_ways(value):
    count = lax.axis_size("x")
    up = [(i, (i + 1) % count) for i in range(count)]
    down = [(count + i, count + (i - 1) % count) for i in range(count)]
    return lax.ppermute(value, ("core", "x"), up + down)


def lanes(x, width):
    return jnp.concatenate([x] * (width // DH), axis=1)


def scores_of(q, k):
    return lax.dot_general(q, k, (((1,), (1,)), ((), ())), preferred_element_type=jnp.float32) * SCALE


def with_ones(v):
    return jnp.concatenate([v, jnp.ones(v.shape, v.dtype)], axis=1)


def absorb(h, s, v, m_ref, acc_ref):
    m_old = m_ref[h]
    m_new = jnp.maximum(m_old, jnp.max(s, axis=1, keepdims=True))
    p = jnp.exp2(s - lanes(m_new, s.shape[1])).astype(jnp.bfloat16)
    pv = jnp.dot(p, with_ones(v), preferred_element_type=jnp.float32)
    acc_ref[h] = acc_ref[h] * lanes(jnp.exp2(m_old - m_new), 2 * DH) + pv
    m_ref[h] = m_new


def reset(m_ref, acc_ref):
    m_ref[...] = jnp.full(m_ref.shape, NEG, jnp.float32)
    acc_ref[...] = jnp.zeros(acc_ref.shape, jnp.float32)


def log2_count(count):
    return jnp.where(count >= 4, 2.0, jnp.where(count >= 3, math.log2(3), jnp.where(count >= 2, 1.0, 0.0)))


def of_head(h):
    return slice(h * DH, (h + 1) * DH)


def absorb_memories(arrays, lengths, counts, queries, buffer, sems, m_ref, acc_ref):
    per_document = arrays[0].shape[0] // KEY_CHUNK
    live = [jnp.where(count > 0, length, 0) for length, count in zip(lengths, counts)]
    biases = [log2_count(count) for count in counts]

    def copies(document, j, chunk):
        rows = pl.ds(j * KEY_CHUNK, KEY_CHUNK)
        return [
            pltpu.make_async_copy(arrays[2 * document + i].at[rows, :], buffer.at[chunk, i], sems.at[chunk, i])
            for i in range(2)
        ]

    for document in range(2):
        for j in range(per_document):

            @pl.when(live[document] > j * KEY_CHUNK)
            def _(document=document, j=j):
                for copy in copies(document, j, document * per_document + j):
                    copy.start()

    def fold(chunk, carry):
        second = chunk >= per_document
        left = jnp.where(second, live[1], live[0]) - jnp.where(second, chunk - per_document, chunk) * KEY_CHUNK

        @pl.when(left > 0)
        def _():
            for copy in copies(0, 0, chunk):
                copy.wait()
            row = lax.broadcasted_iota(jnp.int32, (1, KEY_CHUNK), 1)
            bias = jnp.where(row < left, jnp.where(second, biases[1], biases[0]), NEG)
            for h in range(m_ref.shape[0]):
                keys, values = (buffer[chunk, i, :, of_head(h)] for i in range(2))
                absorb(h, scores_of(queries(h), keys) + bias, values, m_ref, acc_ref)

        return carry

    lax.fori_loop(0, 2 * per_document, fold, 0)


def finish(out_ref, level_ref, m_ref, acc_ref):
    heads, rows = m_ref.shape[:2]
    level_ref[...] = jnp.zeros(level_ref.shape, jnp.float32)
    for h in range(heads):
        total = acc_ref[h, :, DH:]
        seen = total > 0
        safe = jnp.where(seen, total, 1.0)
        out_ref[:rows, of_head(h)] = (acc_ref[h, :, :DH] / safe).astype(jnp.bfloat16)
        rest = jnp.where(seen, m_ref[h] + jnp.log2(safe), NEG).T[:1, :]
        for i in range(3):
            term = rest.astype(jnp.bfloat16).astype(jnp.float32)
            level_ref[3 * h + i : 3 * h + i + 1, :rows] = term
            rest = rest - term
    out_ref[rows:, :] = level_ref[...].astype(jnp.bfloat16)


def home_kernel(offsets, lengths, q_ref, lk_ref, lv_ref, *refs, partner):
    *arrays, out_ref, m_ref, acc_ref, level_ref, buffer, sems = refs
    core, document, yh = lax.axis_index("core"), lax.axis_index(DOC), lax.axis_index("yh")
    heads, rows = m_ref.shape[:2]
    first = (1 - yh if partner else yh) * rows
    count = sum(jnp.where((offsets[0, i] == 1) & (core == 1), 1, 0) for i in range(offsets.shape[1]))
    reset(m_ref, acc_ref)

    def queries(h):
        return q_ref[pl.ds(pl.multiple_of(first, rows), rows), of_head(h)]

    shape = (rows, lk_ref.shape[0])
    seen = lax.broadcasted_iota(jnp.int32, shape, 0) + first >= lax.broadcasted_iota(jnp.int32, shape, 1)
    for h in range(heads):
        s = jnp.where(seen, scores_of(queries(h), lk_ref[:, of_head(h)]), NEG)
        absorb(h, s, lv_ref[:, of_head(h)], m_ref, acc_ref)
    live = lengths[document], lengths[document + 1 - 2 * core]
    absorb_memories(arrays, live, (jnp.int32(1), count), queries, buffer, sems, m_ref, acc_ref)
    finish(out_ref, level_ref, m_ref, acc_ref)


def guest_kernel(lengths, q_ref, *refs, back):
    *arrays, out_ref, m_ref, acc_ref, level_ref, buffer, sems = refs
    rows = m_ref.shape[1]
    core, document = lax.axis_index("core"), lax.axis_index(DOC)
    table = q_ref[rows:, :DH].astype(jnp.float32)
    own = jnp.sum(jnp.where(table == back, 1.0, 0.0)).astype(jnp.int32)
    wanted = (back - 1 + 2 * core).astype(jnp.float32)
    other = jnp.sum(jnp.where(table == wanted, 1.0, 0.0)).astype(jnp.int32)
    reset(m_ref, acc_ref)
    live = lengths[document], lengths[document + 1 - 2 * core]
    absorb_memories(
        arrays, live, (own, other), lambda h: q_ref[:rows, of_head(h)], buffer, sems, m_ref, acc_ref
    )
    finish(out_ref, level_ref, m_ref, acc_ref)


def pack_kernel(offsets, q_ref, *out_refs):
    yh = lax.axis_index("yh")
    rows, width = q_ref.shape[0] // 2, q_ref.shape[1]
    lane = lax.broadcasted_iota(jnp.int32, (TAIL, width), 1)
    top = lax.broadcasted_iota(jnp.int32, (TAIL, width), 0) == 0
    tail = jnp.zeros((TAIL, width), jnp.float32)
    for i in range(offsets.shape[1]):
        tail = jnp.where(top & (lane == i), offsets[0, i].astype(jnp.float32), tail)
    for half, out_ref in zip((1 - yh, yh), out_refs):
        out_ref[:rows, :] = q_ref[pl.ds(pl.multiple_of(half * rows, rows), rows), :]
        out_ref[rows:, :] = tail.astype(jnp.bfloat16)


def whole(shape):
    return pl.BlockSpec(shape, lambda *_: (0,) * len(shape))


def anywhere():
    return pl.BlockSpec(memory_space=pl.ANY)


def pack(queries, offsets):
    rows, width = queries.shape[0] // 2 + TAIL, queries.shape[1]
    return pl.pallas_call(
        pack_kernel,
        grid_spec=pltpu.PrefetchScalarGridSpec(
            num_scalar_prefetch=1, grid=(1,), in_specs=[whole(queries.shape)], out_specs=[whole((rows, width))] * 2
        ),
        out_shape=[jax.ShapeDtypeStruct((rows, width), jnp.bfloat16)] * 2,
        name="pack",
    )(offsets, queries)


def attention(kernel, scalars, blocks, memory, rows):
    mem_rows, width = memory[0].shape
    heads = width // DH
    chunks = 2 * mem_rows // KEY_CHUNK
    return pl.pallas_call(
        kernel,
        grid_spec=pltpu.PrefetchScalarGridSpec(
            num_scalar_prefetch=len(scalars),
            grid=(1,),
            in_specs=[whole(a.shape) for a in blocks] + [anywhere()] * 4,
            out_specs=whole((rows + TAIL, width)),
            scratch_shapes=[
                pltpu.VMEM((heads, rows, DH), jnp.float32),
                pltpu.VMEM((heads, rows, 2 * DH), jnp.float32),
                pltpu.VMEM((TAIL, width), jnp.float32),
                pltpu.VMEM((chunks, 2, KEY_CHUNK, width), jnp.bfloat16),
                pltpu.SemaphoreType.DMA((chunks, 2)),
            ],
        ),
        out_shape=jax.ShapeDtypeStruct((rows + TAIL, width), jnp.bfloat16),
    )(*scalars, *blocks, *memory)


def merge_kernel(home_ref, far_ref, near_ref, *refs):
    *tiles, share_ref, whole_ref = refs
    rows, width = whole_ref.shape
    heads, count = width // DH, len(tiles)
    parts = [home_ref, far_ref, near_ref]
    tails = [part[rows:, :rows].astype(jnp.float32) for part in parts]
    for h in range(heads):
        levels = [tail[3 * h : 3 * h + 1] + tail[3 * h + 1 : 3 * h + 2] + tail[3 * h + 2 : 3 * h + 3] for tail in tails]
        top = jnp.maximum(jnp.maximum(levels[0], levels[1]), levels[2])
        shares = [jnp.exp2(level - top) for level in levels]
        total = shares[0] + shares[1] + shares[2]
        for i, share in enumerate(shares):
            share_ref[3 * h + i : 3 * h + i + 1, :] = share / total
    columns = share_ref[...].T
    for h in range(heads):
        mixed = 0.0
        for i, part in enumerate(parts):
            mixed = mixed + columns[:, 3 * h + i : 3 * h + i + 1] * part[:rows, of_head(h)].astype(jnp.float32)
        whole_ref[:, of_head(h)] = mixed.astype(whole_ref.dtype)
    block = rows // count
    for k, tile in enumerate(tiles):
        place = (lax.axis_index("x") + k) % count
        tile[...] = whole_ref[pl.ds(pl.multiple_of(place * block, block), block), :]


def merge(home, far, near):
    rows, width = far.shape[0] - TAIL, far.shape[1]
    count = lax.axis_size("x")
    tile = (rows // count, width)
    return pl.pallas_call(
        merge_kernel,
        grid=(1,),
        in_specs=[whole(home.shape)] * 3,
        out_specs=[whole(tile)] * count,
        out_shape=[jax.ShapeDtypeStruct(tile, jnp.bfloat16)] * count,
        scratch_shapes=[pltpu.VMEM((DH, rows), jnp.float32), pltpu.VMEM((rows, width), jnp.bfloat16)],
        name="merge",
    )(home, far, near)


def project_kernel(*refs):
    mine, below, opposite, above, own, near, near_other, far, far_other, *extra, out_ref, w_ref, sems = refs
    half = own.shape[0] // 2
    core = lax.axis_index("core")
    copies = []
    for n, src in enumerate((own, near, near_other)):
        for i in range(2):
            copies.append((src.at[pl.ds(i * half, half), :], w_ref.at[2 * n + i]))
    copies.append((far, w_ref.at[6 + core]))
    copies.append((far_other, w_ref.at[7 - core]))
    copies = [pltpu.make_async_copy(src, dst, sems.at[i]) for i, (src, dst) in enumerate(copies)]
    for copy in copies:
        copy.start()
    side = jnp.where(core == 0, below[...], above[...])
    other_side = jnp.where(core == 0, above[...], below[...])
    acc = jnp.zeros(out_ref.shape, jnp.float32)
    for n, tile in enumerate((mine[...], side, other_side, opposite[...])):
        for i in range(2):
            if n < 3:
                copies[2 * n + i].wait()
            elif i == 0:
                copies[6].wait()
                copies[7].wait()
            a = tile[:, i * half : (i + 1) * half]
            acc = acc + jnp.dot(a, w_ref[2 * n + i], preferred_element_type=jnp.float32)
    for ref in extra:
        acc = acc + ref[...].astype(jnp.float32)
    out_ref[...] = acc.astype(out_ref.dtype)


def project(tiles, weights, extra):
    rows = tiles[0].shape[0]
    depth, width = weights[0].shape
    return pl.pallas_call(
        project_kernel,
        grid=(1,),
        in_specs=[whole(t.shape) for t in tiles] + [anywhere()] * len(weights) + [whole(e.shape) for e in extra],
        out_specs=whole((rows, width)),
        scratch_shapes=[pltpu.VMEM((2 * len(tiles), depth // 2, width), jnp.bfloat16), pltpu.SemaphoreType.DMA((8,))],
        out_shape=jax.ShapeDtypeStruct((rows, width), jnp.bfloat16),
    )(*tiles, *weights, *extra)


def after(value, *others):
    return lax.optimization_barrier((value, *others))[0]


def step(queries, local_keys, local_values, mem_keys, mem_values, offsets, mem_lengths, out_weight):
    core = lax.axis_index("core")
    rows = queries.shape[0] // 2

    loads = pack(queries, offsets)
    guests = [[shift(load, DOC, -back) for back in (4, 2)] for load in loads]
    other = [swap(a, "core") for a in (mem_keys, mem_values)]
    memory = (mem_keys, mem_values, *other)
    near = part_ways(after(out_weight, *loads))

    def at_home(queries, partner):
        def kernel(*refs):
            home_kernel(*refs, partner=partner)

        blocks = (queries, local_keys, local_values)
        return attention(kernel, (offsets, mem_lengths), blocks, memory, rows)

    def guest(load, back):
        def kernel(*refs):
            guest_kernel(*refs, back=back)

        out = attention(kernel, (mem_lengths,), (load,), memory, rows)
        return out, shift(out, DOC, back)

    home0 = at_home(queries, True)
    far0, from_far0 = guest(after(guests[0][0], home0), 4)
    near0, from_near0 = guest(after(guests[0][1], far0), 2)
    far1, from_far1 = guest(after(guests[1][0], near0), 4)
    near1, from_near1 = guest(after(guests[1][1], far1), 2)

    half_depth = out_weight.shape[0] // 2
    near = after(near, far1)
    far = part_ways(lax.dynamic_slice_in_dim(near, core * half_depth, half_depth, 0))
    weights = [out_weight, near, swap(near, "core"), far, swap(far, "core")]

    home1 = at_home(after(queries, near1), False)

    def attended(home, far, near):
        mine, *tiles = merge(home, far, near)
        return mine, *(shift(tile, "x", k) for k, tile in enumerate(tiles, 1))

    given = project(attended(home0, from_far0, from_near0), weights, ())
    kept = attended(home1, from_far1, from_near1)
    return project(kept, weights, (swap(given, "yh"),))


def solution(mesh):
    split = Mesh(mesh.devices.reshape(-1, 2, 2, 2, 4), (*DOC, *HEAD))
    placed = (
        P(DOC, HEAD),
        P(DOC, HEAD),
        P(DOC, HEAD),
        P(DOC, HEAD),
        P(DOC, HEAD),
        P(DOC, None),
        P(),
        P(HEAD, None),
    )
    return jax.shard_map(step, mesh=split, in_specs=placed, out_specs=P((*DOC, *HEAD), None), check_vma=False)
```

time: 170 us -> 133 us (0.78)
  Pallas kernels: 79.3 us -> 57.5 us
  blocking collectives: 19.3 us -> 0 us
  waiting for transfers between devices: 12.3 us -> 17.1 us
  local copies, waits for them, and re-layouts: 6.08 us -> 8.21 us
    pallas_call x6, Pallas kernels: 63.2 us -> 38.7 us  [attention(): pl.pallas_call(kernel, grid_spec=pltpu.PrefetchScalarGridSpec(num_scalar_...]
    all_to_all x2 -> x0, blocking collectives: 19.3 us -> none  [attended(): lax.all_to_all(merged.reshape(count, rows // count, width), 'x', 0, 0)]
    ppermute x5, starting transfers between devices: 34.4 us -> 23.8 us  [swap(): return lax.ppermute(value, axis, [(0, 1), (1, 0)])]
    ppermute x8 -> x14, starting transfers between devices: 11.2 us -> 20.2 us  [shift(): lax.ppermute(value, axis, [(i, (i + steps) % count) for i in range(count)])]
    ppermute x2, waiting for transfers between devices: 0.01 us -> 3.75 us  [part_ways(): return lax.ppermute(value, ('core', 'x'), up + down)]
    unnamed x18 -> x36, local copies, waits for them, and re-layouts: 3.72 us -> 6.85 us
    pallas_call x4 -> x5, Pallas kernels: 16.2 us -> 18.8 us  [the longest x2 11.3 us: project(): pl.pallas_call(project_kernel, grid=(1,), in_specs=[whole(t.shape) for t...]
    ppermute x8 -> x14, waiting for transfers between devices: 12.3 us -> 13.3 us  [shift(): lax.ppermute(value, axis, [(i, (i + steps) % count) for i in range(count)])]
  transfers between devices with their start and end apart: 15 -> 21, of which waited for: 1 -> 6; matrix products, arithmetic and copies ran while one was open for 0% -> 0% of each run, Pallas kernels for 44% -> 37%
where the time goes in v2:
time: 133 us; the launch traced here: 131 us
  Pallas kernels  57.5 us (43%)
  starting transfers between devices  48.1 us (36%)
  waiting for transfers between devices  17.1 us (13%)
  local copies, waits for them, and re-layouts  8.21 us (6%)
    pallas_call x6, Pallas kernels, attention(): pl.pallas_call(kernel, grid_spec=pltpu.PrefetchScalarGridSpec(num_scalar_...  38.7 us
    ppermute x5, starting transfers between devices, swap(): return lax.ppermute(value, axis, [(0, 1), (1, 0)])  23.8 us
    ppermute x14, starting transfers between devices, shift(): lax.ppermute(value, axis, [(i, (i + steps) % count) for i in range(count)])  20.2 us
    ppermute x14, waiting for transfers between devices, shift(): lax.ppermute(value, axis, [(i, (i + steps) % count) for i in range(count)])  13.3 us
    pallas_call x2, Pallas kernels, project(): pl.pallas_call(project_kernel, grid=(1,), in_specs=[whole(t.shape) for t...  11.3 us
    unnamed x36, local copies, waits for them, and re-layouts  6.85 us
    pallas_call x2, Pallas kernels, merge(): pl.pallas_call(merge_kernel, grid=(1,), in_specs=[whole(home.shape)] * 3,...  4.89 us
    ppermute x2, starting transfers between devices, part_ways(): return lax.ppermute(value, ('core', 'x'), up + down)  4.02 us
  transfers between devices with their start and end apart: 21, of which 6 were waited for; matrix products, arithmetic and copies ran while one was open for 0% of the time, Pallas kernels for 37%

profile of v2, /device:TPU:1, one launch (start us, length us, event | category | flops | bytes accessed | tf_op | source)
XLA Modules:
  0.0 131.2 jit_solution(3270716687061205917)
XLA Ops:
  0.0 2.6 %pack.1 = (bf16[272,512]{1,0:T(8,128)(2,1)}, bf16[272,512]{1,0:T(8,128)(2,1)}) custom-call(s32[1,4]{1,0:T(1,128)} %refs_0_.11, bf16[512,512]{1,0:T(8,128)(2,1)} %refs_2_.10), custom_call_target="tpu_custom_call" | custom-call | tf_op jit(solution)/shard_map/pack/pallas_call | solution.py:185
  2.6 3.3 %collective-permute-start.11 = (bf16[512,2048]{1,0:T(8,128)(2,1)}, bf16[512,2048]{1,0:T(8,128)(2,1)}, u32[]{:S(2)}, u32[]{:S(2)}) collective-permute-start(bf16[512,2048]{1,0:T(8,128)(2,1)} %refs_4_.7), channel_id=1, source_target_pairs={{0,1},{1,2},{2,3},{3,0},{8,11},{9,8},{10,9},{11,10},{4,5},{5,6},{6... | collective-permute-start | bytes 6291464 | tf_op jit(solution)/shard_map/ppermute | solution.py:33
  5.9 0.0 collective-permute-start.4
  5.9 0.5 collective-permute-start.5
  6.4 5.6 %collective-permute-start.3 = (bf16[272,512]{1,0:T(8,128)(2,1)}, bf16[272,512]{1,0:T(8,128)(2,1)S(1)}, u32[]{:S(2)}, u32[]{:S(2)}) collective-permute-start(bf16[272,512]{1,0:T(8,128)(2,1)} %get-tuple-element.23), channel_id=1, source_target_pairs={{0,224},{8,232},{16,240},{24,248},{32,0},{40,8},{48,16},{56,24},{6... | collective-permute-start | bytes 835592 | tf_op jit(solution)/shard_map/ppermute | solution.py:22
  12.0 1.7 %collective-permute-start.2 = (bf16[272,512]{1,0:T(8,128)(2,1)}, bf16[272,512]{1,0:T(8,128)(2,1)S(1)}, u32[]{:S(2)}, u32[]{:S(2)}) collective-permute-start(bf16[272,512]{1,0:T(8,128)(2,1)} %get-tuple-element.23), channel_id=1, source_target_pairs={{0,240},{8,248},{16,0},{24,8},{32,16},{40,24},{48,32},{56,40},{64,... | collective-permute-start | bytes 835592 | tf_op jit(solution)/shard_map/ppermute | solution.py:22
  13.7 0.0 collective-permute-done.4.refs_7_.refs_4_
  13.7 0.7 collective-permute-start.1
  14.4 0.0 collective-permute-done.5.refs_8_.refs_5_
  14.4 0.2 copy-done
  14.7 1.1 copy-done.1
  15.8 8.5 %shard_map.82.home_ref = bf16[272,512]{1,0:T(8,128)(2,1)} custom-call(s32[1,4]{1,0:T(1,128)} %refs_0_.11, s32[32]{0:T(128)} %refs_1_.3, bf16[512,512]{1,0:T(8,128)(2,1)} %refs_2_.10, bf16[512,512]{1,0:T(8,128)(2,1)} %refs_3_.11, bf16[512,512]{1,0:T(8,128)(2,1)} %refs_4_.5, bf16[1024,512]{1,0:T(8,128)(2,1)} %refs_5_.3, bf16[1024,512]{1,0:T(8,128)(2,1)} %refs_6_.3, ...), custom_call_target="tpu_custom_call" | custom-call | tf_op jit(solution)/shard_map/pallas_call | solution.py:199
  24.3 0.0 collective-permute-done.3.refs_1_
  24.3 0.7 copy-done.7
  25.0 2.8 %shard_map.83 = bf16[272,512]{1,0:T(8,128)(2,1)} custom-call(s32[32]{0:T(128)} %refs_1_.3, bf16[272,512]{1,0:T(8,128)(2,1)} %copy-done.7, bf16[1024,512]{1,0:T(8,128)(2,1)} %refs_5_.3, bf16[1024,512]{1,0:T(8,128)(2,1)} %refs_6_.3, bf16[1024,512]{1,0:T(8,128)(2,1)} %copy-done, bf16[1024,512]{1,0:T(8,128)(2,1)} %copy-done.1), custom_call_target="tpu_custom_call" | custom-call | tf_op jit(solution)/shard_map/pallas_call | solution.py:199
  27.8 0.0 collective-permute-done.2.refs_1_
  27.9 0.7 copy-done.6
  28.6 8.0 %shard_map.84 = bf16[272,512]{1,0:T(8,128)(2,1)} custom-call(s32[32]{0:T(128)} %refs_1_.3, bf16[272,512]{1,0:T(8,128)(2,1)} %copy-done.6, bf16[1024,512]{1,0:T(8,128)(2,1)} %refs_5_.3, bf16[1024,512]{1,0:T(8,128)(2,1)} %refs_6_.3, bf16[1024,512]{1,0:T(8,128)(2,1)} %copy-done, bf16[1024,512]{1,0:T(8,128)(2,1)} %copy-done.1), custom_call_target="tpu_custom_call" | custom-call | tf_op jit(solution)/shard_map/pallas_call | solution.py:199
  36.6 0.0 collective-permute-done.1.refs_1_
  36.6 0.7 copy-done.8
  37.3 2.8 %shard_map.85 = bf16[272,512]{1,0:T(8,128)(2,1)} custom-call(s32[32]{0:T(128)} %refs_1_.3, bf16[272,512]{1,0:T(8,128)(2,1)} %copy-done.8, bf16[1024,512]{1,0:T(8,128)(2,1)} %refs_5_.3, bf16[1024,512]{1,0:T(8,128)(2,1)} %refs_6_.3, bf16[1024,512]{1,0:T(8,128)(2,1)} %copy-done, bf16[1024,512]{1,0:T(8,128)(2,1)} %copy-done.1), custom_call_target="tpu_custom_call" | custom-call | tf_op jit(solution)/shard_map/pallas_call | solution.py:199
  40.1 0.0 collective-permute-done.11.refs_5_
  40.1 1.4 %constant_dynamic-slice_fusion = bf16[256,2048]{1,0:T(8,128)(2,1)S(1)} fusion(bf16[512,2048]{1,0:T(8,128)(2,1)} %collective-permute-done.11.refs_5_, s32[]{:T(128)S(6)} %select_n.3), kind=kLoop, calls=%fused_computation | loop fusion | bytes 2097156 | tf_op jit(solution)/shard_map/dynamic_slice | solution.py:337
  41.5 0.7 collective-permute-start.13
  42.2 9.6 %collective-permute-start.12 = (bf16[512,2048]{1,0:T(8,128)(2,1)}, bf16[512,2048]{1,0:T(8,128)(2,1)S(1)}, u32[]{:S(2)}, u32[]{:S(2)}) collective-permute-start(bf16[512,2048]{1,0:T(8,128)(2,1)} %collective-permute-done.11.refs_5_), channel_id=1, source_target_pairs={{0,8},{8,0},{1,9},{9,1},{2,10},{10,2},{3,11},{11,3},{4,12},{12,4},... | collective-permute-start | bytes 6291464 | tf_op jit(solution)/shard_map/ppermute | solution.py:26
  51.8 3.8 %collective-permute-done.13.refs_7_ = bf16[256,2048]{1,0:T(8,128)(2,1)S(1)} collective-permute-done((bf16[256,2048]{1,0:T(8,128)(2,1)S(1)}, bf16[256,2048]{1,0:T(8,128)(2,1)S(1)}, u32[]{:S(2)}, u32[]{:S(2)}) %collective-permute-start.13) | collective-permute-done | bytes 1048608 | tf_op jit(solution)/shard_map/ppermute | solution.py:33
  55.5 11.1 %collective-permute-start.14 = (bf16[256,2048]{1,0:T(8,128)(2,1)S(1)}, bf16[256,2048]{1,0:T(8,128)(2,1)}, u32[]{:S(2)}, u32[]{:S(2)}) collective-permute-start(bf16[256,2048]{1,0:T(8,128)(2,1)S(1)} %collective-permute-done.13.refs_7_), channel_id=1, source_target_pairs={{0,8},{8,0},{1,9},{9,1},{2,10},{10,2},{3,11},{11,3},{4,12},{12,4},... | collective-permute-start | bytes 3145736 | tf_op jit(solution)/shard_map/ppermute | solution.py:26
  66.6 0.0 collective-permute-start.16
  66.6 0.8 collective-permute-start.15
  67.4 3.5 %collective-permute-start = (bf16[272,512]{1,0:T(8,128)(2,1)}, bf16[272,512]{1,0:T(8,128)(2,1)}, u32[]{:S(2)}, u32[]{:S(2)}) collective-permute-start(bf16[272,512]{1,0:T(8,128)(2,1)} %get-tuple-element.22), channel_id=1, source_target_pairs={{0,240},{8,248},{16,0},{24,8},{32,16},{40,24},{48,32},{56,40},{64,... | collective-permute-start | bytes 835592 | tf_op jit(solution)/shard_map/ppermute | solution.py:22
  70.9 7.9 %collective-permute-done.16.near_ref = bf16[272,512]{1,0:T(8,128)(2,1)S(1)} collective-permute-done((bf16[272,512]{1,0:T(8,128)(2,1)S(1)}, bf16[272,512]{1,0:T(8,128)(2,1)S(1)}, u32[]{:S(2)}, u32[]{:S(2)}) %collective-permute-start.16) | collective-permute-done | bytes 278560 | tf_op jit(solution)/shard_map/ppermute | solution.py:22
  78.8 0.0 collective-permute-done.15.far_ref
  78.8 0.7 copy-done.10
  79.5 2.5 %merge.3 = (bf16[64,512]{1,0:T(8,128)(2,1)}, bf16[64,512]{1,0:T(8,128)(2,1)}, bf16[64,512]{1,0:T(8,128)(2,1)}, bf16[64,512]{1,0:T(8,128)(2,1)}) custom-call(bf16[272,512]{1,0:T(8,128)(2,1)} %shard_map.82.home_ref, bf16[272,512]{1,0:T(8,128)(2,1)} %collective-permute-done.15.far_ref, bf16[272,512]{1,0:T(8,128)(2,1)} %copy-done.10), custom_call_target="tpu_custom_call" | custom-call | tf_op jit(solution)/shard_map/merge/pallas_call | solution.py:247
  82.0 0.0 collective-permute-start.17
  82.0 1.1 collective-permute-start.18
  83.1 0.0 collective-permute-done.refs_1_
  83.1 8.0 %shard_map.86 = bf16[272,512]{1,0:T(8,128)(2,1)} custom-call(s32[32]{0:T(128)} %refs_1_.3, bf16[272,512]{1,0:T(8,128)(2,1)} %collective-permute-done.refs_1_, bf16[1024,512]{1,0:T(8,128)(2,1)} %refs_5_.3, bf16[1024,512]{1,0:T(8,128)(2,1)} %refs_6_.3, bf16[1024,512]{1,0:T(8,128)(2,1)} %copy-done, bf16[1024,512]{1,0:T(8,128)(2,1)} %copy-done.1), custom_call_target="tpu_custom_call" | custom-call | tf_op jit(solution)/shard_map/pallas_call | solution.py:199
  91.2 0.8 collective-permute-start.7
  91.9 0.0 collective-permute-done.17.refs_1_
  91.9 0.2 collective-permute-start.6
  92.1 0.0 collective-permute-done.18.refs_2_
  92.1 1.9 %collective-permute-start.19 = (bf16[64,512]{1,0:T(8,128)(2,1)}, bf16[64,512]{1,0:T(8,128)(2,1)S(1)}, u32[]{:S(2)}, u32[]{:S(2)}) collective-permute-start(bf16[64,512]{1,0:T(8,128)(2,1)} %get-tuple-element.38), channel_id=1, source_target_pairs={{0,3},{1,0},{2,1},{3,2},{4,7},{5,4},{6,5},{7,6},{8,11},{9,8},{10,9... | collective-permute-start | bytes 196616 | tf_op jit(solution)/shard_map/ppermute | solution.py:22
  94.0 2.1 %collective-permute-done.19.refs_3_ = bf16[64,512]{1,0:T(8,128)(2,1)S(1)} collective-permute-done((bf16[64,512]{1,0:T(8,128)(2,1)}, bf16[64,512]{1,0:T(8,128)(2,1)S(1)}, u32[]{:S(2)}, u32[]{:S(2)}) %collective-permute-start.19) | collective-permute-done | bytes 65568 | tf_op jit(solution)/shard_map/ppermute | solution.py:22
  96.1 0.0 collective-permute-done.14.refs_8_
  96.1 0.0 collective-permute-done.12.refs_6_
  96.1 0.6 copy-done.17
  96.7 1.3 %copy-done.2 = bf16[512,2048]{1,0:T(8,128)(2,1)} copy-done((bf16[512,2048]{1,0:T(8,128)(2,1)}, bf16[512,2048]{1,0:T(8,128)(2,1)S(1)}, u32[]{:S(2)}) %copy-start.2) | copy-done | bytes 2097176
  98.1 5.6 %shard_map.88 = bf16[64,2048]{1,0:T(8,128)(2,1)} custom-call(bf16[64,512]{1,0:T(8,128)(2,1)} %get-tuple-element.35.refs_0_, bf16[64,512]{1,0:T(8,128)(2,1)} %copy-done.12, bf16[64,512]{1,0:T(8,128)(2,1)} %copy-done.13, bf16[64,512]{1,0:T(8,128)(2,1)} %copy-done.17, bf16[512,2048]{1,0:T(8,128)(2,1)} %refs_4_.7, ...), custom_call_target="tpu_custom_call" | custom-call | tf_op jit(solution)/shard_map/pallas_call | solution.py:291
  103.7 2.7 %collective-permute-start.20 = (bf16[64,2048]{1,0:T(8,128)(2,1)}, bf16[64,2048]{1,0:T(8,128)(2,1)S(1)}, u32[]{:S(2)}, u32[]{:S(2)}) collective-permute-start(bf16[64,2048]{1,0:T(8,128)(2,1)} %shard_map.88), channel_id=1, source_target_pairs={{0,4},{4,0},{1,5},{5,1},{2,6},{6,2},{3,7},{7,3},{8,12},{12,8},{9,1... | collective-permute-start | bytes 786440 | tf_op jit(solution)/shard_map/ppermute | solution.py:26
  106.4 8.5 %shard_map.87.home_ref = bf16[272,512]{1,0:T(8,128)(2,1)} custom-call(s32[1,4]{1,0:T(1,128)} %refs_0_.11, s32[32]{0:T(128)} %refs_1_.3, bf16[512,512]{1,0:T(8,128)(2,1)} %refs_2_.10, bf16[512,512]{1,0:T(8,128)(2,1)} %refs_3_.11, bf16[512,512]{1,0:T(8,128)(2,1)} %refs_4_.5, bf16[1024,512]{1,0:T(8,128)(2,1)} %refs_5_.3, bf16[1024,512]{1,0:T(8,128)(2,1)} %refs_6_.3, ...), custom_call_target="tpu_custom_call" | custom-call | tf_op jit(solution)/shard_map/pallas_call | solution.py:199
  114.9 0.0 collective-permute-done.7.near_ref
  114.9 0.0 collective-permute-done.6.far_ref
  114.9 2.4 %merge.2 = (bf16[64,512]{1,0:T(8,128)(2,1)}, bf16[64,512]{1,0:T(8,128)(2,1)}, bf16[64,512]{1,0:T(8,128)(2,1)}, bf16[64,512]{1,0:T(8,128)(2,1)}) custom-call(bf16[272,512]{1,0:T(8,128)(2,1)} %shard_map.87.home_ref, bf16[272,512]{1,0:T(8,128)(2,1)} %collective-permute-done.6.far_ref, bf16[272,512]{1,0:T(8,128)(2,1)} %collective-permute-done.7.near_ref), custom_call_target="tpu_custom_call" | custom-call | tf_op jit(solution)/shard_map/merge/pallas_call | solution.py:247
  117.4 1.5 %collective-permute-start.8 = (bf16[64,512]{1,0:T(8,128)(2,1)}, bf16[64,512]{1,0:T(8,128)(2,1)S(1)}, u32[]{:S(2)}, u32[]{:S(2)}) collective-permute-start(bf16[64,512]{1,0:T(8,128)(2,1)} %get-tuple-element.30), channel_id=1, source_target_pairs={{0,1},{1,2},{2,3},{3,0},{4,5},{5,6},{6,7},{7,4},{8,9},{9,10},{10,1... | collective-permute-start | bytes 196616 | tf_op jit(solution)/shard_map/ppermute | solution.py:22
  118.8 2.1 %collective-permute-start.9 = (bf16[64,512]{1,0:T(8,128)(2,1)}, bf16[64,512]{1,0:T(8,128)(2,1)S(1)}, u32[]{:S(2)}, u32[]{:S(2)}) collective-permute-start(bf16[64,512]{1,0:T(8,128)(2,1)} %get-tuple-element.31), channel_id=1, source_target_pairs={{0,2},{1,3},{2,0},{3,1},{4,6},{5,7},{6,4},{7,5},{8,10},{9,11},{10,... | collective-permute-start | bytes 196616 | tf_op jit(solution)/shard_map/ppermute | solution.py:22
  121.0 0.3 collective-permute-start.10
  121.3 0.6 collective-permute-done.8.refs_1_
  121.9 1.8 %collective-permute-done.9.refs_2_ = bf16[64,512]{1,0:T(8,128)(2,1)S(1)} collective-permute-done((bf16[64,512]{1,0:T(8,128)(2,1)}, bf16[64,512]{1,0:T(8,128)(2,1)S(1)}, u32[]{:S(2)}, u32[]{:S(2)}) %collective-permute-start.9) | collective-permute-done | bytes 65568 | tf_op jit(solution)/shard_map/ppermute | solution.py:22
  123.7 0.9 collective-permute-done.10.refs_3_
  124.6 0.0 collective-permute-done.20.refs_9_
  124.6 0.6 copy-done.16
  125.2 0.1 copy-done.11
  125.3 5.8 %shard_map.89 = bf16[64,2048]{1,0:T(8,128)(2,1)} custom-call(bf16[64,512]{1,0:T(8,128)(2,1)} %get-tuple-element.29.refs_0_, bf16[64,512]{1,0:T(8,128)(2,1)} %copy-done.14, bf16[64,512]{1,0:T(8,128)(2,1)} %copy-done.15, bf16[64,512]{1,0:T(8,128)(2,1)} %copy-done.16, bf16[512,2048]{1,0:T(8,128)(2,1)} %refs_4_.7, ...), custom_call_target="tpu_custom_call" | custom-call | tf_op jit(solution)/shard_map/pallas_call | solution.py:291
  (26 shorter events, 0.0 us)
Async XLA Ops:
  2.6 37.6 %collective-permute-start.11 = (bf16[512,2048]{1,0:T(8,128)(2,1)}, bf16[512,2048]{1,0:T(8,128)(2,1)}, u32[]{:S(2)}, u32[]{:S(2)}) collective-permute-start(bf16[512,2048]{1,0:T(8,128)(2,1)} %refs_4_.7), channel_id=1, source_target_pairs={{0,1},{1,2},{2,3},{3,0},{8,11},{9,8},{10,9},{11,10},{4,5},{5,6},{6... | collective-permute-start | bytes 6291464 | tf_op jit(solution)/shard_map/ppermute | solution.py:33
  5.9 7.8 %collective-permute-start.4 = (bf16[1024,512]{1,0:T(8,128)(2,1)}, bf16[1024,512]{1,0:T(8,128)(2,1)S(1)}, u32[]{:S(2)}, u32[]{:S(2)}) collective-permute-start(bf16[1024,512]{1,0:T(8,128)(2,1)} %refs_5_.3), channel_id=1, source_target_pairs={{0,8},{8,0},{1,9},{9,1},{2,10},{10,2},{3,11},{11,3},{4,12},{12,4},... | collective-permute-start | bytes 3145736 | tf_op jit(solution)/shard_map/ppermute | solution.py:26
  5.9 8.6 %collective-permute-start.5 = (bf16[1024,512]{1,0:T(8,128)(2,1)}, bf16[1024,512]{1,0:T(8,128)(2,1)S(1)}, u32[]{:S(2)}, u32[]{:S(2)}) collective-permute-start(bf16[1024,512]{1,0:T(8,128)(2,1)} %refs_6_.3), channel_id=1, source_target_pairs={{0,8},{8,0},{1,9},{9,1},{2,10},{10,2},{3,11},{11,3},{4,12},{12,4},... | collective-permute-start | bytes 3145736 | tf_op jit(solution)/shard_map/ppermute | solution.py:26
  6.4 17.9 %collective-permute-start.3 = (bf16[272,512]{1,0:T(8,128)(2,1)}, bf16[272,512]{1,0:T(8,128)(2,1)S(1)}, u32[]{:S(2)}, u32[]{:S(2)}) collective-permute-start(bf16[272,512]{1,0:T(8,128)(2,1)} %get-tuple-element.23), channel_id=1, source_target_pairs={{0,224},{8,232},{16,240},{24,248},{32,0},{40,8},{48,16},{56,24},{6... | collective-permute-start | bytes 835592 | tf_op jit(solution)/shard_map/ppermute | solution.py:22
  12.0 15.9 %collective-permute-start.2 = (bf16[272,512]{1,0:T(8,128)(2,1)}, bf16[272,512]{1,0:T(8,128)(2,1)S(1)}, u32[]{:S(2)}, u32[]{:S(2)}) collective-permute-start(bf16[272,512]{1,0:T(8,128)(2,1)} %get-tuple-element.23), channel_id=1, source_target_pairs={{0,240},{8,248},{16,0},{24,8},{32,16},{40,24},{48,32},{56,40},{64,... | collective-permute-start | bytes 835592 | tf_op jit(solution)/shard_map/ppermute | solution.py:22
  13.7 1.0 copy-start
  13.7 22.9 %collective-permute-start.1 = (bf16[272,512]{1,0:T(8,128)(2,1)}, bf16[272,512]{1,0:T(8,128)(2,1)S(1)}, u32[]{:S(2)}, u32[]{:S(2)}) collective-permute-start(bf16[272,512]{1,0:T(8,128)(2,1)} %get-tuple-element.22), channel_id=1, source_target_pairs={{0,224},{8,232},{16,240},{24,248},{32,0},{40,8},{48,16},{56,24},{6... | collective-permute-start | bytes 835592 | tf_op jit(solution)/shard_map/ppermute | solution.py:22
  14.7 1.1 copy-start.1
  24.3 0.7 copy-start.7
  27.8 0.7 copy-start.6
  36.6 0.7 copy-start.8
  40.1 26.5 %copy-start.9 = (bf16[272,512]{1,0:T(8,128)(2,1)S(1)}, bf16[272,512]{1,0:T(8,128)(2,1)}, u32[]{:S(2)}) copy-start(bf16[272,512]{1,0:T(8,128)(2,1)} %shard_map.84) | copy-start | bytes 835588
  40.1 26.5 %copy-start.5 = (bf16[272,512]{1,0:T(8,128)(2,1)S(1)}, bf16[272,512]{1,0:T(8,128)(2,1)}, u32[]{:S(2)}) copy-start(bf16[272,512]{1,0:T(8,128)(2,1)} %shard_map.83) | copy-start | bytes 835588
  41.5 14.0 %collective-permute-start.13 = (bf16[256,2048]{1,0:T(8,128)(2,1)S(1)}, bf16[256,2048]{1,0:T(8,128)(2,1)S(1)}, u32[]{:S(2)}, u32[]{:S(2)}) collective-permute-start(bf16[256,2048]{1,0:T(8,128)(2,1)S(1)} %constant_dynamic-slice_fusion), channel_id=1, source_target_pairs={{0,1},{1,2},{2,3},{3,0},{8,11},{9,8},{10,9},{11,10},{4,5},{5,6},{6... | collective-permute-start | bytes 3145736 | tf_op jit(solution)/shard_map/ppermute | solution.py:33
  42.2 53.9 %collective-permute-start.12 = (bf16[512,2048]{1,0:T(8,128)(2,1)}, bf16[512,2048]{1,0:T(8,128)(2,1)S(1)}, u32[]{:S(2)}, u32[]{:S(2)}) collective-permute-start(bf16[512,2048]{1,0:T(8,128)(2,1)} %collective-permute-done.11.refs_5_), channel_id=1, source_target_pairs={{0,8},{8,0},{1,9},{9,1},{2,10},{10,2},{3,11},{11,3},{4,12},{12,4},... | collective-permute-start | bytes 6291464 | tf_op jit(solution)/shard_map/ppermute | solution.py:26
  55.5 35.6 %copy-start.3 = (bf16[256,2048]{1,0:T(8,128)(2,1)}, bf16[256,2048]{1,0:T(8,128)(2,1)S(1)}, u32[]{:S(2)}) copy-start(bf16[256,2048]{1,0:T(8,128)(2,1)S(1)} %collective-permute-done.13.refs_7_) | copy-start | bytes 3145732
  55.5 40.6 %collective-permute-start.14 = (bf16[256,2048]{1,0:T(8,128)(2,1)S(1)}, bf16[256,2048]{1,0:T(8,128)(2,1)}, u32[]{:S(2)}, u32[]{:S(2)}) collective-permute-start(bf16[256,2048]{1,0:T(8,128)(2,1)S(1)} %collective-permute-done.13.refs_7_), channel_id=1, source_target_pairs={{0,8},{8,0},{1,9},{9,1},{2,10},{10,2},{3,11},{11,3},{4,12},{12,4},... | collective-permute-start | bytes 3145736 | tf_op jit(solution)/shard_map/ppermute | solution.py:26
  66.6 12.2 %collective-permute-start.16 = (bf16[272,512]{1,0:T(8,128)(2,1)S(1)}, bf16[272,512]{1,0:T(8,128)(2,1)S(1)}, u32[]{:S(2)}, u32[]{:S(2)}) collective-permute-start(bf16[272,512]{1,0:T(8,128)(2,1)S(1)} %copy-done.9), channel_id=1, source_target_pairs={{0,16},{8,24},{16,32},{24,40},{32,48},{40,56},{48,64},{56,72},{64,... | collective-permute-start | bytes 835592 | tf_op jit(solution)/shard_map/ppermute | solution.py:22
  66.6 12.2 %collective-permute-start.15 = (bf16[272,512]{1,0:T(8,128)(2,1)S(1)}, bf16[272,512]{1,0:T(8,128)(2,1)}, u32[]{:S(2)}, u32[]{:S(2)}) collective-permute-start(bf16[272,512]{1,0:T(8,128)(2,1)S(1)} %copy-done.5), channel_id=1, source_target_pairs={{0,32},{8,40},{16,48},{24,56},{32,64},{40,72},{48,80},{56,88},{64,... | collective-permute-start | bytes 835592 | tf_op jit(solution)/shard_map/ppermute | solution.py:22
  67.4 15.7 %collective-permute-start = (bf16[272,512]{1,0:T(8,128)(2,1)}, bf16[272,512]{1,0:T(8,128)(2,1)}, u32[]{:S(2)}, u32[]{:S(2)}) collective-permute-start(bf16[272,512]{1,0:T(8,128)(2,1)} %get-tuple-element.22), channel_id=1, source_target_pairs={{0,240},{8,248},{16,0},{24,8},{32,16},{40,24},{48,32},{56,40},{64,... | collective-permute-start | bytes 835592 | tf_op jit(solution)/shard_map/ppermute | solution.py:22
  78.8 0.7 copy-start.10
  82.0 9.9 %collective-permute-start.17 = (bf16[64,512]{1,0:T(8,128)(2,1)}, bf16[64,512]{1,0:T(8,128)(2,1)S(1)}, u32[]{:S(2)}, u32[]{:S(2)}) collective-permute-start(bf16[64,512]{1,0:T(8,128)(2,1)} %get-tuple-element.36), channel_id=1, source_target_pairs={{0,1},{1,2},{2,3},{3,0},{4,5},{5,6},{6,7},{7,4},{8,9},{9,10},{10,1... | collective-permute-start | bytes 196616 | tf_op jit(solution)/shard_map/ppermute | solution.py:22
  82.0 9.9 %copy-start.4 = (bf16[272,512]{1,0:T(8,128)(2,1)S(1)}, bf16[272,512]{1,0:T(8,128)(2,1)}, u32[]{:S(2)}) copy-start(bf16[272,512]{1,0:T(8,128)(2,1)} %shard_map.85) | copy-start | bytes 835588
  82.0 10.1 %collective-permute-start.18 = (bf16[64,512]{1,0:T(8,128)(2,1)}, bf16[64,512]{1,0:T(8,128)(2,1)S(1)}, u32[]{:S(2)}, u32[]{:S(2)}) collective-permute-start(bf16[64,512]{1,0:T(8,128)(2,1)} %get-tuple-element.37), channel_id=1, source_target_pairs={{0,2},{1,3},{2,0},{3,1},{4,6},{5,7},{6,4},{7,5},{8,10},{9,11},{10,... | collective-permute-start | bytes 196616 | tf_op jit(solution)/shard_map/ppermute | solution.py:22
  91.2 23.7 %collective-permute-start.7 = (bf16[272,512]{1,0:T(8,128)(2,1)}, bf16[272,512]{1,0:T(8,128)(2,1)}, u32[]{:S(2)}, u32[]{:S(2)}) collective-permute-start(bf16[272,512]{1,0:T(8,128)(2,1)} %shard_map.86), channel_id=1, source_target_pairs={{0,16},{8,24},{16,32},{24,40},{32,48},{40,56},{48,64},{56,72},{64,... | collective-permute-start | bytes 835592 | tf_op jit(solution)/shard_map/ppermute | solution.py:22
  91.9 4.8 %copy-start.12 = (bf16[64,512]{1,0:T(8,128)(2,1)}, bf16[64,512]{1,0:T(8,128)(2,1)S(1)}, u32[]{:S(2)}) copy-start(bf16[64,512]{1,0:T(8,128)(2,1)S(1)} %collective-permute-done.17.refs_1_) | copy-start | bytes 196612
  91.9 23.0 %collective-permute-start.6 = (bf16[272,512]{1,0:T(8,128)(2,1)S(1)}, bf16[272,512]{1,0:T(8,128)(2,1)}, u32[]{:S(2)}, u32[]{:S(2)}) collective-permute-start(bf16[272,512]{1,0:T(8,128)(2,1)S(1)} %copy-done.4), channel_id=1, source_target_pairs={{0,32},{8,40},{16,48},{24,56},{32,64},{40,72},{48,80},{56,88},{64,... | collective-permute-start | bytes 835592 | tf_op jit(solution)/shard_map/ppermute | solution.py:22
  92.1 4.6 %copy-start.13 = (bf16[64,512]{1,0:T(8,128)(2,1)}, bf16[64,512]{1,0:T(8,128)(2,1)S(1)}, u32[]{:S(2)}) copy-start(bf16[64,512]{1,0:T(8,128)(2,1)S(1)} %collective-permute-done.18.refs_2_) | copy-start | bytes 196612
  92.1 4.0 %collective-permute-start.19 = (bf16[64,512]{1,0:T(8,128)(2,1)}, bf16[64,512]{1,0:T(8,128)(2,1)S(1)}, u32[]{:S(2)}, u32[]{:S(2)}) collective-permute-start(bf16[64,512]{1,0:T(8,128)(2,1)} %get-tuple-element.38), channel_id=1, source_target_pairs={{0,3},{1,0},{2,1},{3,2},{4,7},{5,4},{6,5},{7,6},{8,11},{9,8},{10,9... | collective-permute-start | bytes 196616 | tf_op jit(solution)/shard_map/ppermute | solution.py:22
  96.1 0.6 copy-start.17
  96.7 1.3 %copy-start.2 = (bf16[512,2048]{1,0:T(8,128)(2,1)}, bf16[512,2048]{1,0:T(8,128)(2,1)S(1)}, u32[]{:S(2)}) copy-start(bf16[512,2048]{1,0:T(8,128)(2,1)S(1)} %collective-permute-done.12.refs_6_) | copy-start | bytes 6291460
  103.7 20.9 %collective-permute-start.20 = (bf16[64,2048]{1,0:T(8,128)(2,1)}, bf16[64,2048]{1,0:T(8,128)(2,1)S(1)}, u32[]{:S(2)}, u32[]{:S(2)}) collective-permute-start(bf16[64,2048]{1,0:T(8,128)(2,1)} %shard_map.88), channel_id=1, source_target_pairs={{0,4},{4,0},{1,5},{5,1},{2,6},{6,2},{3,7},{7,3},{8,12},{12,8},{9,1... | collective-permute-start | bytes 786440 | tf_op jit(solution)/shard_map/ppermute | solution.py:26
  117.4 4.5 %collective-permute-start.8 = (bf16[64,512]{1,0:T(8,128)(2,1)}, bf16[64,512]{1,0:T(8,128)(2,1)S(1)}, u32[]{:S(2)}, u32[]{:S(2)}) collective-permute-start(bf16[64,512]{1,0:T(8,128)(2,1)} %get-tuple-element.30), channel_id=1, source_target_pairs={{0,1},{1,2},{2,3},{3,0},{4,5},{5,6},{6,7},{7,4},{8,9},{9,10},{10,1... | collective-permute-start | bytes 196616 | tf_op jit(solution)/shard_map/ppermute | solution.py:22
  118.8 4.8 %collective-permute-start.9 = (bf16[64,512]{1,0:T(8,128)(2,1)}, bf16[64,512]{1,0:T(8,128)(2,1)S(1)}, u32[]{:S(2)}, u32[]{:S(2)}) collective-permute-start(bf16[64,512]{1,0:T(8,128)(2,1)} %get-tuple-element.31), channel_id=1, source_target_pairs={{0,2},{1,3},{2,0},{3,1},{4,6},{5,7},{6,4},{7,5},{8,10},{9,11},{10,... | collective-permute-start | bytes 196616 | tf_op jit(solution)/shard_map/ppermute | solution.py:22
  121.0 3.6 %collective-permute-start.10 = (bf16[64,512]{1,0:T(8,128)(2,1)}, bf16[64,512]{1,0:T(8,128)(2,1)S(1)}, u32[]{:S(2)}, u32[]{:S(2)}) collective-permute-start(bf16[64,512]{1,0:T(8,128)(2,1)} %get-tuple-element.32), channel_id=1, source_target_pairs={{0,3},{1,0},{2,1},{3,2},{4,7},{5,4},{6,5},{7,6},{8,11},{9,8},{10,9... | collective-permute-start | bytes 196616 | tf_op jit(solution)/shard_map/ppermute | solution.py:22
  121.9 2.7 %copy-start.14 = (bf16[64,512]{1,0:T(8,128)(2,1)}, bf16[64,512]{1,0:T(8,128)(2,1)S(1)}, u32[]{:S(2)}) copy-start(bf16[64,512]{1,0:T(8,128)(2,1)S(1)} %collective-permute-done.8.refs_1_) | copy-start | bytes 196612
  123.7 0.9 copy-start.15
  124.6 0.6 copy-start.16
  124.6 0.7 copy-start.11

commit v3 on v0

v3 whole, which is shorter than its diff:
```python
import math

import jax
import jax.numpy as jnp
from jax import lax
from jax.experimental import pallas as pl
from jax.experimental.pallas import tpu as pltpu
from jax.sharding import Mesh
from jax.sharding import PartitionSpec as P

DH = 128
DOC = ("z", "yl", "core")
HEAD = ("yh", "x")
NEG = -1e30
KEY_CHUNK = 512
TAIL = 16
SCALE = math.log2(math.e) / math.sqrt(DH)

VMEM_LIMIT = 24 * 2**20


def shift(value, axis, steps):
    count = lax.axis_size(axis)
    return lax.ppermute(value, axis, [(i, (i + steps) % count) for i in range(count)])


def swap(value, axis):
    return lax.ppermute(value, axis, [(0, 1), (1, 0)])


def part_ways(value):
    count = lax.axis_size("x")
    up = [(i, (i + 1) % count) for i in range(count)]
    down = [(count + i, count + (i - 1) % count) for i in range(count)]
    return lax.ppermute(value, ("core", "x"), up + down)


def lanes(x, width):
    return jnp.concatenate([x] * (width // DH), axis=1)


def scores_of(q, k):
    return lax.dot_general(q, k, (((1,), (1,)), ((), ())), preferred_element_type=jnp.float32) * SCALE


def with_ones(v):
    return jnp.concatenate([v, jnp.ones(v.shape, v.dtype)], axis=1)


def absorb(h, s, v, m_ref, acc_ref):
    m_old = m_ref[h]
    m_new = jnp.maximum(m_old, jnp.max(s, axis=1, keepdims=True))
    p = jnp.exp2(s - lanes(m_new, s.shape[1])).astype(jnp.bfloat16)
    pv = jnp.dot(p, with_ones(v), preferred_element_type=jnp.float32)
    acc_ref[h] = acc_ref[h] * lanes(jnp.exp2(m_old - m_new), 2 * DH) + pv
    m_ref[h] = m_new


def reset(m_ref, acc_ref):
    m_ref[...] = jnp.full(m_ref.shape, NEG, jnp.float32)
    acc_ref[...] = jnp.zeros(acc_ref.shape, jnp.float32)


def log2_count(count):
    return jnp.where(count >= 4, 2.0, jnp.where(count >= 3, math.log2(3), jnp.where(count >= 2, 1.0, 0.0)))


def of_head(h):
    return slice(h * DH, (h + 1) * DH)


def absorb_memories(memories, lengths, counts, queries, m_ref, acc_ref):
    for (keys, values), length, count in zip(memories, lengths, counts):
        live, weight = jnp.where(count > 0, length, 0), log2_count(count)

        def fold(chunk, carry, keys=keys, values=values, live=live, weight=weight):
            start = pl.multiple_of(chunk * KEY_CHUNK, KEY_CHUNK)
            row = lax.broadcasted_iota(jnp.int32, (1, KEY_CHUNK), 1) + start
            bias = jnp.where(row < live, weight, NEG)
            for h in range(m_ref.shape[0]):
                k, v = (a[pl.ds(start, KEY_CHUNK), of_head(h)] for a in (keys, values))
                absorb(h, scores_of(queries(h), k) + bias, v, m_ref, acc_ref)
            return carry

        lax.fori_loop(0, (live + KEY_CHUNK - 1) // KEY_CHUNK, fold, 0)


def finish(out_ref, level_ref, m_ref, acc_ref):
    heads, rows = m_ref.shape[:2]
    level_ref[...] = jnp.zeros(level_ref.shape, jnp.float32)
    for h in range(heads):
        total = acc_ref[h, :, DH:]
        seen = total > 0
        safe = jnp.where(seen, total, 1.0)
        out_ref[:rows, of_head(h)] = (acc_ref[h, :, :DH] / safe).astype(jnp.bfloat16)
        rest = jnp.where(seen, m_ref[h] + jnp.log2(safe), NEG).T[:1, :]
        for i in range(3):
            term = rest.astype(jnp.bfloat16).astype(jnp.float32)
            level_ref[3 * h + i : 3 * h + i + 1, :rows] = term
            rest = rest - term
    out_ref[rows:, :] = level_ref[...].astype(jnp.bfloat16)


def home_kernel(offsets, lengths, q_ref, lk_ref, lv_ref, k0, v0, k1, v1, out_ref, m_ref, acc_ref, level_ref, *, half):
    core, document = lax.axis_index("core"), lax.axis_index(DOC)
    heads, rows = m_ref.shape[:2]
    first, keys = half * rows, (half + 1) * rows
    count = sum(jnp.where((offsets[0, i] == 1) & (core == 1), 1, 0) for i in range(offsets.shape[1]))
    reset(m_ref, acc_ref)

    def queries(h):
        return q_ref[first : first + rows, of_head(h)]

    seen = lax.broadcasted_iota(jnp.int32, (rows, keys), 0) + first >= lax.broadcasted_iota(jnp.int32, (rows, keys), 1)
    for h in range(heads):
        s = jnp.where(seen, scores_of(queries(h), lk_ref[:keys, of_head(h)]), NEG)
        absorb(h, s, lv_ref[:keys, of_head(h)], m_ref, acc_ref)
    live = lengths[document], lengths[document + 1 - 2 * core]
    absorb_memories(((k0, v0), (k1, v1)), live, (jnp.int32(1), count), queries, m_ref, acc_ref)
    finish(out_ref, level_ref, m_ref, acc_ref)


def guest_kernel(offsets, lengths, q_ref, k0, v0, k1, v1, *refs, back):
    *extra, m_ref, acc_ref, level_ref = refs
    core, document = lax.axis_index("core"), lax.axis_index(DOC)
    reset(m_ref, acc_ref)
    counts = [
        sum(jnp.where(offsets[0, i] == wanted, 1, 0) for i in range(offsets.shape[1]))
        for wanted in (back, back - 1 + 2 * core)
    ]
    live = lengths[document], lengths[document + 1 - 2 * core]
    absorb_memories(((k0, v0), (k1, v1)), live, counts, lambda h: q_ref[:, of_head(h)], m_ref, acc_ref)
    if len(extra) == 3:
        weights, out_ref, half_ref = extra
        half = half_ref.shape[0]
        half_ref[...] = weights[pl.ds(pl.multiple_of(core * half, half), half), :]
    else:
        (out_ref,) = extra
    finish(out_ref, level_ref, m_ref, acc_ref)


def on_chip(value):
    return pltpu.with_memory_space_constraint(value, pltpu.VMEM)


def kernel_call(kernel, scalars, arrays, outs, scratch):
    space = pl.BlockSpec(memory_space=pltpu.VMEM)
    return pl.pallas_call(
        kernel,
        grid_spec=pltpu.PrefetchScalarGridSpec(
            num_scalar_prefetch=len(scalars),
            grid=(),
            in_specs=[space] * len(arrays),
            out_specs=[space] * len(outs),
            scratch_shapes=scratch,
        ),
        out_shape=[pltpu.VMEM(shape, jnp.bfloat16) for shape in outs],
        compiler_params=pltpu.CompilerParams(vmem_limit_bytes=VMEM_LIMIT),
    )(*scalars, *arrays)


def attention(kernel, scalars, arrays, rows, width, extra=()):
    heads = width // DH
    scratch = [
        pltpu.VMEM((heads, rows, DH), jnp.float32),
        pltpu.VMEM((heads, rows, 2 * DH), jnp.float32),
        pltpu.VMEM((TAIL, width), jnp.float32),
    ]
    return kernel_call(kernel, scalars, arrays, [(rows + TAIL, width), *extra], scratch)


def merge_kernel(*refs):
    *homes, far_ref, near_ref = refs[:4]
    *tiles, share_ref, whole_ref = refs[4:]
    rows, width = whole_ref.shape
    heads, count = width // DH, len(tiles)
    half = rows // 2
    for n, home_ref in enumerate(homes):
        span = slice(n * half, (n + 1) * half)
        parts = [(home_ref, slice(0, half)), (far_ref, span), (near_ref, span)]
        tails = [part[-TAIL:, where].astype(jnp.float32) for part, where in parts]
        for h in range(heads):
            levels = [tail[3 * h : 3 * h + 1] + tail[3 * h + 1 : 3 * h + 2] + tail[3 * h + 2 : 3 * h + 3] for tail in tails]
            top = jnp.maximum(jnp.maximum(levels[0], levels[1]), levels[2])
            shares = [jnp.exp2(level - top) for level in levels]
            total = shares[0] + shares[1] + shares[2]
            for i, share in enumerate(shares):
                share_ref[n, 3 * h + i : 3 * h + i + 1, :] = share / total
        columns = share_ref[n].T
        for h in range(heads):
            mixed = 0.0
            for i, (part, where) in enumerate(parts):
                mixed = mixed + columns[:, 3 * h + i : 3 * h + i + 1] * part[where, of_head(h)].astype(jnp.float32)
            whole_ref[span, of_head(h)] = mixed.astype(whole_ref.dtype)
    block = half // count
    x, yh = lax.axis_index("x"), lax.axis_index("yh")
    for k, tile in enumerate(tiles):
        for n, side in enumerate((1 - yh, yh)):
            first = side * half + (x + k) % count * block
            tile[n * block : (n + 1) * block, :] = whole_ref[pl.ds(pl.multiple_of(first, block), block), :]


def merge(home0, home1, far, near):
    rows, width = far.shape[0] - TAIL, far.shape[1]
    count = lax.axis_size("x")
    scratch = [pltpu.VMEM((2, DH, rows // 2), jnp.float32), pltpu.VMEM((rows, width), jnp.bfloat16)]
    return kernel_call(merge_kernel, (), (home0, home1, far, near), [(rows // count, width)] * count, scratch)


def project_kernel(*refs, part):
    mine, below, opposite, above, own, near, near_other, far, far_other, *extra, out_ref = refs
    rows, half = out_ref.shape[0], far.shape[0]
    core = lax.axis_index("core")

    def tile(ref):
        return ref[part * rows : (part + 1) * rows, :]

    pairs = [
        (tile(mine), own),
        (jnp.where(core == 0, tile(below), tile(above)), near),
        (jnp.where(core == 0, tile(above), tile(below)), near_other),
        (jnp.where(core == 0, tile(opposite)[:, :half], tile(opposite)[:, half:]), far),
        (jnp.where(core == 0, tile(opposite)[:, half:], tile(opposite)[:, :half]), far_other),
    ]
    acc = sum(jnp.dot(a, w[...], preferred_element_type=jnp.float32) for a, w in pairs)
    for ref in extra:
        acc = acc + ref[...].astype(jnp.float32)
    out_ref[...] = acc.astype(out_ref.dtype)


def project(tiles, weights, extra, part):
    def kernel(*refs):
        project_kernel(*refs, part=part)

    out = (tiles[0].shape[0] // 2, weights[0].shape[1])
    return kernel_call(kernel, (), (*tiles, *weights, *extra), [out], [])[0]


def after(value, *others):
    return lax.optimization_barrier((value, *others))[0]


def step(queries, local_keys, local_values, mem_keys, mem_values, offsets, mem_lengths, out_weight):
    rows, width = queries.shape

    def moved(move, value, *where):
        value = move(value, *where)
        return on_chip(value) if value.dtype == jnp.bfloat16 else value

    query_far = moved(shift, queries, DOC, -4)
    query_near = moved(shift, queries, DOC, -2)
    offsets_far = moved(shift, offsets, DOC, -4)
    offsets_near = moved(shift, offsets, DOC, -2)
    other_keys = moved(swap, mem_keys, "core")
    other_values = moved(swap, mem_values, "core")
    memory = (on_chip(mem_keys), on_chip(mem_values), other_keys, other_values)
    local = (on_chip(queries), on_chip(local_keys), on_chip(local_values))
    near_weight = moved(part_ways, out_weight)

    def at_home(local, half):
        def kernel(*refs):
            home_kernel(*refs, half=half)

        return attention(kernel, (offsets, mem_lengths), (*local, *memory), rows // 2, width)[0]

    def guest(load, table, back, *weights):
        def kernel(*refs):
            guest_kernel(*refs, back=back)

        extra = [(w.shape[0] // 2, w.shape[1]) for w in weights]
        out, *rest = attention(kernel, (table, mem_lengths), (load, *memory, *weights), rows, width, extra)
        return moved(shift, out, DOC, back), out, *rest

    home0 = at_home(local, 0)
    from_far, far, *_ = guest(after(query_far, home0), offsets_far, 4)
    from_near, near, passed_on = guest(after(query_near, far), offsets_near, 2, near_weight)
    home1 = at_home((after(local[0], near), *local[1:]), 1)

    far_weight = moved(part_ways, passed_on)
    weights = [
        on_chip(out_weight),
        near_weight,
        moved(swap, after(near_weight, near), "core"),
        far_weight,
        moved(swap, far_weight, "core"),
    ]

    mine, *tiles = merge(home0, home1, from_far, from_near)
    tiles = mine, *(moved(shift, tile, "x", k) for k, tile in enumerate(tiles, 1))
    given = project(tiles, weights, (), 0)
    taken = swap(given, "yh")
    kept = project(tiles, weights, (), 1)
    return (kept.astype(jnp.float32) + taken.astype(jnp.float32)).astype(jnp.bfloat16)


def solution(mesh):
    split = Mesh(mesh.devices.reshape(-1, 2, 2, 2, 4), (*DOC, *HEAD))
    placed = (
        P(DOC, HEAD),
        P(DOC, HEAD),
        P(DOC, HEAD),
        P(DOC, HEAD),
        P(DOC, HEAD),
        P(DOC, None),
        P(),
        P(HEAD, None),
    )
    return jax.shard_map(step, mesh=split, in_specs=placed, out_specs=P((*DOC, *HEAD), None), check_vma=False)
```

time: 247 us -> 104 us (0.42)
  waiting for transfers between devices: 110 us -> 33.3 us
  matrix products: 42.7 us -> 0 us
  local copies, waits for them, and re-layouts: 32.8 us -> 6.89 us
  Pallas kernels: 0 us -> 24.5 us
  other arithmetic: 24.3 us -> 0.77 us
  starting transfers between devices: 17.8 us -> 37 us
  between operations: 18.7 us -> 0.08 us
    reduce_scatter x2 -> x0, waiting for transfers between devices: 59.2 us -> none  [own_block(): tiles = lax.psum_scatter(tiles, axes[k], scatter_dimension=0, tiled=True)]
    dot_general x9 -> x0, matrix products: 42.7 us -> none  [the longest x4 20.8 us: one_head(): jnp.einsum('qd,kd->qk', query_head, key_head, preferred_element_type=jnp....]
    pallas_call x0 -> x7, Pallas kernels: none -> 24.5 us  [kernel_call(): pl.pallas_call(kernel, grid_spec=pltpu.PrefetchScalarGridSpec(num_scalar_...]
    unnamed x29 -> x20, local copies, waits for them, and re-layouts: 26.2 us -> 6.89 us
    ppermute x8 -> x16, starting transfers between devices: 17.8 us -> 37 us  [the longest x5 21 us: swap(): return lax.ppermute(value, axis, [(0, 1), (1, 0)])]
    ppermute x8 -> x16, waiting for transfers between devices: 50.4 us -> 33.3 us  [the longest x9 24.2 us: shift(): lax.ppermute(value, axis, [(i, (i + steps) % count) for i in range(count)])]
    reduce_sum x5 -> x0, other arithmetic: 16.2 us -> none  [the longest x4 15.4 us: one_head(): jnp.sum(exponent, axis=-1, keepdims=True)]
    another operation x2 -> x0, other arithmetic: 4.77 us -> none  [the longest x1 2.65 us: per_device(): key_stack = jnp.stack([entry[0] for entry in fetched])]
  transfers between devices with their start and end apart: 10 -> 16, of which waited for: 8 -> 7; matrix products, arithmetic and copies ran while one was open for 9% -> 0% of each run, Pallas kernels for 0% -> 15%
where the time goes in v3:
time: 104 us; the launch traced here: 103 us
  starting transfers between devices  37 us (36%)
  waiting for transfers between devices  33.3 us (32%)
  Pallas kernels  24.5 us (24%)
  local copies, waits for them, and re-layouts  6.89 us (7%)
    pallas_call x7, Pallas kernels, kernel_call(): pl.pallas_call(kernel, grid_spec=pltpu.PrefetchScalarGridSpec(num_scalar_...  24.5 us
    ppermute x9, waiting for transfers between devices, shift(): lax.ppermute(value, axis, [(i, (i + steps) % count) for i in range(count)])  24.2 us
    ppermute x5, starting transfers between devices, swap(): return lax.ppermute(value, axis, [(0, 1), (1, 0)])  21 us
    ppermute x9, starting transfers between devices, shift(): lax.ppermute(value, axis, [(i, (i + steps) % count) for i in range(count)])  12.4 us
    unnamed x20, local copies, waits for them, and re-layouts  6.89 us
    ppermute x2, waiting for transfers between devices, part_ways(): return lax.ppermute(value, ('core', 'x'), up + down)  5.8 us
    ppermute x2, starting transfers between devices, part_ways(): return lax.ppermute(value, ('core', 'x'), up + down)  3.51 us
    ppermute x5, waiting for transfers between devices, swap(): return lax.ppermute(value, axis, [(0, 1), (1, 0)])  3.23 us
  transfers between devices with their start and end apart: 16, of which 7 were waited for; matrix products, arithmetic and copies ran while one was open for 0% of the time, Pallas kernels for 15%

profile of v3, /device:TPU:1, one launch (start us, length us, event | category | flops | bytes accessed | tf_op | source)
XLA Modules:
  0.0 102.5 jit_solution(14733055816655373374)
XLA Ops:
  0.0 3.3 %collective-permute-start.6 = (bf16[512,2048]{1,0:T(8,128)(2,1)}, bf16[512,2048]{1,0:T(8,128)(2,1)S(1)}, u32[]{:S(2)}, u32[]{:S(2)}) collective-permute-start(bf16[512,2048]{1,0:T(8,128)(2,1)} %refs_4_.11), channel_id=1, source_target_pairs={{0,1},{1,2},{2,3},{3,0},{8,11},{9,8},{10,9},{11,10},{4,5},{5,6},{6... | collective-permute-start | bytes 6291464 | tf_op jit(solution)/shard_map/ppermute | solution.py:35
  3.3 0.0 collective-permute-start
  3.3 0.5 collective-permute-start.1
  3.8 5.6 %collective-permute-start.5 = (bf16[512,512]{1,0:T(8,128)(2,1)}, bf16[512,512]{1,0:T(8,128)(2,1)S(1)}, u32[]{:S(2)}, u32[]{:S(2)}) collective-permute-start(bf16[512,512]{1,0:T(8,128)(2,1)} %refs_2_.2), channel_id=1, source_target_pairs={{0,224},{8,232},{16,240},{24,248},{32,0},{40,8},{48,16},{56,24},{6... | collective-permute-start | bytes 1572872 | tf_op jit(solution)/shard_map/ppermute | solution.py:24
  9.4 1.7 %collective-permute-start.3 = (bf16[512,512]{1,0:T(8,128)(2,1)}, bf16[512,512]{1,0:T(8,128)(2,1)S(1)}, u32[]{:S(2)}, u32[]{:S(2)}) collective-permute-start(bf16[512,512]{1,0:T(8,128)(2,1)} %refs_2_.2), channel_id=1, source_target_pairs={{0,240},{8,248},{16,0},{24,8},{32,16},{40,24},{48,32},{56,40},{64,... | collective-permute-start | bytes 1572872 | tf_op jit(solution)/shard_map/ppermute | solution.py:24
  11.1 0.0 collective-permute-done.refs_7_.refs_5_
  11.1 1.6 %collective-permute-start.2 = (s32[1,4]{1,0:T(1,128)}, s32[1,4]{1,0:T(1,128)S(1)}, u32[]{:S(2)}, u32[]{:S(2)}) collective-permute-start(s32[1,4]{1,0:T(1,128)} %refs_0_.3), channel_id=1, source_target_pairs={{0,240},{8,248},{16,0},{24,8},{32,16},{40,24},{48,32},{56,40},{64,... | collective-permute-start | bytes 56 | tf_op jit(solution)/shard_map/ppermute | solution.py:24
  12.8 0.0 collective-permute-done.1.refs_8_.refs_6_
  12.8 0.7 collective-permute-start.4
  13.5 0.0 copy-start
  13.5 1.2 %copy-done = bf16[1024,512]{1,0:T(8,128)(2,1)S(1)} copy-done((bf16[1024,512]{1,0:T(8,128)(2,1)S(1)}, bf16[1024,512]{1,0:T(8,128)(2,1)}, u32[]{:S(2)}) %copy-start) | copy-done | bytes 1048600
  14.7 0.0 copy-start.2
  14.7 1.2 %copy-done.2 = bf16[1024,512]{1,0:T(8,128)(2,1)S(1)} copy-done((bf16[1024,512]{1,0:T(8,128)(2,1)S(1)}, bf16[1024,512]{1,0:T(8,128)(2,1)}, u32[]{:S(2)}) %copy-start.2) | copy-done | bytes 1048600
  15.9 0.0 copy-start.5
  15.9 1.0 %copy-done.5 = bf16[512,512]{1,0:T(8,128)(2,1)S(1)} copy-done((bf16[512,512]{1,0:T(8,128)(2,1)S(1)}, bf16[512,512]{1,0:T(8,128)(2,1)}, u32[]{:S(2)}) %copy-start.5) | copy-done | bytes 524312
  17.0 0.0 copy-start.6
  17.0 1.0 %copy-done.6 = bf16[512,512]{1,0:T(8,128)(2,1)S(1)} copy-done((bf16[512,512]{1,0:T(8,128)(2,1)S(1)}, bf16[512,512]{1,0:T(8,128)(2,1)}, u32[]{:S(2)}) %copy-start.6) | copy-done | bytes 524312
  18.0 0.0 copy-start.7
  18.0 1.0 %copy-done.7 = bf16[512,512]{1,0:T(8,128)(2,1)S(1)} copy-done((bf16[512,512]{1,0:T(8,128)(2,1)S(1)}, bf16[512,512]{1,0:T(8,128)(2,1)}, u32[]{:S(2)}) %copy-start.7) | copy-done | bytes 524312
  19.1 0.0 copy-start.8
  19.1 0.7 copy-done.8
  19.7 0.0 copy-start.9
  19.7 0.7 copy-done.9
  20.4 0.0 copy-start.1
  20.4 0.0 copy-start.3
  20.4 5.4 %shard_map.82.refs_0_ = bf16[272,512]{1,0:T(8,128)(2,1)S(1)} custom-call(s32[1,4]{1,0:T(1,128)S(1)} %copy-done.9, s32[32]{0:T(128)S(1)} %copy-done.8, bf16[512,512]{1,0:T(8,128)(2,1)S(1)} %copy-done.5, bf16[512,512]{1,0:T(8,128)(2,1)S(1)} %copy-done.6, bf16[512,512]{1,0:T(8,128)(2,1)S(1)} %copy-done.7, bf16[1024,512]{1,0:T(8,128)(2,1)S(1)} %copy-done, ...), custom_call_target="tpu_custom_call" | custom-call | tf_op jit(solution)/shard_map/pallas_call | solution.py:148
  25.8 0.0 collective-permute-done.5.refs_2_
  25.8 6.4 %collective-permute-done.4.refs_0_ = s32[1,4]{1,0:T(1,128)S(1)} collective-permute-done((s32[1,4]{1,0:T(1,128)}, s32[1,4]{1,0:T(1,128)S(1)}, u32[]{:S(2)}, u32[]{:S(2)}) %collective-permute-start.4) | collective-permute-done | bytes 48 | tf_op jit(solution)/shard_map/ppermute | solution.py:24
  32.2 0.0 copy-done.1
  32.2 0.0 copy-done.3
  32.2 1.1 %shard_map.83 = bf16[528,512]{1,0:T(8,128)(2,1)S(1)} custom-call(s32[1,4]{1,0:T(1,128)S(1)} %collective-permute-done.4.refs_0_, s32[32]{0:T(128)S(1)} %copy-done.8, bf16[512,512]{1,0:T(8,128)(2,1)S(1)} %collective-permute-done.5.refs_2_, bf16[1024,512]{1,0:T(8,128)(2,1)S(1)} %copy-done.1, bf16[1024,512]{1,0:T(8,128)(2,1)S(1)} %copy-done.3, ...), custom_call_target="tpu_custom_call" | custom-call | tf_op jit(solution)/shard_map/pallas_call | solution.py:148
  33.3 0.0 collective-permute-done.3.refs_2_
  33.3 0.0 collective-permute-done.2.refs_0_
  33.3 0.0 collective-permute-done.6.refs_7_.refs_5_
  33.3 7.9 %shard_map.84 = (bf16[528,512]{1,0:T(8,128)(2,1)S(1)}, bf16[256,2048]{1,0:T(8,128)(2,1)S(1)}) custom-call(s32[1,4]{1,0:T(1,128)S(1)} %collective-permute-done.2.refs_0_, s32[32]{0:T(128)S(1)} %copy-done.8, bf16[512,512]{1,0:T(8,128)(2,1)S(1)} %collective-permute-done.3.refs_2_, bf16[1024,512]{1,0:T(8,128)(2,1)S(1)} %copy-done.1, ...), custom_call_target="tpu_custom_call" | custom-call | tf_op jit(solution)/shard_map/pallas_call | solution.py:148
  41.2 0.2 collective-permute-start.13
  41.4 8.0 %collective-permute-start.12 = (bf16[512,2048]{1,0:T(8,128)(2,1)S(1)}, bf16[512,2048]{1,0:T(8,128)(2,1)S(1)}, u32[]{:S(2)}, u32[]{:S(2)}) collective-permute-start(bf16[512,2048]{1,0:T(8,128)(2,1)S(1)} %collective-permute-done.6.refs_7_.refs_5_), channel_id=1, source_target_pairs={{0,8},{8,0},{1,9},{9,1},{2,10},{10,2},{3,11},{11,3},{4,12},{12,4},... | collective-permute-start | bytes 6291464 | tf_op jit(solution)/shard_map/ppermute | solution.py:28
  49.4 5.8 %collective-permute-done.13.refs_7_ = bf16[256,2048]{1,0:T(8,128)(2,1)S(1)} collective-permute-done((bf16[256,2048]{1,0:T(8,128)(2,1)S(1)}, bf16[256,2048]{1,0:T(8,128)(2,1)S(1)}, u32[]{:S(2)}, u32[]{:S(2)}) %collective-permute-start.13) | collective-permute-done | bytes 1048608 | tf_op jit(solution)/shard_map/ppermute | solution.py:35
  55.2 9.5 %collective-permute-start.14 = (bf16[256,2048]{1,0:T(8,128)(2,1)S(1)}, bf16[256,2048]{1,0:T(8,128)(2,1)S(1)}, u32[]{:S(2)}, u32[]{:S(2)}) collective-permute-start(bf16[256,2048]{1,0:T(8,128)(2,1)S(1)} %collective-permute-done.13.refs_7_), channel_id=1, source_target_pairs={{0,8},{8,0},{1,9},{9,1},{2,10},{10,2},{3,11},{11,3},{4,12},{12,4},... | collective-permute-start | bytes 3145736 | tf_op jit(solution)/shard_map/ppermute | solution.py:28
  64.8 0.0 collective-permute-start.7
  64.8 0.0 collective-permute-start.8
  64.8 0.0 copy-start.4
  64.8 5.8 %shard_map.85.refs_1_ = bf16[272,512]{1,0:T(8,128)(2,1)S(1)} custom-call(s32[1,4]{1,0:T(1,128)S(1)} %copy-done.9, s32[32]{0:T(128)S(1)} %copy-done.8, bf16[512,512]{1,0:T(8,128)(2,1)S(1)} %copy-done.5, bf16[512,512]{1,0:T(8,128)(2,1)S(1)} %copy-done.6, bf16[512,512]{1,0:T(8,128)(2,1)S(1)} %copy-done.7, bf16[1024,512]{1,0:T(8,128)(2,1)S(1)} %copy-done.1, ...), custom_call_target="tpu_custom_call" | custom-call | tf_op jit(solution)/shard_map/pallas_call | solution.py:148
  70.6 9.2 %collective-permute-done.7.refs_2_ = bf16[528,512]{1,0:T(8,128)(2,1)S(1)} collective-permute-done((bf16[528,512]{1,0:T(8,128)(2,1)S(1)}, bf16[528,512]{1,0:T(8,128)(2,1)S(1)}, u32[]{:S(2)}, u32[]{:S(2)}) %collective-permute-start.7) | collective-permute-done | bytes 540704 | tf_op jit(solution)/shard_map/ppermute | solution.py:24
  79.8 2.5 %collective-permute-done.8.refs_3_ = bf16[528,512]{1,0:T(8,128)(2,1)S(1)} collective-permute-done((bf16[528,512]{1,0:T(8,128)(2,1)S(1)}, bf16[528,512]{1,0:T(8,128)(2,1)S(1)}, u32[]{:S(2)}, u32[]{:S(2)}) %collective-permute-start.8) | collective-permute-done | bytes 540704 | tf_op jit(solution)/shard_map/ppermute | solution.py:24
  82.3 1.1 %shard_map.86 = (bf16[128,512]{1,0:T(8,128)(2,1)S(1)}, bf16[128,512]{1,0:T(8,128)(2,1)S(1)}, bf16[128,512]{1,0:T(8,128)(2,1)S(1)}, bf16[128,512]{1,0:T(8,128)(2,1)S(1)}) custom-call(bf16[272,512]{1,0:T(8,128)(2,1)S(1)} %shard_map.82.refs_0_, bf16[272,512]{1,0:T(8,128)(2,1)S(1)} %shard_map.85.refs_1_, bf16[528,512]{1,0:T(8,128)(2,1)S(1)} %collective-permute-done.7.refs_2_, ...), custom_call_target="tpu_custom_call" | custom-call | tf_op jit(solution)/shard_map/pallas_call | solution.py:148
  83.4 0.1 collective-permute-start.9
  83.5 0.7 collective-permute-start.10
  84.2 1.9 %collective-permute-start.11 = (bf16[128,512]{1,0:T(8,128)(2,1)S(1)}, bf16[128,512]{1,0:T(8,128)(2,1)S(1)}, u32[]{:S(2)}, u32[]{:S(2)}) collective-permute-start(bf16[128,512]{1,0:T(8,128)(2,1)S(1)} %get-tuple-element.22), channel_id=1, source_target_pairs={{0,3},{1,0},{2,1},{3,2},{4,7},{5,4},{6,5},{7,6},{8,11},{9,8},{10,9... | collective-permute-start | bytes 393224 | tf_op jit(solution)/shard_map/ppermute | solution.py:24
  86.2 6.0 %collective-permute-done.9.refs_1_ = bf16[128,512]{1,0:T(8,128)(2,1)S(1)} collective-permute-done((bf16[128,512]{1,0:T(8,128)(2,1)S(1)}, bf16[128,512]{1,0:T(8,128)(2,1)S(1)}, u32[]{:S(2)}, u32[]{:S(2)}) %collective-permute-start.9) | collective-permute-done | bytes 131104 | tf_op jit(solution)/shard_map/ppermute | solution.py:24
  92.2 0.0 collective-permute-done.10.refs_2_
  92.2 0.2 collective-permute-done.11.refs_3_
  92.4 0.0 collective-permute-done.14.refs_8_
  92.4 0.0 collective-permute-done.12.refs_6_
  92.4 0.0 copy-done.4
  92.4 1.6 %shard_map.88 = bf16[64,2048]{1,0:T(8,128)(2,1)S(1)} custom-call(bf16[128,512]{1,0:T(8,128)(2,1)S(1)} %get-tuple-element.19.refs_0_, bf16[128,512]{1,0:T(8,128)(2,1)S(1)} %collective-permute-done.9.refs_1_, bf16[128,512]{1,0:T(8,128)(2,1)S(1)} %collective-permute-done.10.refs_2_, bf16[128,512]{1,0:T(8,128)(2,1)S(1)} %collective-permute-done.11.refs_3_, ...), custom_call_target="tpu_custom_call" | custom-call | tf_op jit(solution)/shard_map/pallas_call | solution.py:148
  94.0 3.0 %collective-permute-start.15 = (bf16[64,2048]{1,0:T(8,128)(2,1)S(1)}, bf16[64,2048]{1,0:T(8,128)(2,1)S(1)}, u32[]{:S(2)}, u32[]{:S(2)}) collective-permute-start(bf16[64,2048]{1,0:T(8,128)(2,1)S(1)} %shard_map.88), channel_id=1, source_target_pairs={{0,4},{4,0},{1,5},{5,1},{2,6},{6,2},{3,7},{7,3},{8,12},{12,8},{9,1... | collective-permute-start | bytes 786440 | tf_op jit(solution)/shard_map/ppermute | solution.py:28
  97.0 1.6 %shard_map.87 = bf16[64,2048]{1,0:T(8,128)(2,1)S(1)} custom-call(bf16[128,512]{1,0:T(8,128)(2,1)S(1)} %get-tuple-element.19.refs_0_, bf16[128,512]{1,0:T(8,128)(2,1)S(1)} %collective-permute-done.9.refs_1_, bf16[128,512]{1,0:T(8,128)(2,1)S(1)} %collective-permute-done.10.refs_2_, bf16[128,512]{1,0:T(8,128)(2,1)S(1)} %collective-permute-done.11.refs_3_, ...), custom_call_target="tpu_custom_call" | custom-call | tf_op jit(solution)/shard_map/pallas_call | solution.py:148
  98.5 3.2 %collective-permute-done.15 = bf16[64,2048]{1,0:T(8,128)(2,1)S(1)} collective-permute-done((bf16[64,2048]{1,0:T(8,128)(2,1)S(1)}, bf16[64,2048]{1,0:T(8,128)(2,1)S(1)}, u32[]{:S(2)}, u32[]{:S(2)}) %collective-permute-start.15) | collective-permute-done | bytes 262176 | tf_op jit(solution)/shard_map/ppermute | solution.py:28
  101.8 0.8 add_convert_fusion
Async XLA Ops:
  0.0 33.3 %collective-permute-start.6 = (bf16[512,2048]{1,0:T(8,128)(2,1)}, bf16[512,2048]{1,0:T(8,128)(2,1)S(1)}, u32[]{:S(2)}, u32[]{:S(2)}) collective-permute-start(bf16[512,2048]{1,0:T(8,128)(2,1)} %refs_4_.11), channel_id=1, source_target_pairs={{0,1},{1,2},{2,3},{3,0},{8,11},{9,8},{10,9},{11,10},{4,5},{5,6},{6... | collective-permute-start | bytes 6291464 | tf_op jit(solution)/shard_map/ppermute | solution.py:35
  3.3 7.8 %collective-permute-start = (bf16[1024,512]{1,0:T(8,128)(2,1)}, bf16[1024,512]{1,0:T(8,128)(2,1)S(1)}, u32[]{:S(2)}, u32[]{:S(2)}) collective-permute-start(bf16[1024,512]{1,0:T(8,128)(2,1)} %refs_5_.3), channel_id=1, source_target_pairs={{0,8},{8,0},{1,9},{9,1},{2,10},{10,2},{3,11},{11,3},{4,12},{12,4},... | collective-permute-start | bytes 3145736 | tf_op jit(solution)/shard_map/ppermute | solution.py:28
  3.3 9.5 %collective-permute-start.1 = (bf16[1024,512]{1,0:T(8,128)(2,1)}, bf16[1024,512]{1,0:T(8,128)(2,1)S(1)}, u32[]{:S(2)}, u32[]{:S(2)}) collective-permute-start(bf16[1024,512]{1,0:T(8,128)(2,1)} %refs_6_.3), channel_id=1, source_target_pairs={{0,8},{8,0},{1,9},{9,1},{2,10},{10,2},{3,11},{11,3},{4,12},{12,4},... | collective-permute-start | bytes 3145736 | tf_op jit(solution)/shard_map/ppermute | solution.py:28
  3.8 22.0 %collective-permute-start.5 = (bf16[512,512]{1,0:T(8,128)(2,1)}, bf16[512,512]{1,0:T(8,128)(2,1)S(1)}, u32[]{:S(2)}, u32[]{:S(2)}) collective-permute-start(bf16[512,512]{1,0:T(8,128)(2,1)} %refs_2_.2), channel_id=1, source_target_pairs={{0,224},{8,232},{16,240},{24,248},{32,0},{40,8},{48,16},{56,24},{6... | collective-permute-start | bytes 1572872 | tf_op jit(solution)/shard_map/ppermute | solution.py:24
  9.4 23.9 %collective-permute-start.3 = (bf16[512,512]{1,0:T(8,128)(2,1)}, bf16[512,512]{1,0:T(8,128)(2,1)S(1)}, u32[]{:S(2)}, u32[]{:S(2)}) collective-permute-start(bf16[512,512]{1,0:T(8,128)(2,1)} %refs_2_.2), channel_id=1, source_target_pairs={{0,240},{8,248},{16,0},{24,8},{32,16},{40,24},{48,32},{56,40},{64,... | collective-permute-start | bytes 1572872 | tf_op jit(solution)/shard_map/ppermute | solution.py:24
  11.1 22.2 %collective-permute-start.2 = (s32[1,4]{1,0:T(1,128)}, s32[1,4]{1,0:T(1,128)S(1)}, u32[]{:S(2)}, u32[]{:S(2)}) collective-permute-start(s32[1,4]{1,0:T(1,128)} %refs_0_.3), channel_id=1, source_target_pairs={{0,240},{8,248},{16,0},{24,8},{32,16},{40,24},{48,32},{56,40},{64,... | collective-permute-start | bytes 56 | tf_op jit(solution)/shard_map/ppermute | solution.py:24
  12.8 19.5 %collective-permute-start.4 = (s32[1,4]{1,0:T(1,128)}, s32[1,4]{1,0:T(1,128)S(1)}, u32[]{:S(2)}, u32[]{:S(2)}) collective-permute-start(s32[1,4]{1,0:T(1,128)} %refs_0_.3), channel_id=1, source_target_pairs={{0,224},{8,232},{16,240},{24,248},{32,0},{40,8},{48,16},{56,24},{6... | collective-permute-start | bytes 56 | tf_op jit(solution)/shard_map/ppermute | solution.py:24
  13.5 1.2 %copy-start = (bf16[1024,512]{1,0:T(8,128)(2,1)S(1)}, bf16[1024,512]{1,0:T(8,128)(2,1)}, u32[]{:S(2)}) copy-start(bf16[1024,512]{1,0:T(8,128)(2,1)} %refs_5_.3) | copy-start | bytes 3145732
  14.7 1.2 %copy-start.2 = (bf16[1024,512]{1,0:T(8,128)(2,1)S(1)}, bf16[1024,512]{1,0:T(8,128)(2,1)}, u32[]{:S(2)}) copy-start(bf16[1024,512]{1,0:T(8,128)(2,1)} %refs_6_.3) | copy-start | bytes 3145732
  15.9 1.0 %copy-start.5 = (bf16[512,512]{1,0:T(8,128)(2,1)S(1)}, bf16[512,512]{1,0:T(8,128)(2,1)}, u32[]{:S(2)}) copy-start(bf16[512,512]{1,0:T(8,128)(2,1)} %refs_2_.2) | copy-start | bytes 1572868
  17.0 1.0 %copy-start.6 = (bf16[512,512]{1,0:T(8,128)(2,1)S(1)}, bf16[512,512]{1,0:T(8,128)(2,1)}, u32[]{:S(2)}) copy-start(bf16[512,512]{1,0:T(8,128)(2,1)} %refs_3_.7) | copy-start | bytes 1572868
  18.0 1.0 %copy-start.7 = (bf16[512,512]{1,0:T(8,128)(2,1)S(1)}, bf16[512,512]{1,0:T(8,128)(2,1)}, u32[]{:S(2)}) copy-start(bf16[512,512]{1,0:T(8,128)(2,1)} %refs_4_.9) | copy-start | bytes 1572868
  19.1 0.7 copy-start.8
  19.7 0.7 copy-start.9
  20.4 11.8 %copy-start.1 = (bf16[1024,512]{1,0:T(8,128)(2,1)S(1)}, bf16[1024,512]{1,0:T(8,128)(2,1)}, u32[]{:S(2)}) copy-start(bf16[1024,512]{1,0:T(8,128)(2,1)} %refs_5_.3) | copy-start | bytes 3145732
  20.4 11.8 %copy-start.3 = (bf16[1024,512]{1,0:T(8,128)(2,1)S(1)}, bf16[1024,512]{1,0:T(8,128)(2,1)}, u32[]{:S(2)}) copy-start(bf16[1024,512]{1,0:T(8,128)(2,1)} %refs_6_.3) | copy-start | bytes 3145732
  41.2 14.0 %collective-permute-start.13 = (bf16[256,2048]{1,0:T(8,128)(2,1)S(1)}, bf16[256,2048]{1,0:T(8,128)(2,1)S(1)}, u32[]{:S(2)}, u32[]{:S(2)}) collective-permute-start(bf16[256,2048]{1,0:T(8,128)(2,1)S(1)} %get-tuple-element.24), channel_id=1, source_target_pairs={{0,1},{1,2},{2,3},{3,0},{8,11},{9,8},{10,9},{11,10},{4,5},{5,6},{6... | collective-permute-start | bytes 3145736 | tf_op jit(solution)/shard_map/ppermute | solution.py:35
  41.4 50.9 %collective-permute-start.12 = (bf16[512,2048]{1,0:T(8,128)(2,1)S(1)}, bf16[512,2048]{1,0:T(8,128)(2,1)S(1)}, u32[]{:S(2)}, u32[]{:S(2)}) collective-permute-start(bf16[512,2048]{1,0:T(8,128)(2,1)S(1)} %collective-permute-done.6.refs_7_.refs_5_), channel_id=1, source_target_pairs={{0,8},{8,0},{1,9},{9,1},{2,10},{10,2},{3,11},{11,3},{4,12},{12,4},... | collective-permute-start | bytes 6291464 | tf_op jit(solution)/shard_map/ppermute | solution.py:28
  55.2 37.1 %collective-permute-start.14 = (bf16[256,2048]{1,0:T(8,128)(2,1)S(1)}, bf16[256,2048]{1,0:T(8,128)(2,1)S(1)}, u32[]{:S(2)}, u32[]{:S(2)}) collective-permute-start(bf16[256,2048]{1,0:T(8,128)(2,1)S(1)} %collective-permute-done.13.refs_7_), channel_id=1, source_target_pairs={{0,8},{8,0},{1,9},{9,1},{2,10},{10,2},{3,11},{11,3},{4,12},{12,4},... | collective-permute-start | bytes 3145736 | tf_op jit(solution)/shard_map/ppermute | solution.py:28
  64.8 15.0 %collective-permute-start.7 = (bf16[528,512]{1,0:T(8,128)(2,1)S(1)}, bf16[528,512]{1,0:T(8,128)(2,1)S(1)}, u32[]{:S(2)}, u32[]{:S(2)}) collective-permute-start(bf16[528,512]{1,0:T(8,128)(2,1)S(1)} %shard_map.83), channel_id=1, source_target_pairs={{0,32},{8,40},{16,48},{24,56},{32,64},{40,72},{48,80},{56,88},{64,... | collective-permute-start | bytes 1622024 | tf_op jit(solution)/shard_map/ppermute | solution.py:24
  64.8 17.5 %collective-permute-start.8 = (bf16[528,512]{1,0:T(8,128)(2,1)S(1)}, bf16[528,512]{1,0:T(8,128)(2,1)S(1)}, u32[]{:S(2)}, u32[]{:S(2)}) collective-permute-start(bf16[528,512]{1,0:T(8,128)(2,1)S(1)} %get-tuple-element.17), channel_id=1, source_target_pairs={{0,16},{8,24},{16,32},{24,40},{32,48},{40,56},{48,64},{56,72},{64,... | collective-permute-start | bytes 1622024 | tf_op jit(solution)/shard_map/ppermute | solution.py:24
  64.8 27.6 %copy-start.4 = (bf16[512,2048]{1,0:T(8,128)(2,1)S(1)}, bf16[512,2048]{1,0:T(8,128)(2,1)}, u32[]{:S(2)}) copy-start(bf16[512,2048]{1,0:T(8,128)(2,1)} %refs_4_.11) | copy-start | bytes 6291460
  83.4 8.8 %collective-permute-start.9 = (bf16[128,512]{1,0:T(8,128)(2,1)S(1)}, bf16[128,512]{1,0:T(8,128)(2,1)S(1)}, u32[]{:S(2)}, u32[]{:S(2)}) collective-permute-start(bf16[128,512]{1,0:T(8,128)(2,1)S(1)} %get-tuple-element.20), channel_id=1, source_target_pairs={{0,1},{1,2},{2,3},{3,0},{4,5},{5,6},{6,7},{7,4},{8,9},{9,10},{10,1... | collective-permute-start | bytes 393224 | tf_op jit(solution)/shard_map/ppermute | solution.py:24
  83.5 8.7 %collective-permute-start.10 = (bf16[128,512]{1,0:T(8,128)(2,1)S(1)}, bf16[128,512]{1,0:T(8,128)(2,1)S(1)}, u32[]{:S(2)}, u32[]{:S(2)}) collective-permute-start(bf16[128,512]{1,0:T(8,128)(2,1)S(1)} %get-tuple-element.21), channel_id=1, source_target_pairs={{0,2},{1,3},{2,0},{3,1},{4,6},{5,7},{6,4},{7,5},{8,10},{9,11},{10,... | collective-permute-start | bytes 393224 | tf_op jit(solution)/shard_map/ppermute | solution.py:24
  84.2 8.1 %collective-permute-start.11 = (bf16[128,512]{1,0:T(8,128)(2,1)S(1)}, bf16[128,512]{1,0:T(8,128)(2,1)S(1)}, u32[]{:S(2)}, u32[]{:S(2)}) collective-permute-start(bf16[128,512]{1,0:T(8,128)(2,1)S(1)} %get-tuple-element.22), channel_id=1, source_target_pairs={{0,3},{1,0},{2,1},{3,2},{4,7},{5,4},{6,5},{7,6},{8,11},{9,8},{10,9... | collective-permute-start | bytes 393224 | tf_op jit(solution)/shard_map/ppermute | solution.py:24
  94.0 7.8 %collective-permute-start.15 = (bf16[64,2048]{1,0:T(8,128)(2,1)S(1)}, bf16[64,2048]{1,0:T(8,128)(2,1)S(1)}, u32[]{:S(2)}, u32[]{:S(2)}) collective-permute-start(bf16[64,2048]{1,0:T(8,128)(2,1)S(1)} %shard_map.88), channel_id=1, source_target_pairs={{0,4},{4,0},{1,5},{5,1},{2,6},{6,2},{3,7},{7,3},{8,12},{12,8},{9,1... | collective-permute-start | bytes 786440 | tf_op jit(solution)/shard_map/ppermute | solution.py:28

commit v4 on v3

--- a/solution.py
+++ b/solution.py
@@ -121,7 +121,7 @@
 
 
 def guest_kernel(offsets, lengths, q_ref, k0, v0, k1, v1, *refs, back):
-    *extra, m_ref, acc_ref, level_ref = refs
+    out_ref, m_ref, acc_ref, level_ref = refs
     core, document = lax.axis_index("core"), lax.axis_index(DOC)
     reset(m_ref, acc_ref)
     counts = [
@@ -130,12 +130,6 @@
     ]
     live = lengths[document], lengths[document + 1 - 2 * core]
     absorb_memories(((k0, v0), (k1, v1)), live, counts, lambda h: q_ref[:, of_head(h)], m_ref, acc_ref)
-    if len(extra) == 3:
-        weights, out_ref, half_ref = extra
-        half = half_ref.shape[0]
-        half_ref[...] = weights[pl.ds(pl.multiple_of(core * half, half), half), :]
-    else:
-        (out_ref,) = extra
     finish(out_ref, level_ref, m_ref, acc_ref)
 
 
@@ -159,14 +153,46 @@
     )(*scalars, *arrays)
 
 
-def attention(kernel, scalars, arrays, rows, width, extra=()):
+def attention(kernel, scalars, arrays, rows, width):
     heads = width // DH
     scratch = [
         pltpu.VMEM((heads, rows, DH), jnp.float32),
         pltpu.VMEM((heads, rows, 2 * DH), jnp.float32),
         pltpu.VMEM((TAIL, width), jnp.float32),
     ]
-    return kernel_call(kernel, scalars, arrays, [(rows + TAIL, width), *extra], scratch)
+    return kernel_call(kernel, scalars, arrays, [(rows + TAIL, width)], scratch)[0]
+
+
+def load_kernel(*refs):
+    *pairs, sems = refs
+    count = len(pairs) // 2
+    copies = [pltpu.make_async_copy(pairs[i], pairs[count + i], sems.at[i]) for i in range(count)]
+    for copy in copies:
+        copy.start()
+    for copy in copies:
+        copy.wait()
+
+
+def load(*arrays):
+    return pl.pallas_call(
+        load_kernel,
+        in_specs=[pl.BlockSpec(memory_space=pltpu.HBM)] * len(arrays),
+        out_specs=[pl.BlockSpec(memory_space=pltpu.VMEM)] * len(arrays),
+        out_shape=[pltpu.VMEM(a.shape, a.dtype) for a in arrays],
+        scratch_shapes=[pltpu.SemaphoreType.DMA((len(arrays),))],
+        compiler_params=pltpu.CompilerParams(vmem_limit_bytes=VMEM_LIMIT),
+        name="load",
+    )(*(pltpu.with_memory_space_constraint(a, pltpu.HBM) for a in arrays))
+
+
+def pass_on_kernel(weights, half_ref):
+    half = half_ref.shape[0]
+    half_ref[...] = weights[pl.ds(pl.multiple_of(lax.axis_index("core") * half, half), half), :]
+
+
+def pass_on(weights):
+    depth, width = weights.shape
+    return kernel_call(pass_on_kernel, (), (weights,), [(depth // 2, width)], [])[0]
 
 
 def merge_kernel(*refs):
@@ -253,37 +279,32 @@
     offsets_near = moved(shift, offsets, DOC, -2)
     other_keys = moved(swap, mem_keys, "core")
     other_values = moved(swap, mem_values, "core")
-    memory = (on_chip(mem_keys), on_chip(mem_values), other_keys, other_values)
-    local = (on_chip(queries), on_chip(local_keys), on_chip(local_values))
     near_weight = moved(part_ways, out_weight)
+    own_keys, own_values, own_weight, *local = load(mem_keys, mem_values, out_weight, queries, local_keys, local_values)
+    memory = (own_keys, own_values, other_keys, other_values)
 
     def at_home(local, half):
         def kernel(*refs):
             home_kernel(*refs, half=half)
 
-        return attention(kernel, (offsets, mem_lengths), (*local, *memory), rows // 2, width)[0]
-
-    def guest(load, table, back, *weights):
+        return attention(kernel, (offsets, mem_lengths), (*local, *memory), rows // 2, width)
+
+    def guest(load, table, back):
         def kernel(*refs):
             guest_kernel(*refs, back=back)
 
-        extra = [(w.shape[0] // 2, w.shape[1]) for w in weights]
-        out, *rest = attention(kernel, (table, mem_lengths), (load, *memory, *weights), rows, width, extra)
-        return moved(shift, out, DOC, back), out, *rest
+        out = attention(kernel, (table, mem_lengths), (load, *memory), rows, width)
+        return moved(shift, out, DOC, back), out
 
     home0 = at_home(local, 0)
-    from_far, far, *_ = guest(after(query_far, home0), offsets_far, 4)
-    from_near, near, passed_on = guest(after(query_near, far), offsets_near, 2, near_weight)
-    home1 = at_home((after(local[0], near), *local[1:]), 1)
-
+    from_far, far = guest(after(query_far, home0), offsets_far, 4)
+    from_near, near = guest(after(query_near, far), offsets_near, 2)
+
+    near_weight = after(near_weight, near)
+    passed_on = pass_on(near_weight)
+    home1 = at_home((after(local[0], near, passed_on), *local[1:]), 1)
     far_weight = moved(part_ways, passed_on)
-    weights = [
-        on_chip(out_weight),
-        near_weight,
-        moved(swap, after(near_weight, near), "core"),
-        far_weight,
-        moved(swap, far_weight, "core"),
-    ]
+    weights = [own_weight, near_weight, moved(swap, near_weight, "core"), far_weight, moved(swap, far_weight, "core")]
 
     mine, *tiles = merge(home0, home1, from_far, from_near)
     tiles = mine, *(moved(shift, tile, "x", k) for k, tile in enumerate(tiles, 1))

time: 104 us -> 104 us (level)
  waiting for transfers between devices: 33.3 us -> 46.4 us
  starting transfers between devices: 37 us -> 28.2 us
  local copies, waits for them, and re-layouts: 6.89 us -> 0.01 us
  Pallas kernels: 24.5 us -> 27.2 us
    ppermute x5, starting transfers between devices: 21 us -> 13.2 us  [swap(): return lax.ppermute(value, axis, [(0, 1), (1, 0)])]
    ppermute x2, waiting for transfers between devices: 5.8 us -> 13.3 us  [part_ways(): return lax.ppermute(value, ('core', 'x'), up + down)]
    unnamed x20 -> x4, local copies, waits for them, and re-layouts: 6.89 us -> 0.01 us
    ppermute x9, waiting for transfers between devices: 24.2 us -> 29.8 us  [shift(): lax.ppermute(value, axis, [(i, (i + steps) % count) for i in range(count)])]
    pallas_call x0 -> x1, Pallas kernels: none -> 2.67 us  [load(): pl.pallas_call(load_kernel, in_specs=[pl.BlockSpec(memory_space=pltpu.HBM...]
    ppermute x9, starting transfers between devices: 12.4 us -> 11 us  [shift(): lax.ppermute(value, axis, [(i, (i + steps) % count) for i in range(count)])]
    pallas_call x7 -> x8, Pallas kernels: 24.5 us -> 24.5 us  [kernel_call(): pl.pallas_call(kernel, grid_spec=pltpu.PrefetchScalarGridSpec(num_scalar_...]
  transfers between devices with their start and end apart: 16 -> 16, of which waited for: 7 -> 8; matrix products, arithmetic and copies ran while one was open for 0% -> 0% of each run, Pallas kernels for 15% -> 25%
where the time goes in v4:
time: 104 us; the launch traced here: 103 us
  waiting for transfers between devices  46.4 us (45%)
  starting transfers between devices  28.2 us (27%)
  Pallas kernels  27.2 us (26%)
    ppermute x9, waiting for transfers between devices, shift(): lax.ppermute(value, axis, [(i, (i + steps) % count) for i in range(count)])  29.8 us
    pallas_call x8, Pallas kernels, kernel_call(): pl.pallas_call(kernel, grid_spec=pltpu.PrefetchScalarGridSpec(num_scalar_...  24.5 us
    ppermute x2, waiting for transfers between devices, part_ways(): return lax.ppermute(value, ('core', 'x'), up + down)  13.3 us
    ppermute x5, starting transfers between devices, swap(): return lax.ppermute(value, axis, [(0, 1), (1, 0)])  13.2 us
    ppermute x9, starting transfers between devices, shift(): lax.ppermute(value, axis, [(i, (i + steps) % count) for i in range(count)])  11 us
    ppermute x2, starting transfers between devices, part_ways(): return lax.ppermute(value, ('core', 'x'), up + down)  3.95 us
    ppermute x5, waiting for transfers between devices, swap(): return lax.ppermute(value, axis, [(0, 1), (1, 0)])  3.22 us
    pallas_call x1, Pallas kernels, load(): pl.pallas_call(load_kernel, in_specs=[pl.BlockSpec(memory_space=pltpu.HBM...  2.67 us
  transfers between devices with their start and end apart: 16, of which 8 were waited for; matrix products, arithmetic and copies ran while one was open for 0% of the time, Pallas kernels for 25%

profile of v4, /device:TPU:1, one launch (start us, length us, event | category | flops | bytes accessed | tf_op | source)
XLA Modules:
  0.0 102.7 jit_solution(4413019530440290751)
XLA Ops:
  0.0 0.0 copy-start.1
  0.0 0.0 copy-start
  0.0 3.3 %collective-permute-start.6 = (bf16[512,2048]{1,0:T(8,128)(2,1)}, bf16[512,2048]{1,0:T(8,128)(2,1)S(1)}, u32[]{:S(2)}, u32[]{:S(2)}) collective-permute-start(bf16[512,2048]{1,0:T(8,128)(2,1)} %refs_2_.1), channel_id=1, source_target_pairs={{0,1},{1,2},{2,3},{3,0},{8,11},{9,8},{10,9},{11,10},{4,5},{5,6},{6... | collective-permute-start | bytes 6291464 | tf_op jit(solution)/shard_map/ppermute | solution.py:35
  3.3 0.0 collective-permute-start
  3.3 0.5 collective-permute-start.1
  3.8 5.6 %collective-permute-start.5 = (bf16[512,512]{1,0:T(8,128)(2,1)}, bf16[512,512]{1,0:T(8,128)(2,1)S(1)}, u32[]{:S(2)}, u32[]{:S(2)}) collective-permute-start(bf16[512,512]{1,0:T(8,128)(2,1)} %refs_3_.1), channel_id=1, source_target_pairs={{0,224},{8,232},{16,240},{24,248},{32,0},{40,8},{48,16},{56,24},{6... | collective-permute-start | bytes 1572872 | tf_op jit(solution)/shard_map/ppermute | solution.py:24
  9.4 1.7 %collective-permute-start.3 = (bf16[512,512]{1,0:T(8,128)(2,1)}, bf16[512,512]{1,0:T(8,128)(2,1)S(1)}, u32[]{:S(2)}, u32[]{:S(2)}) collective-permute-start(bf16[512,512]{1,0:T(8,128)(2,1)} %refs_3_.1), channel_id=1, source_target_pairs={{0,240},{8,248},{16,0},{24,8},{32,16},{40,24},{48,32},{56,40},{64,... | collective-permute-start | bytes 1572872 | tf_op jit(solution)/shard_map/ppermute | solution.py:24
  11.1 2.7 %load.1 = (bf16[1024,512]{1,0:T(8,128)(2,1)S(1)}, bf16[1024,512]{1,0:T(8,128)(2,1)S(1)}, bf16[512,2048]{1,0:T(8,128)(2,1)S(1)}, bf16[512,512]{1,0:T(8,128)(2,1)S...) custom-call(bf16[1024,512]{1,0:T(8,128)(2,1)} %refs_0_.3, bf16[1024,512]{1,0:T(8,128)(2,1)} %refs_1_.5, ...), custom_call_target="tpu_custom_call" | custom-call | tf_op jit(solution)/shard_map/load/pallas_call | solution.py:177
  13.8 0.0 collective-permute-done.refs_7_.refs_5_
  13.8 0.0 copy-done.1
  13.8 0.2 collective-permute-start.2
  14.1 0.0 collective-permute-done.1.refs_8_.refs_6_
  14.1 0.7 collective-permute-start.4
  14.8 0.0 copy-done
  14.8 5.4 %shard_map.82.refs_0_ = bf16[272,512]{1,0:T(8,128)(2,1)S(1)} custom-call(s32[1,4]{1,0:T(1,128)S(1)} %copy-done.1, s32[32]{0:T(128)S(1)} %copy-done, bf16[512,512]{1,0:T(8,128)(2,1)S(1)} %get-tuple-element.27.refs_2_, bf16[512,512]{1,0:T(8,128)(2,1)S(1)} %get-tuple-element.20.refs_3_, bf16[512,512]{1,0:T(8,128)(2,1)S(1)} %get-tuple-element.21.refs_4_, ...), custom_call_target="tpu_custom_call" | custom-call | tf_op jit(solution)/shard_map/pallas_call | solution.py:142
  20.3 0.7 collective-permute-done.5.refs_2_
  21.0 11.2 %collective-permute-done.4.refs_0_ = s32[1,4]{1,0:T(1,128)S(1)} collective-permute-done((s32[1,4]{1,0:T(1,128)S(1)}, s32[1,4]{1,0:T(1,128)S(1)}, u32[]{:S(2)}, u32[]{:S(2)}) %collective-permute-start.4) | collective-permute-done | bytes 48 | tf_op jit(solution)/shard_map/ppermute | solution.py:24
  32.2 1.1 %shard_map.83 = bf16[528,512]{1,0:T(8,128)(2,1)S(1)} custom-call(s32[1,4]{1,0:T(1,128)S(1)} %collective-permute-done.4.refs_0_, s32[32]{0:T(128)S(1)} %copy-done, bf16[512,512]{1,0:T(8,128)(2,1)S(1)} %collective-permute-done.5.refs_2_, bf16[1024,512]{1,0:T(8,128)(2,1)S(1)} %get-tuple-element.22.refs_5_.refs_3_, ...), custom_call_target="tpu_custom_call" | custom-call | tf_op jit(solution)/shard_map/pallas_call | solution.py:142
  33.3 0.0 collective-permute-done.3.refs_2_
  33.3 0.0 collective-permute-done.2.refs_0_
  33.3 7.9 %shard_map.84 = bf16[528,512]{1,0:T(8,128)(2,1)S(1)} custom-call(s32[1,4]{1,0:T(1,128)S(1)} %collective-permute-done.2.refs_0_, s32[32]{0:T(128)S(1)} %copy-done, bf16[512,512]{1,0:T(8,128)(2,1)S(1)} %collective-permute-done.3.refs_2_, bf16[1024,512]{1,0:T(8,128)(2,1)S(1)} %get-tuple-element.22.refs_5_.refs_3_, ...), custom_call_target="tpu_custom_call" | custom-call | tf_op jit(solution)/shard_map/pallas_call | solution.py:142
  41.2 0.0 collective-permute-done.6.weights.refs_5_
  41.2 0.1 shard_map.85
  41.3 7.6 %collective-permute-start.12 = (bf16[512,2048]{1,0:T(8,128)(2,1)S(1)}, bf16[512,2048]{1,0:T(8,128)(2,1)S(1)}, u32[]{:S(2)}, u32[]{:S(2)}) collective-permute-start(bf16[512,2048]{1,0:T(8,128)(2,1)S(1)} %collective-permute-done.6.weights.refs_5_), channel_id=1, source_target_pairs={{0,8},{8,0},{1,9},{9,1},{2,10},{10,2},{3,11},{11,3},{4,12},{12,4},... | collective-permute-start | bytes 6291464 | tf_op jit(solution)/shard_map/ppermute | solution.py:28
  48.8 0.7 collective-permute-start.13
  49.5 13.3 %collective-permute-done.13.refs_7_ = bf16[256,2048]{1,0:T(8,128)(2,1)S(1)} collective-permute-done((bf16[256,2048]{1,0:T(8,128)(2,1)S(1)}, bf16[256,2048]{1,0:T(8,128)(2,1)S(1)}, u32[]{:S(2)}, u32[]{:S(2)}) %collective-permute-start.13) | collective-permute-done | bytes 1048608 | tf_op jit(solution)/shard_map/ppermute | solution.py:35
  62.8 2.2 %collective-permute-start.14 = (bf16[256,2048]{1,0:T(8,128)(2,1)S(1)}, bf16[256,2048]{1,0:T(8,128)(2,1)S(1)}, u32[]{:S(2)}, u32[]{:S(2)}) collective-permute-start(bf16[256,2048]{1,0:T(8,128)(2,1)S(1)} %collective-permute-done.13.refs_7_), channel_id=1, source_target_pairs={{0,8},{8,0},{1,9},{9,1},{2,10},{10,2},{3,11},{11,3},{4,12},{12,4},... | collective-permute-start | bytes 3145736 | tf_op jit(solution)/shard_map/ppermute | solution.py:28
  64.9 0.0 collective-permute-start.7
  65.0 0.0 collective-permute-start.8
  65.0 5.8 %shard_map.86.refs_1_ = bf16[272,512]{1,0:T(8,128)(2,1)S(1)} custom-call(s32[1,4]{1,0:T(1,128)S(1)} %copy-done.1, s32[32]{0:T(128)S(1)} %copy-done, bf16[512,512]{1,0:T(8,128)(2,1)S(1)} %get-tuple-element.27.refs_2_, bf16[512,512]{1,0:T(8,128)(2,1)S(1)} %get-tuple-element.20.refs_3_, bf16[512,512]{1,0:T(8,128)(2,1)S(1)} %get-tuple-element.21.refs_4_, ...), custom_call_target="tpu_custom_call" | custom-call | tf_op jit(solution)/shard_map/pallas_call | solution.py:142
  70.8 9.2 %collective-permute-done.7.refs_2_ = bf16[528,512]{1,0:T(8,128)(2,1)S(1)} collective-permute-done((bf16[528,512]{1,0:T(8,128)(2,1)S(1)}, bf16[528,512]{1,0:T(8,128)(2,1)S(1)}, u32[]{:S(2)}, u32[]{:S(2)}) %collective-permute-start.7) | collective-permute-done | bytes 540704 | tf_op jit(solution)/shard_map/ppermute | solution.py:24
  80.0 2.5 %collective-permute-done.8.refs_3_ = bf16[528,512]{1,0:T(8,128)(2,1)S(1)} collective-permute-done((bf16[528,512]{1,0:T(8,128)(2,1)S(1)}, bf16[528,512]{1,0:T(8,128)(2,1)S(1)}, u32[]{:S(2)}, u32[]{:S(2)}) %collective-permute-start.8) | collective-permute-done | bytes 540704 | tf_op jit(solution)/shard_map/ppermute | solution.py:24
  82.5 1.1 %shard_map.87 = (bf16[128,512]{1,0:T(8,128)(2,1)S(1)}, bf16[128,512]{1,0:T(8,128)(2,1)S(1)}, bf16[128,512]{1,0:T(8,128)(2,1)S(1)}, bf16[128,512]{1,0:T(8,128)(2,1)S(1)}) custom-call(bf16[272,512]{1,0:T(8,128)(2,1)S(1)} %shard_map.82.refs_0_, bf16[272,512]{1,0:T(8,128)(2,1)S(1)} %shard_map.86.refs_1_, bf16[528,512]{1,0:T(8,128)(2,1)S(1)} %collective-permute-done.7.refs_2_, ...), custom_call_target="tpu_custom_call" | custom-call | tf_op jit(solution)/shard_map/pallas_call | solution.py:142
  83.6 0.1 collective-permute-start.9
  83.7 0.7 collective-permute-start.10
  84.4 1.9 %collective-permute-start.11 = (bf16[128,512]{1,0:T(8,128)(2,1)S(1)}, bf16[128,512]{1,0:T(8,128)(2,1)S(1)}, u32[]{:S(2)}, u32[]{:S(2)}) collective-permute-start(bf16[128,512]{1,0:T(8,128)(2,1)S(1)} %get-tuple-element.31), channel_id=1, source_target_pairs={{0,3},{1,0},{2,1},{3,2},{4,7},{5,4},{6,5},{7,6},{8,11},{9,8},{10,9... | collective-permute-start | bytes 393224 | tf_op jit(solution)/shard_map/ppermute | solution.py:24
  86.3 6.1 %collective-permute-done.9.refs_1_ = bf16[128,512]{1,0:T(8,128)(2,1)S(1)} collective-permute-done((bf16[128,512]{1,0:T(8,128)(2,1)S(1)}, bf16[128,512]{1,0:T(8,128)(2,1)S(1)}, u32[]{:S(2)}, u32[]{:S(2)}) %collective-permute-start.9) | collective-permute-done | bytes 131104 | tf_op jit(solution)/shard_map/ppermute | solution.py:24
  92.5 0.0 collective-permute-done.10.refs_2_
  92.5 0.1 collective-permute-done.11.refs_3_
  92.5 0.0 collective-permute-done.12.refs_6_
  92.5 0.0 collective-permute-done.14.refs_8_
  92.6 1.6 %shard_map.89 = bf16[64,2048]{1,0:T(8,128)(2,1)S(1)} custom-call(bf16[128,512]{1,0:T(8,128)(2,1)S(1)} %get-tuple-element.28.refs_0_, bf16[128,512]{1,0:T(8,128)(2,1)S(1)} %collective-permute-done.9.refs_1_, bf16[128,512]{1,0:T(8,128)(2,1)S(1)} %collective-permute-done.10.refs_2_, bf16[128,512]{1,0:T(8,128)(2,1)S(1)} %collective-permute-done.11.refs_3_, ...), custom_call_target="tpu_custom_call" | custom-call | tf_op jit(solution)/shard_map/pallas_call | solution.py:142
  94.1 3.0 %collective-permute-start.15 = (bf16[64,2048]{1,0:T(8,128)(2,1)S(1)}, bf16[64,2048]{1,0:T(8,128)(2,1)S(1)}, u32[]{:S(2)}, u32[]{:S(2)}) collective-permute-start(bf16[64,2048]{1,0:T(8,128)(2,1)S(1)} %shard_map.89), channel_id=1, source_target_pairs={{0,4},{4,0},{1,5},{5,1},{2,6},{6,2},{3,7},{7,3},{8,12},{12,8},{9,1... | collective-permute-start | bytes 786440 | tf_op jit(solution)/shard_map/ppermute | solution.py:28
  97.1 1.6 %shard_map.88 = bf16[64,2048]{1,0:T(8,128)(2,1)S(1)} custom-call(bf16[128,512]{1,0:T(8,128)(2,1)S(1)} %get-tuple-element.28.refs_0_, bf16[128,512]{1,0:T(8,128)(2,1)S(1)} %collective-permute-done.9.refs_1_, bf16[128,512]{1,0:T(8,128)(2,1)S(1)} %collective-permute-done.10.refs_2_, bf16[128,512]{1,0:T(8,128)(2,1)S(1)} %collective-permute-done.11.refs_3_, ...), custom_call_target="tpu_custom_call" | custom-call | tf_op jit(solution)/shard_map/pallas_call | solution.py:142
  98.7 3.2 %collective-permute-done.15 = bf16[64,2048]{1,0:T(8,128)(2,1)S(1)} collective-permute-done((bf16[64,2048]{1,0:T(8,128)(2,1)S(1)}, bf16[64,2048]{1,0:T(8,128)(2,1)S(1)}, u32[]{:S(2)}, u32[]{:S(2)}) %collective-permute-start.15) | collective-permute-done | bytes 262176 | tf_op jit(solution)/shard_map/ppermute | solution.py:28
  101.9 0.8 add_convert_fusion
Async XLA Ops:
  0.0 13.8 %copy-start.1 = (s32[1,4]{1,0:T(1,128)S(1)}, s32[1,4]{1,0:T(1,128)}, u32[]{:S(2)}) copy-start(s32[1,4]{1,0:T(1,128)} %refs_0_.5) | copy-start | bytes 52
  0.0 14.8 %copy-start = (s32[32]{0:T(128)S(1)}, s32[32]{0:T(128)}, u32[]{:S(2)}) copy-start(s32[32]{0:T(128)} %refs_1_.9) | copy-start | bytes 388
  0.0 41.2 %collective-permute-start.6 = (bf16[512,2048]{1,0:T(8,128)(2,1)}, bf16[512,2048]{1,0:T(8,128)(2,1)S(1)}, u32[]{:S(2)}, u32[]{:S(2)}) collective-permute-start(bf16[512,2048]{1,0:T(8,128)(2,1)} %refs_2_.1), channel_id=1, source_target_pairs={{0,1},{1,2},{2,3},{3,0},{8,11},{9,8},{10,9},{11,10},{4,5},{5,6},{6... | collective-permute-start | bytes 6291464 | tf_op jit(solution)/shard_map/ppermute | solution.py:35
  3.3 10.5 %collective-permute-start = (bf16[1024,512]{1,0:T(8,128)(2,1)}, bf16[1024,512]{1,0:T(8,128)(2,1)S(1)}, u32[]{:S(2)}, u32[]{:S(2)}) collective-permute-start(bf16[1024,512]{1,0:T(8,128)(2,1)} %refs_0_.3), channel_id=1, source_target_pairs={{0,8},{8,0},{1,9},{9,1},{2,10},{10,2},{3,11},{11,3},{4,12},{12,4},... | collective-permute-start | bytes 3145736 | tf_op jit(solution)/shard_map/ppermute | solution.py:28
  3.3 10.8 %collective-permute-start.1 = (bf16[1024,512]{1,0:T(8,128)(2,1)}, bf16[1024,512]{1,0:T(8,128)(2,1)S(1)}, u32[]{:S(2)}, u32[]{:S(2)}) collective-permute-start(bf16[1024,512]{1,0:T(8,128)(2,1)} %refs_1_.5), channel_id=1, source_target_pairs={{0,8},{8,0},{1,9},{9,1},{2,10},{10,2},{3,11},{11,3},{4,12},{12,4},... | collective-permute-start | bytes 3145736 | tf_op jit(solution)/shard_map/ppermute | solution.py:28
  3.8 17.2 %collective-permute-start.5 = (bf16[512,512]{1,0:T(8,128)(2,1)}, bf16[512,512]{1,0:T(8,128)(2,1)S(1)}, u32[]{:S(2)}, u32[]{:S(2)}) collective-permute-start(bf16[512,512]{1,0:T(8,128)(2,1)} %refs_3_.1), channel_id=1, source_target_pairs={{0,224},{8,232},{16,240},{24,248},{32,0},{40,8},{48,16},{56,24},{6... | collective-permute-start | bytes 1572872 | tf_op jit(solution)/shard_map/ppermute | solution.py:24
  9.4 23.9 %collective-permute-start.3 = (bf16[512,512]{1,0:T(8,128)(2,1)}, bf16[512,512]{1,0:T(8,128)(2,1)S(1)}, u32[]{:S(2)}, u32[]{:S(2)}) collective-permute-start(bf16[512,512]{1,0:T(8,128)(2,1)} %refs_3_.1), channel_id=1, source_target_pairs={{0,240},{8,248},{16,0},{24,8},{32,16},{40,24},{48,32},{56,40},{64,... | collective-permute-start | bytes 1572872 | tf_op jit(solution)/shard_map/ppermute | solution.py:24
  13.8 19.5 %collective-permute-start.2 = (s32[1,4]{1,0:T(1,128)S(1)}, s32[1,4]{1,0:T(1,128)S(1)}, u32[]{:S(2)}, u32[]{:S(2)}) collective-permute-start(s32[1,4]{1,0:T(1,128)S(1)} %copy-done.1), channel_id=1, source_target_pairs={{0,240},{8,248},{16,0},{24,8},{32,16},{40,24},{48,32},{56,40},{64,... | collective-permute-start | bytes 56 | tf_op jit(solution)/shard_map/ppermute | solution.py:24
  14.1 18.1 %collective-permute-start.4 = (s32[1,4]{1,0:T(1,128)S(1)}, s32[1,4]{1,0:T(1,128)S(1)}, u32[]{:S(2)}, u32[]{:S(2)}) collective-permute-start(s32[1,4]{1,0:T(1,128)S(1)} %copy-done.1), channel_id=1, source_target_pairs={{0,224},{8,232},{16,240},{24,248},{32,0},{40,8},{48,16},{56,24},{6... | collective-permute-start | bytes 56 | tf_op jit(solution)/shard_map/ppermute | solution.py:24
  41.3 51.3 %collective-permute-start.12 = (bf16[512,2048]{1,0:T(8,128)(2,1)S(1)}, bf16[512,2048]{1,0:T(8,128)(2,1)S(1)}, u32[]{:S(2)}, u32[]{:S(2)}) collective-permute-start(bf16[512,2048]{1,0:T(8,128)(2,1)S(1)} %collective-permute-done.6.weights.refs_5_), channel_id=1, source_target_pairs={{0,8},{8,0},{1,9},{9,1},{2,10},{10,2},{3,11},{11,3},{4,12},{12,4},... | collective-permute-start | bytes 6291464 | tf_op jit(solution)/shard_map/ppermute | solution.py:28
  48.8 13.9 %collective-permute-start.13 = (bf16[256,2048]{1,0:T(8,128)(2,1)S(1)}, bf16[256,2048]{1,0:T(8,128)(2,1)S(1)}, u32[]{:S(2)}, u32[]{:S(2)}) collective-permute-start(bf16[256,2048]{1,0:T(8,128)(2,1)S(1)} %shard_map.85), channel_id=1, source_target_pairs={{0,1},{1,2},{2,3},{3,0},{8,11},{9,8},{10,9},{11,10},{4,5},{5,6},{6... | collective-permute-start | bytes 3145736 | tf_op jit(solution)/shard_map/ppermute | solution.py:35
  62.8 29.8 %collective-permute-start.14 = (bf16[256,2048]{1,0:T(8,128)(2,1)S(1)}, bf16[256,2048]{1,0:T(8,128)(2,1)S(1)}, u32[]{:S(2)}, u32[]{:S(2)}) collective-permute-start(bf16[256,2048]{1,0:T(8,128)(2,1)S(1)} %collective-permute-done.13.refs_7_), channel_id=1, source_target_pairs={{0,8},{8,0},{1,9},{9,1},{2,10},{10,2},{3,11},{11,3},{4,12},{12,4},... | collective-permute-start | bytes 3145736 | tf_op jit(solution)/shard_map/ppermute | solution.py:28
  64.9 15.0 %collective-permute-start.7 = (bf16[528,512]{1,0:T(8,128)(2,1)S(1)}, bf16[528,512]{1,0:T(8,128)(2,1)S(1)}, u32[]{:S(2)}, u32[]{:S(2)}) collective-permute-start(bf16[528,512]{1,0:T(8,128)(2,1)S(1)} %shard_map.83), channel_id=1, source_target_pairs={{0,32},{8,40},{16,48},{24,56},{32,64},{40,72},{48,80},{56,88},{64,... | collective-permute-start | bytes 1622024 | tf_op jit(solution)/shard_map/ppermute | solution.py:24
  65.0 17.5 %collective-permute-start.8 = (bf16[528,512]{1,0:T(8,128)(2,1)S(1)}, bf16[528,512]{1,0:T(8,128)(2,1)S(1)}, u32[]{:S(2)}, u32[]{:S(2)}) collective-permute-start(bf16[528,512]{1,0:T(8,128)(2,1)S(1)} %shard_map.84), channel_id=1, source_target_pairs={{0,16},{8,24},{16,32},{24,40},{32,48},{40,56},{48,64},{56,72},{64,... | collective-permute-start | bytes 1622024 | tf_op jit(solution)/shard_map/ppermute | solution.py:24
  83.6 8.9 %collective-permute-start.9 = (bf16[128,512]{1,0:T(8,128)(2,1)S(1)}, bf16[128,512]{1,0:T(8,128)(2,1)S(1)}, u32[]{:S(2)}, u32[]{:S(2)}) collective-permute-start(bf16[128,512]{1,0:T(8,128)(2,1)S(1)} %get-tuple-element.29), channel_id=1, source_target_pairs={{0,1},{1,2},{2,3},{3,0},{4,5},{5,6},{6,7},{7,4},{8,9},{9,10},{10,1... | collective-permute-start | bytes 393224 | tf_op jit(solution)/shard_map/ppermute | solution.py:24
  83.7 8.8 %collective-permute-start.10 = (bf16[128,512]{1,0:T(8,128)(2,1)S(1)}, bf16[128,512]{1,0:T(8,128)(2,1)S(1)}, u32[]{:S(2)}, u32[]{:S(2)}) collective-permute-start(bf16[128,512]{1,0:T(8,128)(2,1)S(1)} %get-tuple-element.30), channel_id=1, source_target_pairs={{0,2},{1,3},{2,0},{3,1},{4,6},{5,7},{6,4},{7,5},{8,10},{9,11},{10,... | collective-permute-start | bytes 393224 | tf_op jit(solution)/shard_map/ppermute | solution.py:24
  84.4 8.1 %collective-permute-start.11 = (bf16[128,512]{1,0:T(8,128)(2,1)S(1)}, bf16[128,512]{1,0:T(8,128)(2,1)S(1)}, u32[]{:S(2)}, u32[]{:S(2)}) collective-permute-start(bf16[128,512]{1,0:T(8,128)(2,1)S(1)} %get-tuple-element.31), channel_id=1, source_target_pairs={{0,3},{1,0},{2,1},{3,2},{4,7},{5,4},{6,5},{7,6},{8,11},{9,8},{10,9... | collective-permute-start | bytes 393224 | tf_op jit(solution)/shard_map/ppermute | solution.py:24
  94.1 7.8 %collective-permute-start.15 = (bf16[64,2048]{1,0:T(8,128)(2,1)S(1)}, bf16[64,2048]{1,0:T(8,128)(2,1)S(1)}, u32[]{:S(2)}, u32[]{:S(2)}) collective-permute-start(bf16[64,2048]{1,0:T(8,128)(2,1)S(1)} %shard_map.89), channel_id=1, source_target_pairs={{0,4},{4,0},{1,5},{5,1},{2,6},{6,2},{3,7},{7,3},{8,12},{12,8},{9,1... | collective-permute-start | bytes 786440 | tf_op jit(solution)/shard_map/ppermute | solution.py:28

commit v5 on v4

--- a/solution.py
+++ b/solution.py
@@ -85,43 +85,53 @@
         lax.fori_loop(0, (live + KEY_CHUNK - 1) // KEY_CHUNK, fold, 0)
 
 
-def finish(out_ref, level_ref, m_ref, acc_ref):
-    heads, rows = m_ref.shape[:2]
-    level_ref[...] = jnp.zeros(level_ref.shape, jnp.float32)
-    for h in range(heads):
-        total = acc_ref[h, :, DH:]
-        seen = total > 0
-        safe = jnp.where(seen, total, 1.0)
-        out_ref[:rows, of_head(h)] = (acc_ref[h, :, :DH] / safe).astype(jnp.bfloat16)
-        rest = jnp.where(seen, m_ref[h] + jnp.log2(safe), NEG).T[:1, :]
-        for i in range(3):
-            term = rest.astype(jnp.bfloat16).astype(jnp.float32)
-            level_ref[3 * h + i : 3 * h + i + 1, :rows] = term
-            rest = rest - term
-    out_ref[rows:, :] = level_ref[...].astype(jnp.bfloat16)
-
-
-def home_kernel(offsets, lengths, q_ref, lk_ref, lv_ref, k0, v0, k1, v1, out_ref, m_ref, acc_ref, level_ref, *, half):
+def finish(out_refs, level_ref, m_ref, acc_ref):
+    heads = m_ref.shape[0]
+    for n, out_ref in enumerate(out_refs):
+        rows = out_ref.shape[0] - TAIL
+        span = slice(n * rows, (n + 1) * rows)
+        level_ref[...] = jnp.zeros(level_ref.shape, jnp.float32)
+        for h in range(heads):
+            total = acc_ref[h, span, DH:]
+            seen = total > 0
+            safe = jnp.where(seen, total, 1.0)
+            out_ref[:rows, of_head(h)] = (acc_ref[h, span, :DH] / safe).astype(jnp.bfloat16)
+            rest = jnp.where(seen, m_ref[h, span, :] + jnp.log2(safe), NEG).T[:1, :]
+            for i in range(3):
+                term = rest.astype(jnp.bfloat16).astype(jnp.float32)
+                level_ref[3 * h + i : 3 * h + i + 1, :rows] = term
+                rest = rest - term
+        out_ref[rows:, :] = level_ref[...].astype(jnp.bfloat16)
+
+
+def halves(ref, h):
+    rows, yh = ref.shape[0] // 2, lax.axis_index("yh")
+    return [ref[pl.ds(pl.multiple_of(half * rows, rows), rows), of_head(h)] for half in (1 - yh, yh)]
+
+
+def home_kernel(offsets, lengths, q_ref, lk_ref, lv_ref, k0, v0, k1, v1, *refs, half):
+    *out_refs, m_ref, acc_ref, level_ref = refs
     core, document = lax.axis_index("core"), lax.axis_index(DOC)
     heads, rows = m_ref.shape[:2]
-    first, keys = half * rows, (half + 1) * rows
+    keys, yh = lk_ref.shape[0], lax.axis_index("yh")
+    first = (yh if half else 1 - yh) * rows
     count = sum(jnp.where((offsets[0, i] == 1) & (core == 1), 1, 0) for i in range(offsets.shape[1]))
     reset(m_ref, acc_ref)
 
     def queries(h):
-        return q_ref[first : first + rows, of_head(h)]
+        return halves(q_ref, h)[half]
 
     seen = lax.broadcasted_iota(jnp.int32, (rows, keys), 0) + first >= lax.broadcasted_iota(jnp.int32, (rows, keys), 1)
     for h in range(heads):
-        s = jnp.where(seen, scores_of(queries(h), lk_ref[:keys, of_head(h)]), NEG)
-        absorb(h, s, lv_ref[:keys, of_head(h)], m_ref, acc_ref)
+        s = jnp.where(seen, scores_of(queries(h), lk_ref[:, of_head(h)]), NEG)
+        absorb(h, s, lv_ref[:, of_head(h)], m_ref, acc_ref)
     live = lengths[document], lengths[document + 1 - 2 * core]
     absorb_memories(((k0, v0), (k1, v1)), live, (jnp.int32(1), count), queries, m_ref, acc_ref)
-    finish(out_ref, level_ref, m_ref, acc_ref)
+    finish(out_refs, level_ref, m_ref, acc_ref)
 
 
 def guest_kernel(offsets, lengths, q_ref, k0, v0, k1, v1, *refs, back):
-    out_ref, m_ref, acc_ref, level_ref = refs
+    *out_refs, m_ref, acc_ref, level_ref = refs
     core, document = lax.axis_index("core"), lax.axis_index(DOC)
     reset(m_ref, acc_ref)
     counts = [
@@ -129,8 +139,8 @@
         for wanted in (back, back - 1 + 2 * core)
     ]
     live = lengths[document], lengths[document + 1 - 2 * core]
-    absorb_memories(((k0, v0), (k1, v1)), live, counts, lambda h: q_ref[:, of_head(h)], m_ref, acc_ref)
-    finish(out_ref, level_ref, m_ref, acc_ref)
+    absorb_memories(((k0, v0), (k1, v1)), live, counts, lambda h: jnp.concatenate(halves(q_ref, h), axis=0), m_ref, acc_ref)
+    finish(out_refs, level_ref, m_ref, acc_ref)
 
 
 def on_chip(value):
@@ -153,14 +163,14 @@
     )(*scalars, *arrays)
 
 
-def attention(kernel, scalars, arrays, rows, width):
+def attention(kernel, scalars, arrays, rows, width, parts=1):
     heads = width // DH
     scratch = [
         pltpu.VMEM((heads, rows, DH), jnp.float32),
         pltpu.VMEM((heads, rows, 2 * DH), jnp.float32),
         pltpu.VMEM((TAIL, width), jnp.float32),
     ]
-    return kernel_call(kernel, scalars, arrays, [(rows + TAIL, width)], scratch)[0]
+    return kernel_call(kernel, scalars, arrays, [(rows // parts + TAIL, width)] * parts, scratch)
 
 
 def load_kernel(*refs):
@@ -195,71 +205,60 @@
     return kernel_call(pass_on_kernel, (), (weights,), [(depth // 2, width)], [])[0]
 
 
-def merge_kernel(*refs):
-    *homes, far_ref, near_ref = refs[:4]
-    *tiles, share_ref, whole_ref = refs[4:]
+def merge_kernel(home_ref, near_ref, far_ref, *refs, half):
+    *tiles, share_ref, whole_ref = refs
     rows, width = whole_ref.shape
     heads, count = width // DH, len(tiles)
-    half = rows // 2
-    for n, home_ref in enumerate(homes):
-        span = slice(n * half, (n + 1) * half)
-        parts = [(home_ref, slice(0, half)), (far_ref, span), (near_ref, span)]
-        tails = [part[-TAIL:, where].astype(jnp.float32) for part, where in parts]
-        for h in range(heads):
-            levels = [tail[3 * h : 3 * h + 1] + tail[3 * h + 1 : 3 * h + 2] + tail[3 * h + 2 : 3 * h + 3] for tail in tails]
-            top = jnp.maximum(jnp.maximum(levels[0], levels[1]), levels[2])
-            shares = [jnp.exp2(level - top) for level in levels]
-            total = shares[0] + shares[1] + shares[2]
-            for i, share in enumerate(shares):
-                share_ref[n, 3 * h + i : 3 * h + i + 1, :] = share / total
-        columns = share_ref[n].T
-        for h in range(heads):
-            mixed = 0.0
-            for i, (part, where) in enumerate(parts):
-                mixed = mixed + columns[:, 3 * h + i : 3 * h + i + 1] * part[where, of_head(h)].astype(jnp.float32)
-            whole_ref[span, of_head(h)] = mixed.astype(whole_ref.dtype)
-    block = half // count
-    x, yh = lax.axis_index("x"), lax.axis_index("yh")
+    first = slice(0, rows)
+    parts = [(home_ref, first), (far_ref, slice(half * rows, (half + 1) * rows)), (near_ref, first)]
+    tails = [part[-TAIL:, where].astype(jnp.float32) for part, where in parts]
+    for h in range(heads):
+        levels = [tail[3 * h : 3 * h + 1] + tail[3 * h + 1 : 3 * h + 2] + tail[3 * h + 2 : 3 * h + 3] for tail in tails]
+        top = jnp.maximum(jnp.maximum(levels[0], levels[1]), levels[2])
+        shares = [jnp.exp2(level - top) for level in levels]
+        total = shares[0] + shares[1] + shares[2]
+        for i, share in enumerate(shares):
+            share_ref[3 * h + i : 3 * h + i + 1, :] = share / total
+    columns = share_ref[...].T
+    for h in range(heads):
+        mixed = 0.0
+        for i, (part, where) in enumerate(parts):
+            mixed = mixed + columns[:, 3 * h + i : 3 * h + i + 1] * part[where, of_head(h)].astype(jnp.float32)
+        whole_ref[:, of_head(h)] = mixed.astype(whole_ref.dtype)
+    block, x = rows // count, lax.axis_index("x")
     for k, tile in enumerate(tiles):
-        for n, side in enumerate((1 - yh, yh)):
-            first = side * half + (x + k) % count * block
-            tile[n * block : (n + 1) * block, :] = whole_ref[pl.ds(pl.multiple_of(first, block), block), :]
-
-
-def merge(home0, home1, far, near):
-    rows, width = far.shape[0] - TAIL, far.shape[1]
+        tile[...] = whole_ref[pl.ds(pl.multiple_of((x + k) % count * block, block), block), :]
+
+
+def merge(home, near, far, half):
+    def kernel(*refs):
+        merge_kernel(*refs, half=half)
+
+    rows, width = home.shape[0] - TAIL, home.shape[1]
     count = lax.axis_size("x")
-    scratch = [pltpu.VMEM((2, DH, rows // 2), jnp.float32), pltpu.VMEM((rows, width), jnp.bfloat16)]
-    return kernel_call(merge_kernel, (), (home0, home1, far, near), [(rows // count, width)] * count, scratch)
-
-
-def project_kernel(*refs, part):
-    mine, below, opposite, above, own, near, near_other, far, far_other, *extra, out_ref = refs
-    rows, half = out_ref.shape[0], far.shape[0]
+    scratch = [pltpu.VMEM((DH, rows), jnp.float32), pltpu.VMEM((rows, width), jnp.bfloat16)]
+    return kernel_call(kernel, (), (home, near, far), [(rows // count, width)] * count, scratch)
+
+
+def project_kernel(*refs):
+    mine, below, opposite, above, own, near, near_other, far, far_other, out_ref = refs
+    half = far.shape[0]
     core = lax.axis_index("core")
 
-    def tile(ref):
-        return ref[part * rows : (part + 1) * rows, :]
-
     pairs = [
-        (tile(mine), own),
-        (jnp.where(core == 0, tile(below), tile(above)), near),
-        (jnp.where(core == 0, tile(above), tile(below)), near_other),
-        (jnp.where(core == 0, tile(opposite)[:, :half], tile(opposite)[:, half:]), far),
-        (jnp.where(core == 0, tile(opposite)[:, half:], tile(opposite)[:, :half]), far_other),
+        (mine[...], own),
+        (jnp.where(core == 0, below[...], above[...]), near),
+        (jnp.where(core == 0, above[...], below[...]), near_other),
+        (jnp.where(core == 0, opposite[:, :half], opposite[:, half:]), far),
+        (jnp.where(core == 0, opposite[:, half:], opposite[:, :half]), far_other),
     ]
     acc = sum(jnp.dot(a, w[...], preferred_element_type=jnp.float32) for a, w in pairs)
-    for ref in extra:
-        acc = acc + ref[...].astype(jnp.float32)
     out_ref[...] = acc.astype(out_ref.dtype)
 
 
-def project(tiles, weights, extra, part):
-    def kernel(*refs):
-        project_kernel(*refs, part=part)
-
-    out = (tiles[0].shape[0] // 2, weights[0].shape[1])
-    return kernel_call(kernel, (), (*tiles, *weights, *extra), [out], [])[0]
+def project(tiles, weights):
+    out = (tiles[0].shape[0], weights[0].shape[1])
+    return kernel_call(project_kernel, (), (*tiles, *weights), [out], [])[0]
 
 
 def after(value, *others):
@@ -287,30 +286,35 @@
         def kernel(*refs):
             home_kernel(*refs, half=half)
 
-        return attention(kernel, (offsets, mem_lengths), (*local, *memory), rows // 2, width)
-
-    def guest(load, table, back):
+        return attention(kernel, (offsets, mem_lengths), (*local, *memory), rows // 2, width)[0]
+
+    def guest(load, table, back, parts=1):
         def kernel(*refs):
             guest_kernel(*refs, back=back)
 
-        out = attention(kernel, (table, mem_lengths), (load, *memory), rows, width)
-        return moved(shift, out, DOC, back), out
+        return attention(kernel, (table, mem_lengths), (load, *memory), rows, width, parts)
 
     home0 = at_home(local, 0)
-    from_far, far = guest(after(query_far, home0), offsets_far, 4)
-    from_near, near = guest(after(query_near, far), offsets_near, 2)
-
-    near_weight = after(near_weight, near)
+    (far,) = guest(after(query_far, home0), offsets_far, 4)
+    from_far = moved(shift, far, DOC, 4)
+    near = guest(after(query_near, far), offsets_near, 2, 2)
+    from_near = [moved(shift, out, DOC, 2) for out in near]
+
+    near_weight = after(near_weight, *near)
     passed_on = pass_on(near_weight)
-    home1 = at_home((after(local[0], near, passed_on), *local[1:]), 1)
+    home1 = at_home((after(local[0], *near, passed_on), *local[1:]), 1)
     far_weight = moved(part_ways, passed_on)
     weights = [own_weight, near_weight, moved(swap, near_weight, "core"), far_weight, moved(swap, far_weight, "core")]
 
-    mine, *tiles = merge(home0, home1, from_far, from_near)
-    tiles = mine, *(moved(shift, tile, "x", k) for k, tile in enumerate(tiles, 1))
-    given = project(tiles, weights, (), 0)
+    def tiles_of(home, near, half):
+        mine, *tiles = merge(home, near, from_far, half)
+        return mine, *(moved(shift, tile, "x", k) for k, tile in enumerate(tiles, 1))
+
+    given = tiles_of(after(home0, home1), from_near[0], 0)
+    kept = tiles_of(home1, after(from_near[1], given[0]), 1)
+    given = project(given, weights)
     taken = swap(given, "yh")
-    kept = project(tiles, weights, (), 1)
+    kept = project(kept, weights)
     return (kept.astype(jnp.float32) + taken.astype(jnp.float32)).astype(jnp.bfloat16)
 
 

time: 104 us -> 105 us (level)
  the two profiles are of different devices: /device:TPU:1 before, /device:TPU:2 now
where the time goes in v5:
time: 105 us
  waiting for transfers between devices  44.6 us (42%)
  Pallas kernels  30.5 us (29%)
  starting transfers between devices  29.3 us (28%)
    ppermute x13, waiting for transfers between devices, shift(): lax.ppermute(value, axis, [(i, (i + steps) % count) for i in range(count)])  31 us
    pallas_call x9, Pallas kernels, kernel_call(): pl.pallas_call(kernel, grid_spec=pltpu.PrefetchScalarGridSpec(num_scalar_...  27.8 us
    ppermute x13, starting transfers between devices, shift(): lax.ppermute(value, axis, [(i, (i + steps) % count) for i in range(count)])  22.8 us
    ppermute x2, waiting for transfers between devices, part_ways(): return lax.ppermute(value, ('core', 'x'), up + down)  13.6 us
    ppermute x5, starting transfers between devices, swap(): return lax.ppermute(value, axis, [(0, 1), (1, 0)])  3.8 us
    ppermute x2, starting transfers between devices, part_ways(): return lax.ppermute(value, ('core', 'x'), up + down)  2.77 us
    pallas_call x1, Pallas kernels, load(): pl.pallas_call(load_kernel, in_specs=[pl.BlockSpec(memory_space=pltpu.HBM...  2.67 us
  transfers between devices with their start and end apart: 20, of which 9 were waited for; matrix products, arithmetic and copies ran while one was open for 0% of the time, Pallas kernels for 29%

profile of v5, /device:TPU:2, one launch (start us, length us, event | category | flops | bytes accessed | tf_op | source)
XLA Modules:
  0.0 105.3 jit_solution(4121767592476703491)
XLA Ops:
  0.0 0.0 copy-start.1
  0.0 0.0 copy-start
  0.0 1.5 %collective-permute-start.6 = (bf16[512,2048]{1,0:T(8,128)(2,1)}, bf16[512,2048]{1,0:T(8,128)(2,1)S(1)}, u32[]{:S(2)}, u32[]{:S(2)}) collective-permute-start(bf16[512,2048]{1,0:T(8,128)(2,1)} %refs_2_.1), channel_id=1, source_target_pairs={{0,1},{1,2},{2,3},{3,0},{8,11},{9,8},{10,9},{11,10},{4,5},{5,6},{6... | collective-permute-start | bytes 6291464 | tf_op jit(solution)/shard_map/ppermute | solution.py:35
  1.5 0.0 collective-permute-start.4
  1.5 0.5 collective-permute-start.5
  2.0 5.9 %collective-permute-start.3 = (bf16[512,512]{1,0:T(8,128)(2,1)}, bf16[512,512]{1,0:T(8,128)(2,1)S(1)}, u32[]{:S(2)}, u32[]{:S(2)}) collective-permute-start(bf16[512,512]{1,0:T(8,128)(2,1)} %refs_3_.1), channel_id=1, source_target_pairs={{0,224},{8,232},{16,240},{24,248},{32,0},{40,8},{48,16},{56,24},{6... | collective-permute-start | bytes 1572872 | tf_op jit(solution)/shard_map/ppermute | solution.py:24
  7.9 2.0 %collective-permute-start.1 = (bf16[512,512]{1,0:T(8,128)(2,1)}, bf16[512,512]{1,0:T(8,128)(2,1)S(1)}, u32[]{:S(2)}, u32[]{:S(2)}) collective-permute-start(bf16[512,512]{1,0:T(8,128)(2,1)} %refs_3_.1), channel_id=1, source_target_pairs={{0,240},{8,248},{16,0},{24,8},{32,16},{40,24},{48,32},{56,40},{64,... | collective-permute-start | bytes 1572872 | tf_op jit(solution)/shard_map/ppermute | solution.py:24
  9.9 2.7 %load.1 = (bf16[1024,512]{1,0:T(8,128)(2,1)S(1)}, bf16[1024,512]{1,0:T(8,128)(2,1)S(1)}, bf16[512,2048]{1,0:T(8,128)(2,1)S(1)}, bf16[512,512]{1,0:T(8,128)(2,1)S...) custom-call(bf16[1024,512]{1,0:T(8,128)(2,1)} %refs_0_.3, bf16[1024,512]{1,0:T(8,128)(2,1)} %refs_1_.5, ...), custom_call_target="tpu_custom_call" | custom-call | tf_op jit(solution)/shard_map/load/pallas_call | solution.py:187
  12.6 0.0 collective-permute-done.4.refs_7_.refs_5_
  12.6 0.0 copy-done.1
  12.6 1.1 %collective-permute-start.2 = (s32[1,4]{1,0:T(1,128)S(1)}, s32[1,4]{1,0:T(1,128)S(1)}, u32[]{:S(2)}, u32[]{:S(2)}) collective-permute-start(s32[1,4]{1,0:T(1,128)S(1)} %copy-done.1), channel_id=1, source_target_pairs={{0,224},{8,232},{16,240},{24,248},{32,0},{40,8},{48,16},{56,24},{6... | collective-permute-start | bytes 56 | tf_op jit(solution)/shard_map/ppermute | solution.py:24
  13.7 0.0 collective-permute-done.5.refs_8_.refs_6_
  13.7 0.5 collective-permute-start
  14.1 0.0 copy-done
  14.1 3.9 %shard_map.82.refs_0_ = bf16[272,512]{1,0:T(8,128)(2,1)S(1)} custom-call(s32[1,4]{1,0:T(1,128)S(1)} %copy-done.1, s32[32]{0:T(128)S(1)} %copy-done, bf16[512,512]{1,0:T(8,128)(2,1)S(1)} %get-tuple-element.37.refs_2_, bf16[512,512]{1,0:T(8,128)(2,1)S(1)} %get-tuple-element.28.refs_3_, bf16[512,512]{1,0:T(8,128)(2,1)S(1)} %get-tuple-element.29.refs_4_, ...), custom_call_target="tpu_custom_call" | custom-call | tf_op jit(solution)/shard_map/pallas_call | solution.py:152
  18.0 2.5 %collective-permute-done.3.refs_2_ = bf16[512,512]{1,0:T(8,128)(2,1)S(1)} collective-permute-done((bf16[512,512]{1,0:T(8,128)(2,1)}, bf16[512,512]{1,0:T(8,128)(2,1)S(1)}, u32[]{:S(2)}, u32[]{:S(2)}) %collective-permute-start.3) | collective-permute-done | bytes 524320 | tf_op jit(solution)/shard_map/ppermute | solution.py:24
  20.5 10.3 %collective-permute-done.2.refs_0_ = s32[1,4]{1,0:T(1,128)S(1)} collective-permute-done((s32[1,4]{1,0:T(1,128)S(1)}, s32[1,4]{1,0:T(1,128)S(1)}, u32[]{:S(2)}, u32[]{:S(2)}) %collective-permute-start.2) | collective-permute-done | bytes 48 | tf_op jit(solution)/shard_map/ppermute | solution.py:24
  30.8 7.7 %shard_map.83 = bf16[528,512]{1,0:T(8,128)(2,1)S(1)} custom-call(s32[1,4]{1,0:T(1,128)S(1)} %collective-permute-done.2.refs_0_, s32[32]{0:T(128)S(1)} %copy-done, bf16[512,512]{1,0:T(8,128)(2,1)S(1)} %collective-permute-done.3.refs_2_, bf16[1024,512]{1,0:T(8,128)(2,1)S(1)} %get-tuple-element.30.refs_5_.refs_3_, ...), custom_call_target="tpu_custom_call" | custom-call | tf_op jit(solution)/shard_map/pallas_call | solution.py:152
  38.5 0.0 collective-permute-done.1.refs_2_
  38.5 0.0 collective-permute-done.refs_0_
  38.5 7.9 %shard_map.84 = (bf16[272,512]{1,0:T(8,128)(2,1)S(1)}, bf16[272,512]{1,0:T(8,128)(2,1)S(1)}) custom-call(s32[1,4]{1,0:T(1,128)S(1)} %collective-permute-done.refs_0_, s32[32]{0:T(128)S(1)} %copy-done, bf16[512,512]{1,0:T(8,128)(2,1)S(1)} %collective-permute-done.1.refs_2_, bf16[1024,512]{1,0:T(8,128)(2,1)S(1)} %get-tuple-element.30.refs_5_.refs_3_, ...), custom_call_target="tpu_custom_call" | custom-call | tf_op jit(solution)/shard_map/pallas_call | solution.py:152
  46.4 0.0 collective-permute-done.6.weights.refs_5_
  46.4 0.1 shard_map.85
  46.5 1.3 %collective-permute-start.14 = (bf16[256,2048]{1,0:T(8,128)(2,1)S(1)}, bf16[256,2048]{1,0:T(8,128)(2,1)S(1)}, u32[]{:S(2)}, u32[]{:S(2)}) collective-permute-start(bf16[256,2048]{1,0:T(8,128)(2,1)S(1)} %shard_map.85), channel_id=1, source_target_pairs={{0,1},{1,2},{2,3},{3,0},{8,11},{9,8},{10,9},{11,10},{4,5},{5,6},{6... | collective-permute-start | bytes 3145736 | tf_op jit(solution)/shard_map/ppermute | solution.py:35
  47.7 0.0 collective-permute-start.13
  47.7 13.6 %collective-permute-done.14.refs_7_ = bf16[256,2048]{1,0:T(8,128)(2,1)S(1)} collective-permute-done((bf16[256,2048]{1,0:T(8,128)(2,1)S(1)}, bf16[256,2048]{1,0:T(8,128)(2,1)S(1)}, u32[]{:S(2)}, u32[]{:S(2)}) %collective-permute-start.14) | collective-permute-done | bytes 1048608 | tf_op jit(solution)/shard_map/ppermute | solution.py:35
  61.3 0.0 collective-permute-start.15
  61.3 0.0 collective-permute-start.9
  61.3 0.0 collective-permute-start.8
  61.4 3.9 %shard_map.86.refs_0_ = bf16[272,512]{1,0:T(8,128)(2,1)S(1)} custom-call(s32[1,4]{1,0:T(1,128)S(1)} %copy-done.1, s32[32]{0:T(128)S(1)} %copy-done, bf16[512,512]{1,0:T(8,128)(2,1)S(1)} %get-tuple-element.37.refs_2_, bf16[512,512]{1,0:T(8,128)(2,1)S(1)} %get-tuple-element.28.refs_3_, bf16[512,512]{1,0:T(8,128)(2,1)S(1)} %get-tuple-element.29.refs_4_, ...), custom_call_target="tpu_custom_call" | custom-call | tf_op jit(solution)/shard_map/pallas_call | solution.py:152
  65.3 8.6 %collective-permute-done.8.refs_1_ = bf16[272,512]{1,0:T(8,128)(2,1)S(1)} collective-permute-done((bf16[272,512]{1,0:T(8,128)(2,1)S(1)}, bf16[272,512]{1,0:T(8,128)(2,1)S(1)}, u32[]{:S(2)}, u32[]{:S(2)}) %collective-permute-start.8) | collective-permute-done | bytes 278560 | tf_op jit(solution)/shard_map/ppermute | solution.py:24
  73.8 3.4 %collective-permute-done.9.refs_2_ = bf16[528,512]{1,0:T(8,128)(2,1)S(1)} collective-permute-done((bf16[528,512]{1,0:T(8,128)(2,1)S(1)}, bf16[528,512]{1,0:T(8,128)(2,1)S(1)}, u32[]{:S(2)}, u32[]{:S(2)}) %collective-permute-start.9) | collective-permute-done | bytes 540704 | tf_op jit(solution)/shard_map/ppermute | solution.py:24
  77.2 0.6 shard_map.87
  77.9 1.3 %collective-permute-start.16 = (bf16[64,512]{1,0:T(8,128)(2,1)S(1)}, bf16[64,512]{1,0:T(8,128)(2,1)S(1)}, u32[]{:S(2)}, u32[]{:S(2)}) collective-permute-start(bf16[64,512]{1,0:T(8,128)(2,1)S(1)} %get-tuple-element.46), channel_id=1, source_target_pairs={{0,1},{1,2},{2,3},{3,0},{4,5},{5,6},{6,7},{7,4},{8,9},{9,10},{10,1... | collective-permute-start | bytes 196616 | tf_op jit(solution)/shard_map/ppermute | solution.py:24
  79.2 0.0 collective-permute-start.7
  79.2 3.4 %collective-permute-start.17 = (bf16[64,512]{1,0:T(8,128)(2,1)S(1)}, bf16[64,512]{1,0:T(8,128)(2,1)S(1)}, u32[]{:S(2)}, u32[]{:S(2)}) collective-permute-start(bf16[64,512]{1,0:T(8,128)(2,1)S(1)} %get-tuple-element.47), channel_id=1, source_target_pairs={{0,2},{1,3},{2,0},{3,1},{4,6},{5,7},{6,4},{7,5},{8,10},{9,11},{10,... | collective-permute-start | bytes 196616 | tf_op jit(solution)/shard_map/ppermute | solution.py:24
  82.6 0.7 collective-permute-done.16.refs_1_
  83.3 3.5 %collective-permute-start.18 = (bf16[64,512]{1,0:T(8,128)(2,1)S(1)}, bf16[64,512]{1,0:T(8,128)(2,1)S(1)}, u32[]{:S(2)}, u32[]{:S(2)}) collective-permute-start(bf16[64,512]{1,0:T(8,128)(2,1)S(1)} %get-tuple-element.48), channel_id=1, source_target_pairs={{0,3},{1,0},{2,1},{3,2},{4,7},{5,4},{6,5},{7,6},{8,11},{9,8},{10,9... | collective-permute-start | bytes 196616 | tf_op jit(solution)/shard_map/ppermute | solution.py:24
  86.8 0.0 collective-permute-done.17.refs_2_
  86.8 1.9 %collective-permute-done.18.refs_3_ = bf16[64,512]{1,0:T(8,128)(2,1)S(1)} collective-permute-done((bf16[64,512]{1,0:T(8,128)(2,1)S(1)}, bf16[64,512]{1,0:T(8,128)(2,1)S(1)}, u32[]{:S(2)}, u32[]{:S(2)}) %collective-permute-start.18) | collective-permute-done | bytes 65568 | tf_op jit(solution)/shard_map/ppermute | solution.py:24
  88.7 0.0 collective-permute-done.15.refs_8_
  88.7 0.0 collective-permute-done.13.refs_6_
  88.7 1.6 %shard_map.90 = bf16[64,2048]{1,0:T(8,128)(2,1)S(1)} custom-call(bf16[64,512]{1,0:T(8,128)(2,1)S(1)} %get-tuple-element.39.refs_0_, bf16[64,512]{1,0:T(8,128)(2,1)S(1)} %collective-permute-done.16.refs_1_, bf16[64,512]{1,0:T(8,128)(2,1)S(1)} %collective-permute-done.17.refs_2_, bf16[64,512]{1,0:T(8,128)(2,1)S(1)} %collective-permute-done.18.refs_3_, ...), custom_call_target="tpu_custom_call" | custom-call | tf_op jit(solution)/shard_map/pallas_call | solution.py:152
  90.3 3.3 %collective-permute-start.19 = (bf16[64,2048]{1,0:T(8,128)(2,1)S(1)}, bf16[64,2048]{1,0:T(8,128)(2,1)S(1)}, u32[]{:S(2)}, u32[]{:S(2)}) collective-permute-start(bf16[64,2048]{1,0:T(8,128)(2,1)S(1)} %shard_map.90), channel_id=1, source_target_pairs={{0,4},{4,0},{1,5},{5,1},{2,6},{6,2},{3,7},{7,3},{8,12},{12,8},{9,1... | collective-permute-start | bytes 786440 | tf_op jit(solution)/shard_map/ppermute | solution.py:28
  93.6 0.0 collective-permute-done.7.refs_1_
  93.6 0.6 shard_map.88
  94.2 0.1 collective-permute-start.10
  94.3 4.4 %collective-permute-start.11 = (bf16[64,512]{1,0:T(8,128)(2,1)S(1)}, bf16[64,512]{1,0:T(8,128)(2,1)S(1)}, u32[]{:S(2)}, u32[]{:S(2)}) collective-permute-start(bf16[64,512]{1,0:T(8,128)(2,1)S(1)} %get-tuple-element.43), channel_id=1, source_target_pairs={{0,2},{1,3},{2,0},{3,1},{4,6},{5,7},{6,4},{7,5},{8,10},{9,11},{10,... | collective-permute-start | bytes 196616 | tf_op jit(solution)/shard_map/ppermute | solution.py:24
  98.7 0.6 collective-permute-start.12
  99.3 0.0 collective-permute-done.10.refs_1_
  99.3 1.6 %collective-permute-done.11.refs_2_ = bf16[64,512]{1,0:T(8,128)(2,1)S(1)} collective-permute-done((bf16[64,512]{1,0:T(8,128)(2,1)S(1)}, bf16[64,512]{1,0:T(8,128)(2,1)S(1)}, u32[]{:S(2)}, u32[]{:S(2)}) %collective-permute-start.11) | collective-permute-done | bytes 65568 | tf_op jit(solution)/shard_map/ppermute | solution.py:24
  101.0 2.0 %collective-permute-done.12.refs_3_ = bf16[64,512]{1,0:T(8,128)(2,1)S(1)} collective-permute-done((bf16[64,512]{1,0:T(8,128)(2,1)S(1)}, bf16[64,512]{1,0:T(8,128)(2,1)S(1)}, u32[]{:S(2)}, u32[]{:S(2)}) %collective-permute-start.12) | collective-permute-done | bytes 65568 | tf_op jit(solution)/shard_map/ppermute | solution.py:24
  103.0 1.6 %shard_map.89 = bf16[64,2048]{1,0:T(8,128)(2,1)S(1)} custom-call(bf16[64,512]{1,0:T(8,128)(2,1)S(1)} %get-tuple-element.41.refs_0_, bf16[64,512]{1,0:T(8,128)(2,1)S(1)} %collective-permute-done.10.refs_1_, bf16[64,512]{1,0:T(8,128)(2,1)S(1)} %collective-permute-done.11.refs_2_, bf16[64,512]{1,0:T(8,128)(2,1)S(1)} %collective-permute-done.12.refs_3_, ...), custom_call_target="tpu_custom_call" | custom-call | tf_op jit(solution)/shard_map/pallas_call | solution.py:152
  104.5 0.0 collective-permute-done.19
  104.6 0.8 add_convert_fusion
Async XLA Ops:
  0.0 12.6 %copy-start.1 = (s32[1,4]{1,0:T(1,128)S(1)}, s32[1,4]{1,0:T(1,128)}, u32[]{:S(2)}) copy-start(s32[1,4]{1,0:T(1,128)} %refs_0_.5) | copy-start | bytes 52
  0.0 14.1 %copy-start = (s32[32]{0:T(128)S(1)}, s32[32]{0:T(128)}, u32[]{:S(2)}) copy-start(s32[32]{0:T(128)} %refs_1_.9) | copy-start | bytes 388
  0.0 46.4 %collective-permute-start.6 = (bf16[512,2048]{1,0:T(8,128)(2,1)}, bf16[512,2048]{1,0:T(8,128)(2,1)S(1)}, u32[]{:S(2)}, u32[]{:S(2)}) collective-permute-start(bf16[512,2048]{1,0:T(8,128)(2,1)} %refs_2_.1), channel_id=1, source_target_pairs={{0,1},{1,2},{2,3},{3,0},{8,11},{9,8},{10,9},{11,10},{4,5},{5,6},{6... | collective-permute-start | bytes 6291464 | tf_op jit(solution)/shard_map/ppermute | solution.py:35
  1.5 11.1 %collective-permute-start.4 = (bf16[1024,512]{1,0:T(8,128)(2,1)}, bf16[1024,512]{1,0:T(8,128)(2,1)S(1)}, u32[]{:S(2)}, u32[]{:S(2)}) collective-permute-start(bf16[1024,512]{1,0:T(8,128)(2,1)} %refs_0_.3), channel_id=1, source_target_pairs={{0,8},{8,0},{1,9},{9,1},{2,10},{10,2},{3,11},{11,3},{4,12},{12,4},... | collective-permute-start | bytes 3145736 | tf_op jit(solution)/shard_map/ppermute | solution.py:28
  1.5 12.2 %collective-permute-start.5 = (bf16[1024,512]{1,0:T(8,128)(2,1)}, bf16[1024,512]{1,0:T(8,128)(2,1)S(1)}, u32[]{:S(2)}, u32[]{:S(2)}) collective-permute-start(bf16[1024,512]{1,0:T(8,128)(2,1)} %refs_1_.5), channel_id=1, source_target_pairs={{0,8},{8,0},{1,9},{9,1},{2,10},{10,2},{3,11},{11,3},{4,12},{12,4},... | collective-permute-start | bytes 3145736 | tf_op jit(solution)/shard_map/ppermute | solution.py:28
  2.0 18.5 %collective-permute-start.3 = (bf16[512,512]{1,0:T(8,128)(2,1)}, bf16[512,512]{1,0:T(8,128)(2,1)S(1)}, u32[]{:S(2)}, u32[]{:S(2)}) collective-permute-start(bf16[512,512]{1,0:T(8,128)(2,1)} %refs_3_.1), channel_id=1, source_target_pairs={{0,224},{8,232},{16,240},{24,248},{32,0},{40,8},{48,16},{56,24},{6... | collective-permute-start | bytes 1572872 | tf_op jit(solution)/shard_map/ppermute | solution.py:24
  7.9 30.6 %collective-permute-start.1 = (bf16[512,512]{1,0:T(8,128)(2,1)}, bf16[512,512]{1,0:T(8,128)(2,1)S(1)}, u32[]{:S(2)}, u32[]{:S(2)}) collective-permute-start(bf16[512,512]{1,0:T(8,128)(2,1)} %refs_3_.1), channel_id=1, source_target_pairs={{0,240},{8,248},{16,0},{24,8},{32,16},{40,24},{48,32},{56,40},{64,... | collective-permute-start | bytes 1572872 | tf_op jit(solution)/shard_map/ppermute | solution.py:24
  12.6 18.2 %collective-permute-start.2 = (s32[1,4]{1,0:T(1,128)S(1)}, s32[1,4]{1,0:T(1,128)S(1)}, u32[]{:S(2)}, u32[]{:S(2)}) collective-permute-start(s32[1,4]{1,0:T(1,128)S(1)} %copy-done.1), channel_id=1, source_target_pairs={{0,224},{8,232},{16,240},{24,248},{32,0},{40,8},{48,16},{56,24},{6... | collective-permute-start | bytes 56 | tf_op jit(solution)/shard_map/ppermute | solution.py:24
  13.7 24.8 %collective-permute-start = (s32[1,4]{1,0:T(1,128)S(1)}, s32[1,4]{1,0:T(1,128)S(1)}, u32[]{:S(2)}, u32[]{:S(2)}) collective-permute-start(s32[1,4]{1,0:T(1,128)S(1)} %copy-done.1), channel_id=1, source_target_pairs={{0,240},{8,248},{16,0},{24,8},{32,16},{40,24},{48,32},{56,40},{64,... | collective-permute-start | bytes 56 | tf_op jit(solution)/shard_map/ppermute | solution.py:24
  46.5 14.9 %collective-permute-start.14 = (bf16[256,2048]{1,0:T(8,128)(2,1)S(1)}, bf16[256,2048]{1,0:T(8,128)(2,1)S(1)}, u32[]{:S(2)}, u32[]{:S(2)}) collective-permute-start(bf16[256,2048]{1,0:T(8,128)(2,1)S(1)} %shard_map.85), channel_id=1, source_target_pairs={{0,1},{1,2},{2,3},{3,0},{8,11},{9,8},{10,9},{11,10},{4,5},{5,6},{6... | collective-permute-start | bytes 3145736 | tf_op jit(solution)/shard_map/ppermute | solution.py:35
  47.7 41.0 %collective-permute-start.13 = (bf16[512,2048]{1,0:T(8,128)(2,1)S(1)}, bf16[512,2048]{1,0:T(8,128)(2,1)S(1)}, u32[]{:S(2)}, u32[]{:S(2)}) collective-permute-start(bf16[512,2048]{1,0:T(8,128)(2,1)S(1)} %collective-permute-done.6.weights.refs_5_), channel_id=1, source_target_pairs={{0,8},{8,0},{1,9},{9,1},{2,10},{10,2},{3,11},{11,3},{4,12},{12,4},... | collective-permute-start | bytes 6291464 | tf_op jit(solution)/shard_map/ppermute | solution.py:28
  61.3 27.4 %collective-permute-start.15 = (bf16[256,2048]{1,0:T(8,128)(2,1)S(1)}, bf16[256,2048]{1,0:T(8,128)(2,1)S(1)}, u32[]{:S(2)}, u32[]{:S(2)}) collective-permute-start(bf16[256,2048]{1,0:T(8,128)(2,1)S(1)} %collective-permute-done.14.refs_7_), channel_id=1, source_target_pairs={{0,8},{8,0},{1,9},{9,1},{2,10},{10,2},{3,11},{11,3},{4,12},{12,4},... | collective-permute-start | bytes 3145736 | tf_op jit(solution)/shard_map/ppermute | solution.py:28
  61.3 15.9 %collective-permute-start.9 = (bf16[528,512]{1,0:T(8,128)(2,1)S(1)}, bf16[528,512]{1,0:T(8,128)(2,1)S(1)}, u32[]{:S(2)}, u32[]{:S(2)}) collective-permute-start(bf16[528,512]{1,0:T(8,128)(2,1)S(1)} %shard_map.83), channel_id=1, source_target_pairs={{0,32},{8,40},{16,48},{24,56},{32,64},{40,72},{48,80},{56,88},{64,... | collective-permute-start | bytes 1622024 | tf_op jit(solution)/shard_map/ppermute | solution.py:24
  61.3 12.5 %collective-permute-start.8 = (bf16[272,512]{1,0:T(8,128)(2,1)S(1)}, bf16[272,512]{1,0:T(8,128)(2,1)S(1)}, u32[]{:S(2)}, u32[]{:S(2)}) collective-permute-start(bf16[272,512]{1,0:T(8,128)(2,1)S(1)} %get-tuple-element.34), channel_id=1, source_target_pairs={{0,16},{8,24},{16,32},{24,40},{32,48},{40,56},{48,64},{56,72},{64,... | collective-permute-start | bytes 835592 | tf_op jit(solution)/shard_map/ppermute | solution.py:24
  77.9 5.4 %collective-permute-start.16 = (bf16[64,512]{1,0:T(8,128)(2,1)S(1)}, bf16[64,512]{1,0:T(8,128)(2,1)S(1)}, u32[]{:S(2)}, u32[]{:S(2)}) collective-permute-start(bf16[64,512]{1,0:T(8,128)(2,1)S(1)} %get-tuple-element.46), channel_id=1, source_target_pairs={{0,1},{1,2},{2,3},{3,0},{4,5},{5,6},{6,7},{7,4},{8,9},{9,10},{10,1... | collective-permute-start | bytes 196616 | tf_op jit(solution)/shard_map/ppermute | solution.py:24
  79.2 14.4 %collective-permute-start.7 = (bf16[272,512]{1,0:T(8,128)(2,1)S(1)}, bf16[272,512]{1,0:T(8,128)(2,1)S(1)}, u32[]{:S(2)}, u32[]{:S(2)}) collective-permute-start(bf16[272,512]{1,0:T(8,128)(2,1)S(1)} %get-tuple-element.35), channel_id=1, source_target_pairs={{0,16},{8,24},{16,32},{24,40},{32,48},{40,56},{48,64},{56,72},{64,... | collective-permute-start | bytes 835592 | tf_op jit(solution)/shard_map/ppermute | solution.py:24
  79.2 7.6 %collective-permute-start.17 = (bf16[64,512]{1,0:T(8,128)(2,1)S(1)}, bf16[64,512]{1,0:T(8,128)(2,1)S(1)}, u32[]{:S(2)}, u32[]{:S(2)}) collective-permute-start(bf16[64,512]{1,0:T(8,128)(2,1)S(1)} %get-tuple-element.47), channel_id=1, source_target_pairs={{0,2},{1,3},{2,0},{3,1},{4,6},{5,7},{6,4},{7,5},{8,10},{9,11},{10,... | collective-permute-start | bytes 196616 | tf_op jit(solution)/shard_map/ppermute | solution.py:24
  83.3 5.4 %collective-permute-start.18 = (bf16[64,512]{1,0:T(8,128)(2,1)S(1)}, bf16[64,512]{1,0:T(8,128)(2,1)S(1)}, u32[]{:S(2)}, u32[]{:S(2)}) collective-permute-start(bf16[64,512]{1,0:T(8,128)(2,1)S(1)} %get-tuple-element.48), channel_id=1, source_target_pairs={{0,3},{1,0},{2,1},{3,2},{4,7},{5,4},{6,5},{7,6},{8,11},{9,8},{10,9... | collective-permute-start | bytes 196616 | tf_op jit(solution)/shard_map/ppermute | solution.py:24
  90.3 14.3 %collective-permute-start.19 = (bf16[64,2048]{1,0:T(8,128)(2,1)S(1)}, bf16[64,2048]{1,0:T(8,128)(2,1)S(1)}, u32[]{:S(2)}, u32[]{:S(2)}) collective-permute-start(bf16[64,2048]{1,0:T(8,128)(2,1)S(1)} %shard_map.90), channel_id=1, source_target_pairs={{0,4},{4,0},{1,5},{5,1},{2,6},{6,2},{3,7},{7,3},{8,12},{12,8},{9,1... | collective-permute-start | bytes 786440 | tf_op jit(solution)/shard_map/ppermute | solution.py:28
  94.2 5.1 %collective-permute-start.10 = (bf16[64,512]{1,0:T(8,128)(2,1)S(1)}, bf16[64,512]{1,0:T(8,128)(2,1)S(1)}, u32[]{:S(2)}, u32[]{:S(2)}) collective-permute-start(bf16[64,512]{1,0:T(8,128)(2,1)S(1)} %get-tuple-element.42), channel_id=1, source_target_pairs={{0,1},{1,2},{2,3},{3,0},{4,5},{5,6},{6,7},{7,4},{8,9},{9,10},{10,1... | collective-permute-start | bytes 196616 | tf_op jit(solution)/shard_map/ppermute | solution.py:24
  94.3 6.7 %collective-permute-start.11 = (bf16[64,512]{1,0:T(8,128)(2,1)S(1)}, bf16[64,512]{1,0:T(8,128)(2,1)S(1)}, u32[]{:S(2)}, u32[]{:S(2)}) collective-permute-start(bf16[64,512]{1,0:T(8,128)(2,1)S(1)} %get-tuple-element.43), channel_id=1, source_target_pairs={{0,2},{1,3},{2,0},{3,1},{4,6},{5,7},{6,4},{7,5},{8,10},{9,11},{10,... | collective-permute-start | bytes 196616 | tf_op jit(solution)/shard_map/ppermute | solution.py:24
  98.7 4.3 %collective-permute-start.12 = (bf16[64,512]{1,0:T(8,128)(2,1)S(1)}, bf16[64,512]{1,0:T(8,128)(2,1)S(1)}, u32[]{:S(2)}, u32[]{:S(2)}) collective-permute-start(bf16[64,512]{1,0:T(8,128)(2,1)S(1)} %get-tuple-element.44), channel_id=1, source_target_pairs={{0,3},{1,0},{2,1},{3,2},{4,7},{5,4},{6,5},{7,6},{8,11},{9,8},{10,9... | collective-permute-start | bytes 196616 | tf_op jit(solution)/shard_map/ppermute | solution.py:24

commit v6 on v4

--- a/solution.py
+++ b/solution.py
@@ -120,16 +120,17 @@
     finish(out_ref, level_ref, m_ref, acc_ref)
 
 
-def guest_kernel(offsets, lengths, q_ref, k0, v0, k1, v1, *refs, back):
+def guest_kernel(offsets, lengths, q_ref, k0, v0, k1, v1, *refs, back, first):
     out_ref, m_ref, acc_ref, level_ref = refs
     core, document = lax.axis_index("core"), lax.axis_index(DOC)
+    span = slice(first, first + m_ref.shape[1])
     reset(m_ref, acc_ref)
     counts = [
         sum(jnp.where(offsets[0, i] == wanted, 1, 0) for i in range(offsets.shape[1]))
         for wanted in (back, back - 1 + 2 * core)
     ]
     live = lengths[document], lengths[document + 1 - 2 * core]
-    absorb_memories(((k0, v0), (k1, v1)), live, counts, lambda h: q_ref[:, of_head(h)], m_ref, acc_ref)
+    absorb_memories(((k0, v0), (k1, v1)), live, counts, lambda h: q_ref[span, of_head(h)], m_ref, acc_ref)
     finish(out_ref, level_ref, m_ref, acc_ref)
 
 
@@ -195,15 +196,14 @@
     return kernel_call(pass_on_kernel, (), (weights,), [(depth // 2, width)], [])[0]
 
 
-def merge_kernel(*refs):
-    *homes, far_ref, near_ref = refs[:4]
-    *tiles, share_ref, whole_ref = refs[4:]
+def merge_kernel(home0, home1, near0, near1, far_ref, *refs):
+    *tiles, share_ref, whole_ref = refs
     rows, width = whole_ref.shape
     heads, count = width // DH, len(tiles)
     half = rows // 2
-    for n, home_ref in enumerate(homes):
-        span = slice(n * half, (n + 1) * half)
-        parts = [(home_ref, slice(0, half)), (far_ref, span), (near_ref, span)]
+    for n, (home_ref, near_ref) in enumerate(((home0, near0), (home1, near1))):
+        first, span = slice(0, half), slice(n * half, (n + 1) * half)
+        parts = [(home_ref, first), (far_ref, span), (near_ref, first)]
         tails = [part[-TAIL:, where].astype(jnp.float32) for part, where in parts]
         for h in range(heads):
             levels = [tail[3 * h : 3 * h + 1] + tail[3 * h + 1 : 3 * h + 2] + tail[3 * h + 2 : 3 * h + 3] for tail in tails]
@@ -226,11 +226,11 @@
             tile[n * block : (n + 1) * block, :] = whole_ref[pl.ds(pl.multiple_of(first, block), block), :]
 
 
-def merge(home0, home1, far, near):
+def merge(homes, nears, far):
     rows, width = far.shape[0] - TAIL, far.shape[1]
     count = lax.axis_size("x")
     scratch = [pltpu.VMEM((2, DH, rows // 2), jnp.float32), pltpu.VMEM((rows, width), jnp.bfloat16)]
-    return kernel_call(merge_kernel, (), (home0, home1, far, near), [(rows // count, width)] * count, scratch)
+    return kernel_call(merge_kernel, (), (*homes, *nears, far), [(rows // count, width)] * count, scratch)
 
 
 def project_kernel(*refs, part):
@@ -289,24 +289,28 @@
 
         return attention(kernel, (offsets, mem_lengths), (*local, *memory), rows // 2, width)
 
-    def guest(load, table, back):
+    def guest(load, table, back, first, rows):
         def kernel(*refs):
-            guest_kernel(*refs, back=back)
+            guest_kernel(*refs, back=back, first=first)
 
         out = attention(kernel, (table, mem_lengths), (load, *memory), rows, width)
-        return moved(shift, out, DOC, back), out
+        return out, moved(shift, out, DOC, back)
 
     home0 = at_home(local, 0)
-    from_far, far = guest(after(query_far, home0), offsets_far, 4)
-    from_near, near = guest(after(query_near, far), offsets_near, 2)
-
-    near_weight = after(near_weight, near)
+    far, from_far = guest(after(query_far, home0), offsets_far, 4, 0, rows)
+    query_near = after(query_near, far)
+    near0, from_near0 = guest(query_near, offsets_near, 2, 0, rows // 2)
+
+    near_weight = after(near_weight, near0)
     passed_on = pass_on(near_weight)
-    home1 = at_home((after(local[0], near, passed_on), *local[1:]), 1)
     far_weight = moved(part_ways, passed_on)
+
+    near1, from_near1 = guest(after(query_near, near0, passed_on), offsets_near, 2, rows // 2, rows // 2)
+    home1 = at_home((after(local[0], near1), *local[1:]), 1)
+    near_weight = after(near_weight, near1)
     weights = [own_weight, near_weight, moved(swap, near_weight, "core"), far_weight, moved(swap, far_weight, "core")]
 
-    mine, *tiles = merge(home0, home1, from_far, from_near)
+    mine, *tiles = merge((home0, home1), (from_near0, from_near1), from_far)
     tiles = mine, *(moved(shift, tile, "x", k) for k, tile in enumerate(tiles, 1))
     given = project(tiles, weights, (), 0)
     taken = swap(given, "yh")

time: 104 us -> 103 us (level)
  waiting for transfers between devices: 46.4 us -> 34.9 us
  starting transfers between devices: 28.2 us -> 36.1 us
  Pallas kernels: 27.2 us -> 29.6 us
    ppermute x2, waiting for transfers between devices: 13.3 us -> 0.61 us  [part_ways(): return lax.ppermute(value, ('core', 'x'), up + down)]
    ppermute x5, starting transfers between devices: 13.2 us -> 21.5 us  [swap(): return lax.ppermute(value, axis, [(0, 1), (1, 0)])]
    pallas_call x8 -> x9, Pallas kernels: 24.5 us -> 27 us  [kernel_call(): pl.pallas_call(kernel, grid_spec=pltpu.PrefetchScalarGridSpec(num_scalar_...]
    ppermute x9 -> x10, waiting for transfers between devices: 29.8 us -> 31 us  [shift(): lax.ppermute(value, axis, [(i, (i + steps) % count) for i in range(count)])]
    ppermute x9 -> x10, starting transfers between devices: 11 us -> 11 us  [shift(): lax.ppermute(value, axis, [(i, (i + steps) % count) for i in range(count)])]
  transfers between devices with their start and end apart: 16 -> 17, of which waited for: 8 -> 9; matrix products, arithmetic and copies ran while one was open for 0% -> 0% of each run, Pallas kernels for 25% -> 28%
where the time goes in v6:
time: 103 us; the launch traced here: 101 us
  starting transfers between devices  36.1 us (35%)
  waiting for transfers between devices  34.9 us (34%)
  Pallas kernels  29.6 us (29%)
    ppermute x10, waiting for transfers between devices, shift(): lax.ppermute(value, axis, [(i, (i + steps) % count) for i in range(count)])  31 us
    pallas_call x9, Pallas kernels, kernel_call(): pl.pallas_call(kernel, grid_spec=pltpu.PrefetchScalarGridSpec(num_scalar_...  27 us
    ppermute x5, starting transfers between devices, swap(): return lax.ppermute(value, axis, [(0, 1), (1, 0)])  21.5 us
    ppermute x10, starting transfers between devices, shift(): lax.ppermute(value, axis, [(i, (i + steps) % count) for i in range(count)])  11 us
    ppermute x2, starting transfers between devices, part_ways(): return lax.ppermute(value, ('core', 'x'), up + down)  3.51 us
    ppermute x5, waiting for transfers between devices, swap(): return lax.ppermute(value, axis, [(0, 1), (1, 0)])  3.22 us
    pallas_call x1, Pallas kernels, load(): pl.pallas_call(load_kernel, in_specs=[pl.BlockSpec(memory_space=pltpu.HBM...  2.67 us
  transfers between devices with their start and end apart: 17, of which 9 were waited for; matrix products, arithmetic and copies ran while one was open for 0% of the time, Pallas kernels for 28%

profile of v6, /device:TPU:1, one launch (start us, length us, event | category | flops | bytes accessed | tf_op | source)
XLA Modules:
  0.0 101.4 jit_solution(12548948880134233339)
XLA Ops:
  0.0 0.0 copy-start.1
  0.0 0.0 copy-start
  0.0 3.3 %collective-permute-start.6 = (bf16[512,2048]{1,0:T(8,128)(2,1)}, bf16[512,2048]{1,0:T(8,128)(2,1)S(1)}, u32[]{:S(2)}, u32[]{:S(2)}) collective-permute-start(bf16[512,2048]{1,0:T(8,128)(2,1)} %refs_2_.1), channel_id=1, source_target_pairs={{0,1},{1,2},{2,3},{3,0},{8,11},{9,8},{10,9},{11,10},{4,5},{5,6},{6... | collective-permute-start | bytes 6291464 | tf_op jit(solution)/shard_map/ppermute | solution.py:35
  3.3 0.0 collective-permute-start
  3.3 0.5 collective-permute-start.1
  3.8 5.6 %collective-permute-start.5 = (bf16[512,512]{1,0:T(8,128)(2,1)}, bf16[512,512]{1,0:T(8,128)(2,1)S(1)}, u32[]{:S(2)}, u32[]{:S(2)}) collective-permute-start(bf16[512,512]{1,0:T(8,128)(2,1)} %refs_3_.1), channel_id=1, source_target_pairs={{0,224},{8,232},{16,240},{24,248},{32,0},{40,8},{48,16},{56,24},{6... | collective-permute-start | bytes 1572872 | tf_op jit(solution)/shard_map/ppermute | solution.py:24
  9.4 1.7 %collective-permute-start.3 = (bf16[512,512]{1,0:T(8,128)(2,1)}, bf16[512,512]{1,0:T(8,128)(2,1)S(1)}, u32[]{:S(2)}, u32[]{:S(2)}) collective-permute-start(bf16[512,512]{1,0:T(8,128)(2,1)} %refs_3_.1), channel_id=1, source_target_pairs={{0,240},{8,248},{16,0},{24,8},{32,16},{40,24},{48,32},{56,40},{64,... | collective-permute-start | bytes 1572872 | tf_op jit(solution)/shard_map/ppermute | solution.py:24
  11.1 2.7 %load.1 = (bf16[1024,512]{1,0:T(8,128)(2,1)S(1)}, bf16[1024,512]{1,0:T(8,128)(2,1)S(1)}, bf16[512,2048]{1,0:T(8,128)(2,1)S(1)}, bf16[512,512]{1,0:T(8,128)(2,1)S...) custom-call(bf16[1024,512]{1,0:T(8,128)(2,1)} %refs_0_.3, bf16[1024,512]{1,0:T(8,128)(2,1)} %refs_1_.6, ...), custom_call_target="tpu_custom_call" | custom-call | tf_op jit(solution)/shard_map/load/pallas_call | solution.py:178
  13.8 0.0 collective-permute-done.refs_7_.refs_5_
  13.8 0.0 copy-done.1
  13.8 0.2 collective-permute-start.2
  14.1 0.0 collective-permute-done.1.refs_8_.refs_6_
  14.1 0.7 collective-permute-start.4
  14.8 0.0 copy-done
  14.8 5.4 %shard_map.82.home0 = bf16[272,512]{1,0:T(8,128)(2,1)S(1)} custom-call(s32[1,4]{1,0:T(1,128)S(1)} %copy-done.1, s32[32]{0:T(128)S(1)} %copy-done, bf16[512,512]{1,0:T(8,128)(2,1)S(1)} %get-tuple-element.30.refs_2_, bf16[512,512]{1,0:T(8,128)(2,1)S(1)} %get-tuple-element.22.refs_3_, bf16[512,512]{1,0:T(8,128)(2,1)S(1)} %get-tuple-element.23.refs_4_, ...), custom_call_target="tpu_custom_call" | custom-call | tf_op jit(solution)/shard_map/pallas_call | solution.py:143
  20.3 0.7 collective-permute-done.5.refs_2_
  21.0 11.2 %collective-permute-done.4.refs_0_ = s32[1,4]{1,0:T(1,128)S(1)} collective-permute-done((s32[1,4]{1,0:T(1,128)S(1)}, s32[1,4]{1,0:T(1,128)S(1)}, u32[]{:S(2)}, u32[]{:S(2)}) %collective-permute-start.4) | collective-permute-done | bytes 48 | tf_op jit(solution)/shard_map/ppermute | solution.py:24
  32.2 1.1 %shard_map.83 = bf16[528,512]{1,0:T(8,128)(2,1)S(1)} custom-call(s32[1,4]{1,0:T(1,128)S(1)} %collective-permute-done.4.refs_0_, s32[32]{0:T(128)S(1)} %copy-done, bf16[512,512]{1,0:T(8,128)(2,1)S(1)} %collective-permute-done.5.refs_2_, bf16[1024,512]{1,0:T(8,128)(2,1)S(1)} %get-tuple-element.24.refs_5_.refs_3_, ...), custom_call_target="tpu_custom_call" | custom-call | tf_op jit(solution)/shard_map/pallas_call | solution.py:143
  33.3 0.0 collective-permute-done.3.refs_2_
  33.3 0.0 collective-permute-done.2.refs_0_
  33.3 5.1 %shard_map.84 = bf16[272,512]{1,0:T(8,128)(2,1)S(1)} custom-call(s32[1,4]{1,0:T(1,128)S(1)} %collective-permute-done.2.refs_0_, s32[32]{0:T(128)S(1)} %copy-done, bf16[512,512]{1,0:T(8,128)(2,1)S(1)} %collective-permute-done.3.refs_2_, bf16[1024,512]{1,0:T(8,128)(2,1)S(1)} %get-tuple-element.24.refs_5_.refs_3_, ...), custom_call_target="tpu_custom_call" | custom-call | tf_op jit(solution)/shard_map/pallas_call | solution.py:143
  38.4 0.0 collective-permute-done.6.weights.refs_5_
  38.4 0.1 shard_map.85
  38.5 0.2 collective-permute-start.14
  38.7 4.9 %shard_map.86 = bf16[272,512]{1,0:T(8,128)(2,1)S(1)} custom-call(s32[1,4]{1,0:T(1,128)S(1)} %collective-permute-done.2.refs_0_, s32[32]{0:T(128)S(1)} %copy-done, bf16[512,512]{1,0:T(8,128)(2,1)S(1)} %collective-permute-done.3.refs_2_, bf16[1024,512]{1,0:T(8,128)(2,1)S(1)} %get-tuple-element.24.refs_5_.refs_3_, ...), custom_call_target="tpu_custom_call" | custom-call | tf_op jit(solution)/shard_map/pallas_call | solution.py:143
  43.7 8.3 %collective-permute-start.13 = (bf16[512,2048]{1,0:T(8,128)(2,1)S(1)}, bf16[512,2048]{1,0:T(8,128)(2,1)S(1)}, u32[]{:S(2)}, u32[]{:S(2)}) collective-permute-start(bf16[512,2048]{1,0:T(8,128)(2,1)S(1)} %collective-permute-done.6.weights.refs_5_), channel_id=1, source_target_pairs={{0,8},{8,0},{1,9},{9,1},{2,10},{10,2},{3,11},{11,3},{4,12},{12,4},... | collective-permute-start | bytes 6291464 | tf_op jit(solution)/shard_map/ppermute | solution.py:28
  51.9 0.6 collective-permute-done.14.refs_7_
  52.5 9.7 %collective-permute-start.15 = (bf16[256,2048]{1,0:T(8,128)(2,1)S(1)}, bf16[256,2048]{1,0:T(8,128)(2,1)S(1)}, u32[]{:S(2)}, u32[]{:S(2)}) collective-permute-start(bf16[256,2048]{1,0:T(8,128)(2,1)S(1)} %collective-permute-done.14.refs_7_), channel_id=1, source_target_pairs={{0,8},{8,0},{1,9},{9,1},{2,10},{10,2},{3,11},{11,3},{4,12},{12,4},... | collective-permute-start | bytes 3145736 | tf_op jit(solution)/shard_map/ppermute | solution.py:28
  62.3 0.0 collective-permute-start.9
  62.3 0.0 collective-permute-start.7
  62.3 0.0 collective-permute-start.8
  62.3 6.1 %shard_map.87.home1 = bf16[272,512]{1,0:T(8,128)(2,1)S(1)} custom-call(s32[1,4]{1,0:T(1,128)S(1)} %copy-done.1, s32[32]{0:T(128)S(1)} %copy-done, bf16[512,512]{1,0:T(8,128)(2,1)S(1)} %get-tuple-element.30.refs_2_, bf16[512,512]{1,0:T(8,128)(2,1)S(1)} %get-tuple-element.22.refs_3_, bf16[512,512]{1,0:T(8,128)(2,1)S(1)} %get-tuple-element.23.refs_4_, ...), custom_call_target="tpu_custom_call" | custom-call | tf_op jit(solution)/shard_map/pallas_call | solution.py:143
  68.3 6.9 %collective-permute-done.7.near0 = bf16[272,512]{1,0:T(8,128)(2,1)S(1)} collective-permute-done((bf16[272,512]{1,0:T(8,128)(2,1)S(1)}, bf16[272,512]{1,0:T(8,128)(2,1)S(1)}, u32[]{:S(2)}, u32[]{:S(2)}) %collective-permute-start.7) | collective-permute-done | bytes 278560 | tf_op jit(solution)/shard_map/ppermute | solution.py:24
  75.2 2.1 %collective-permute-done.9.far_ref = bf16[528,512]{1,0:T(8,128)(2,1)S(1)} collective-permute-done((bf16[528,512]{1,0:T(8,128)(2,1)S(1)}, bf16[528,512]{1,0:T(8,128)(2,1)S(1)}, u32[]{:S(2)}, u32[]{:S(2)}) %collective-permute-start.9) | collective-permute-done | bytes 540704 | tf_op jit(solution)/shard_map/ppermute | solution.py:24
  77.3 3.9 %collective-permute-done.8.near1 = bf16[272,512]{1,0:T(8,128)(2,1)S(1)} collective-permute-done((bf16[272,512]{1,0:T(8,128)(2,1)S(1)}, bf16[272,512]{1,0:T(8,128)(2,1)S(1)}, u32[]{:S(2)}, u32[]{:S(2)}) %collective-permute-start.8) | collective-permute-done | bytes 278560 | tf_op jit(solution)/shard_map/ppermute | solution.py:24
  81.2 1.1 %shard_map.88 = (bf16[128,512]{1,0:T(8,128)(2,1)S(1)}, bf16[128,512]{1,0:T(8,128)(2,1)S(1)}, bf16[128,512]{1,0:T(8,128)(2,1)S(1)}, bf16[128,512]{1,0:T(8,128)(2,1)S(1)}) custom-call(bf16[272,512]{1,0:T(8,128)(2,1)S(1)} %shard_map.82.home0, bf16[272,512]{1,0:T(8,128)(2,1)S(1)} %shard_map.87.home1, bf16[272,512]{1,0:T(8,128)(2,1)S(1)} %collective-permute-done.7.near0, ...), custom_call_target="tpu_custom_call" | custom-call | tf_op jit(solution)/shard_map/pallas_call | solution.py:143
  82.3 0.1 collective-permute-start.10
  82.4 0.6 collective-permute-start.11
  83.0 2.1 %collective-permute-start.12 = (bf16[128,512]{1,0:T(8,128)(2,1)S(1)}, bf16[128,512]{1,0:T(8,128)(2,1)S(1)}, u32[]{:S(2)}, u32[]{:S(2)}) collective-permute-start(bf16[128,512]{1,0:T(8,128)(2,1)S(1)} %get-tuple-element.34), channel_id=1, source_target_pairs={{0,3},{1,0},{2,1},{3,2},{4,7},{5,4},{6,5},{7,6},{8,11},{9,8},{10,9... | collective-permute-start | bytes 393224 | tf_op jit(solution)/shard_map/ppermute | solution.py:24
  85.1 6.1 %collective-permute-done.10.refs_1_ = bf16[128,512]{1,0:T(8,128)(2,1)S(1)} collective-permute-done((bf16[128,512]{1,0:T(8,128)(2,1)S(1)}, bf16[128,512]{1,0:T(8,128)(2,1)S(1)}, u32[]{:S(2)}, u32[]{:S(2)}) %collective-permute-start.10) | collective-permute-done | bytes 131104 | tf_op jit(solution)/shard_map/ppermute | solution.py:24
  91.2 0.0 collective-permute-done.11.refs_2_
  91.2 0.1 collective-permute-done.12.refs_3_
  91.3 0.0 collective-permute-done.15.refs_8_
  91.3 0.0 collective-permute-done.13.refs_6_
  91.3 1.6 %shard_map.90 = bf16[64,2048]{1,0:T(8,128)(2,1)S(1)} custom-call(bf16[128,512]{1,0:T(8,128)(2,1)S(1)} %get-tuple-element.31.refs_0_, bf16[128,512]{1,0:T(8,128)(2,1)S(1)} %collective-permute-done.10.refs_1_, bf16[128,512]{1,0:T(8,128)(2,1)S(1)} %collective-permute-done.11.refs_2_, bf16[128,512]{1,0:T(8,128)(2,1)S(1)} %collective-permute-done.12.refs_3_, ...), custom_call_target="tpu_custom_call" | custom-call | tf_op jit(solution)/shard_map/pallas_call | solution.py:143
  92.9 3.0 %collective-permute-start.16 = (bf16[64,2048]{1,0:T(8,128)(2,1)S(1)}, bf16[64,2048]{1,0:T(8,128)(2,1)S(1)}, u32[]{:S(2)}, u32[]{:S(2)}) collective-permute-start(bf16[64,2048]{1,0:T(8,128)(2,1)S(1)} %shard_map.90), channel_id=1, source_target_pairs={{0,4},{4,0},{1,5},{5,1},{2,6},{6,2},{3,7},{7,3},{8,12},{12,8},{9,1... | collective-permute-start | bytes 786440 | tf_op jit(solution)/shard_map/ppermute | solution.py:28
  95.9 1.6 %shard_map.89 = bf16[64,2048]{1,0:T(8,128)(2,1)S(1)} custom-call(bf16[128,512]{1,0:T(8,128)(2,1)S(1)} %get-tuple-element.31.refs_0_, bf16[128,512]{1,0:T(8,128)(2,1)S(1)} %collective-permute-done.10.refs_1_, bf16[128,512]{1,0:T(8,128)(2,1)S(1)} %collective-permute-done.11.refs_2_, bf16[128,512]{1,0:T(8,128)(2,1)S(1)} %collective-permute-done.12.refs_3_, ...), custom_call_target="tpu_custom_call" | custom-call | tf_op jit(solution)/shard_map/pallas_call | solution.py:143
  97.5 3.2 %collective-permute-done.16 = bf16[64,2048]{1,0:T(8,128)(2,1)S(1)} collective-permute-done((bf16[64,2048]{1,0:T(8,128)(2,1)S(1)}, bf16[64,2048]{1,0:T(8,128)(2,1)S(1)}, u32[]{:S(2)}, u32[]{:S(2)}) %collective-permute-start.16) | collective-permute-done | bytes 262176 | tf_op jit(solution)/shard_map/ppermute | solution.py:28
  100.7 0.8 add_convert_fusion
Async XLA Ops:
  0.0 13.8 %copy-start.1 = (s32[1,4]{1,0:T(1,128)S(1)}, s32[1,4]{1,0:T(1,128)}, u32[]{:S(2)}) copy-start(s32[1,4]{1,0:T(1,128)} %refs_0_.5) | copy-start | bytes 52
  0.0 14.8 %copy-start = (s32[32]{0:T(128)S(1)}, s32[32]{0:T(128)}, u32[]{:S(2)}) copy-start(s32[32]{0:T(128)} %refs_1_.11) | copy-start | bytes 388
  0.0 38.4 %collective-permute-start.6 = (bf16[512,2048]{1,0:T(8,128)(2,1)}, bf16[512,2048]{1,0:T(8,128)(2,1)S(1)}, u32[]{:S(2)}, u32[]{:S(2)}) collective-permute-start(bf16[512,2048]{1,0:T(8,128)(2,1)} %refs_2_.1), channel_id=1, source_target_pairs={{0,1},{1,2},{2,3},{3,0},{8,11},{9,8},{10,9},{11,10},{4,5},{5,6},{6... | collective-permute-start | bytes 6291464 | tf_op jit(solution)/shard_map/ppermute | solution.py:35
  3.3 10.5 %collective-permute-start = (bf16[1024,512]{1,0:T(8,128)(2,1)}, bf16[1024,512]{1,0:T(8,128)(2,1)S(1)}, u32[]{:S(2)}, u32[]{:S(2)}) collective-permute-start(bf16[1024,512]{1,0:T(8,128)(2,1)} %refs_0_.3), channel_id=1, source_target_pairs={{0,8},{8,0},{1,9},{9,1},{2,10},{10,2},{3,11},{11,3},{4,12},{12,4},... | collective-permute-start | bytes 3145736 | tf_op jit(solution)/shard_map/ppermute | solution.py:28
  3.3 10.8 %collective-permute-start.1 = (bf16[1024,512]{1,0:T(8,128)(2,1)}, bf16[1024,512]{1,0:T(8,128)(2,1)S(1)}, u32[]{:S(2)}, u32[]{:S(2)}) collective-permute-start(bf16[1024,512]{1,0:T(8,128)(2,1)} %refs_1_.6), channel_id=1, source_target_pairs={{0,8},{8,0},{1,9},{9,1},{2,10},{10,2},{3,11},{11,3},{4,12},{12,4},... | collective-permute-start | bytes 3145736 | tf_op jit(solution)/shard_map/ppermute | solution.py:28
  3.8 17.2 %collective-permute-start.5 = (bf16[512,512]{1,0:T(8,128)(2,1)}, bf16[512,512]{1,0:T(8,128)(2,1)S(1)}, u32[]{:S(2)}, u32[]{:S(2)}) collective-permute-start(bf16[512,512]{1,0:T(8,128)(2,1)} %refs_3_.1), channel_id=1, source_target_pairs={{0,224},{8,232},{16,240},{24,248},{32,0},{40,8},{48,16},{56,24},{6... | collective-permute-start | bytes 1572872 | tf_op jit(solution)/shard_map/ppermute | solution.py:24
  9.4 23.9 %collective-permute-start.3 = (bf16[512,512]{1,0:T(8,128)(2,1)}, bf16[512,512]{1,0:T(8,128)(2,1)S(1)}, u32[]{:S(2)}, u32[]{:S(2)}) collective-permute-start(bf16[512,512]{1,0:T(8,128)(2,1)} %refs_3_.1), channel_id=1, source_target_pairs={{0,240},{8,248},{16,0},{24,8},{32,16},{40,24},{48,32},{56,40},{64,... | collective-permute-start | bytes 1572872 | tf_op jit(solution)/shard_map/ppermute | solution.py:24
  13.8 19.5 %collective-permute-start.2 = (s32[1,4]{1,0:T(1,128)S(1)}, s32[1,4]{1,0:T(1,128)S(1)}, u32[]{:S(2)}, u32[]{:S(2)}) collective-permute-start(s32[1,4]{1,0:T(1,128)S(1)} %copy-done.1), channel_id=1, source_target_pairs={{0,240},{8,248},{16,0},{24,8},{32,16},{40,24},{48,32},{56,40},{64,... | collective-permute-start | bytes 56 | tf_op jit(solution)/shard_map/ppermute | solution.py:24
  14.1 18.1 %collective-permute-start.4 = (s32[1,4]{1,0:T(1,128)S(1)}, s32[1,4]{1,0:T(1,128)S(1)}, u32[]{:S(2)}, u32[]{:S(2)}) collective-permute-start(s32[1,4]{1,0:T(1,128)S(1)} %copy-done.1), channel_id=1, source_target_pairs={{0,224},{8,232},{16,240},{24,248},{32,0},{40,8},{48,16},{56,24},{6... | collective-permute-start | bytes 56 | tf_op jit(solution)/shard_map/ppermute | solution.py:24
  38.5 14.0 %collective-permute-start.14 = (bf16[256,2048]{1,0:T(8,128)(2,1)S(1)}, bf16[256,2048]{1,0:T(8,128)(2,1)S(1)}, u32[]{:S(2)}, u32[]{:S(2)}) collective-permute-start(bf16[256,2048]{1,0:T(8,128)(2,1)S(1)} %shard_map.85), channel_id=1, source_target_pairs={{0,1},{1,2},{2,3},{3,0},{8,11},{9,8},{10,9},{11,10},{4,5},{5,6},{6... | collective-permute-start | bytes 3145736 | tf_op jit(solution)/shard_map/ppermute | solution.py:35
  43.7 47.7 %collective-permute-start.13 = (bf16[512,2048]{1,0:T(8,128)(2,1)S(1)}, bf16[512,2048]{1,0:T(8,128)(2,1)S(1)}, u32[]{:S(2)}, u32[]{:S(2)}) collective-permute-start(bf16[512,2048]{1,0:T(8,128)(2,1)S(1)} %collective-permute-done.6.weights.refs_5_), channel_id=1, source_target_pairs={{0,8},{8,0},{1,9},{9,1},{2,10},{10,2},{3,11},{11,3},{4,12},{12,4},... | collective-permute-start | bytes 6291464 | tf_op jit(solution)/shard_map/ppermute | solution.py:28
  52.5 38.8 %collective-permute-start.15 = (bf16[256,2048]{1,0:T(8,128)(2,1)S(1)}, bf16[256,2048]{1,0:T(8,128)(2,1)S(1)}, u32[]{:S(2)}, u32[]{:S(2)}) collective-permute-start(bf16[256,2048]{1,0:T(8,128)(2,1)S(1)} %collective-permute-done.14.refs_7_), channel_id=1, source_target_pairs={{0,8},{8,0},{1,9},{9,1},{2,10},{10,2},{3,11},{11,3},{4,12},{12,4},... | collective-permute-start | bytes 3145736 | tf_op jit(solution)/shard_map/ppermute | solution.py:28
  62.3 15.0 %collective-permute-start.9 = (bf16[528,512]{1,0:T(8,128)(2,1)S(1)}, bf16[528,512]{1,0:T(8,128)(2,1)S(1)}, u32[]{:S(2)}, u32[]{:S(2)}) collective-permute-start(bf16[528,512]{1,0:T(8,128)(2,1)S(1)} %shard_map.83), channel_id=1, source_target_pairs={{0,32},{8,40},{16,48},{24,56},{32,64},{40,72},{48,80},{56,88},{64,... | collective-permute-start | bytes 1622024 | tf_op jit(solution)/shard_map/ppermute | solution.py:24
  62.3 13.0 %collective-permute-start.7 = (bf16[272,512]{1,0:T(8,128)(2,1)S(1)}, bf16[272,512]{1,0:T(8,128)(2,1)S(1)}, u32[]{:S(2)}, u32[]{:S(2)}) collective-permute-start(bf16[272,512]{1,0:T(8,128)(2,1)S(1)} %shard_map.84), channel_id=1, source_target_pairs={{0,16},{8,24},{16,32},{24,40},{32,48},{40,56},{48,64},{56,72},{64,... | collective-permute-start | bytes 835592 | tf_op jit(solution)/shard_map/ppermute | solution.py:24
  62.3 18.9 %collective-permute-start.8 = (bf16[272,512]{1,0:T(8,128)(2,1)S(1)}, bf16[272,512]{1,0:T(8,128)(2,1)S(1)}, u32[]{:S(2)}, u32[]{:S(2)}) collective-permute-start(bf16[272,512]{1,0:T(8,128)(2,1)S(1)} %shard_map.86), channel_id=1, source_target_pairs={{0,16},{8,24},{16,32},{24,40},{32,48},{40,56},{48,64},{56,72},{64,... | collective-permute-start | bytes 835592 | tf_op jit(solution)/shard_map/ppermute | solution.py:24
  82.3 8.9 %collective-permute-start.10 = (bf16[128,512]{1,0:T(8,128)(2,1)S(1)}, bf16[128,512]{1,0:T(8,128)(2,1)S(1)}, u32[]{:S(2)}, u32[]{:S(2)}) collective-permute-start(bf16[128,512]{1,0:T(8,128)(2,1)S(1)} %get-tuple-element.32), channel_id=1, source_target_pairs={{0,1},{1,2},{2,3},{3,0},{4,5},{5,6},{6,7},{7,4},{8,9},{9,10},{10,1... | collective-permute-start | bytes 393224 | tf_op jit(solution)/shard_map/ppermute | solution.py:24
  82.4 8.8 %collective-permute-start.11 = (bf16[128,512]{1,0:T(8,128)(2,1)S(1)}, bf16[128,512]{1,0:T(8,128)(2,1)S(1)}, u32[]{:S(2)}, u32[]{:S(2)}) collective-permute-start(bf16[128,512]{1,0:T(8,128)(2,1)S(1)} %get-tuple-element.33), channel_id=1, source_target_pairs={{0,2},{1,3},{2,0},{3,1},{4,6},{5,7},{6,4},{7,5},{8,10},{9,11},{10,... | collective-permute-start | bytes 393224 | tf_op jit(solution)/shard_map/ppermute | solution.py:24
  83.0 8.3 %collective-permute-start.12 = (bf16[128,512]{1,0:T(8,128)(2,1)S(1)}, bf16[128,512]{1,0:T(8,128)(2,1)S(1)}, u32[]{:S(2)}, u32[]{:S(2)}) collective-permute-start(bf16[128,512]{1,0:T(8,128)(2,1)S(1)} %get-tuple-element.34), channel_id=1, source_target_pairs={{0,3},{1,0},{2,1},{3,2},{4,7},{5,4},{6,5},{7,6},{8,11},{9,8},{10,9... | collective-permute-start | bytes 393224 | tf_op jit(solution)/shard_map/ppermute | solution.py:24
  92.9 7.8 %collective-permute-start.16 = (bf16[64,2048]{1,0:T(8,128)(2,1)S(1)}, bf16[64,2048]{1,0:T(8,128)(2,1)S(1)}, u32[]{:S(2)}, u32[]{:S(2)}) collective-permute-start(bf16[64,2048]{1,0:T(8,128)(2,1)S(1)} %shard_map.90), channel_id=1, source_target_pairs={{0,4},{4,0},{1,5},{5,1},{2,6},{6,2},{3,7},{7,3},{8,12},{12,8},{9,1... | collective-permute-start | bytes 786440 | tf_op jit(solution)/shard_map/ppermute | solution.py:28

commit v7 on v5

--- a/solution.py
+++ b/solution.py
@@ -22,6 +22,16 @@
 def shift(value, axis, steps):
     count = lax.axis_size(axis)
     return lax.ppermute(value, axis, [(i, (i + steps) % count) for i in range(count)])
+
+
+def return_tile(value, steps, along):
+    documents, count = lax.axis_size(DOC), lax.axis_size("x")
+    pairs = [
+        (d * count + x, (d + steps) % documents * count + (x + along) % count)
+        for d in range(documents)
+        for x in range(count)
+    ]
+    return lax.ppermute(value, (*DOC, "x"), pairs)
 
 
 def swap(value, axis):
@@ -104,42 +114,50 @@
         out_ref[rows:, :] = level_ref[...].astype(jnp.bfloat16)
 
 
-def halves(ref, h):
-    rows, yh = ref.shape[0] // 2, lax.axis_index("yh")
-    return [ref[pl.ds(pl.multiple_of(half * rows, rows), rows), of_head(h)] for half in (1 - yh, yh)]
-
-
-def home_kernel(offsets, lengths, q_ref, lk_ref, lv_ref, k0, v0, k1, v1, *refs, half):
-    *out_refs, m_ref, acc_ref, level_ref = refs
+def tile_order(tiles, rows):
+    count, yh = lax.axis_size("x"), lax.axis_index("yh")
+    block = rows // (2 * count)
+    return block, [half * (count * block) + (lax.axis_index("x") + k) % count * block for k in tiles for half in (1 - yh, yh)]
+
+
+def gather(q_ref, into_ref, block, firsts):
+    for n, first in enumerate(firsts):
+        into_ref[n * block : (n + 1) * block, :] = q_ref[pl.ds(pl.multiple_of(first, block), block), :]
+
+
+def home_kernel(offsets, lengths, q_ref, lk_ref, lv_ref, k0, v0, k1, v1, *refs, tiles):
+    out_ref, m_ref, acc_ref, level_ref, rows_ref = refs
     core, document = lax.axis_index("core"), lax.axis_index(DOC)
-    heads, rows = m_ref.shape[:2]
-    keys, yh = lk_ref.shape[0], lax.axis_index("yh")
-    first = (yh if half else 1 - yh) * rows
+    heads, keys = m_ref.shape[0], lk_ref.shape[0]
     count = sum(jnp.where((offsets[0, i] == 1) & (core == 1), 1, 0) for i in range(offsets.shape[1]))
     reset(m_ref, acc_ref)
+    block, firsts = tile_order(tiles, q_ref.shape[0])
+    gather(q_ref, rows_ref, block, firsts)
 
     def queries(h):
-        return halves(q_ref, h)[half]
-
-    seen = lax.broadcasted_iota(jnp.int32, (rows, keys), 0) + first >= lax.broadcasted_iota(jnp.int32, (rows, keys), 1)
+        return rows_ref[:, of_head(h)]
+
+    row = jnp.concatenate([lax.broadcasted_iota(jnp.int32, (block, keys), 0) + first for first in firsts], axis=0)
+    seen = row >= lax.broadcasted_iota(jnp.int32, row.shape, 1)
     for h in range(heads):
         s = jnp.where(seen, scores_of(queries(h), lk_ref[:, of_head(h)]), NEG)
         absorb(h, s, lv_ref[:, of_head(h)], m_ref, acc_ref)
     live = lengths[document], lengths[document + 1 - 2 * core]
     absorb_memories(((k0, v0), (k1, v1)), live, (jnp.int32(1), count), queries, m_ref, acc_ref)
-    finish(out_refs, level_ref, m_ref, acc_ref)
+    finish([out_ref], level_ref, m_ref, acc_ref)
 
 
 def guest_kernel(offsets, lengths, q_ref, k0, v0, k1, v1, *refs, back):
-    *out_refs, m_ref, acc_ref, level_ref = refs
+    *out_refs, m_ref, acc_ref, level_ref, rows_ref = refs
     core, document = lax.axis_index("core"), lax.axis_index(DOC)
     reset(m_ref, acc_ref)
+    gather(q_ref, rows_ref, *tile_order(range(lax.axis_size("x")), q_ref.shape[0]))
     counts = [
         sum(jnp.where(offsets[0, i] == wanted, 1, 0) for i in range(offsets.shape[1]))
         for wanted in (back, back - 1 + 2 * core)
     ]
     live = lengths[document], lengths[document + 1 - 2 * core]
-    absorb_memories(((k0, v0), (k1, v1)), live, counts, lambda h: jnp.concatenate(halves(q_ref, h), axis=0), m_ref, acc_ref)
+    absorb_memories(((k0, v0), (k1, v1)), live, counts, lambda h: rows_ref[:, of_head(h)], m_ref, acc_ref)
     finish(out_refs, level_ref, m_ref, acc_ref)
 
 
@@ -169,6 +187,7 @@
         pltpu.VMEM((heads, rows, DH), jnp.float32),
         pltpu.VMEM((heads, rows, 2 * DH), jnp.float32),
         pltpu.VMEM((TAIL, width), jnp.float32),
+        pltpu.VMEM((rows, width), jnp.bfloat16),
     ]
     return kernel_call(kernel, scalars, arrays, [(rows // parts + TAIL, width)] * parts, scratch)
 
@@ -205,60 +224,86 @@
     return kernel_call(pass_on_kernel, (), (weights,), [(depth // 2, width)], [])[0]
 
 
-def merge_kernel(home_ref, near_ref, far_ref, *refs, half):
-    *tiles, share_ref, whole_ref = refs
-    rows, width = whole_ref.shape
-    heads, count = width // DH, len(tiles)
-    first = slice(0, rows)
-    parts = [(home_ref, first), (far_ref, slice(half * rows, (half + 1) * rows)), (near_ref, first)]
-    tails = [part[-TAIL:, where].astype(jnp.float32) for part, where in parts]
+def levels_of(part, where):
+    terms = part[-TAIL:, where].astype(jnp.float32)
+    return [terms[3 * h : 3 * h + 1] + terms[3 * h + 1 : 3 * h + 2] + terms[3 * h + 2 : 3 * h + 3] for h in range(TAIL // 3)]
+
+
+def merged(parts, heads, share_ref):
+    levels = [levels_of(part, where) for part, where in parts]
+    joint = []
     for h in range(heads):
-        levels = [tail[3 * h : 3 * h + 1] + tail[3 * h + 1 : 3 * h + 2] + tail[3 * h + 2 : 3 * h + 3] for tail in tails]
-        top = jnp.maximum(jnp.maximum(levels[0], levels[1]), levels[2])
-        shares = [jnp.exp2(level - top) for level in levels]
-        total = shares[0] + shares[1] + shares[2]
+        a, b = levels[0][h], levels[1][h]
+        top = jnp.maximum(a, b)
+        shares = jnp.exp2(a - top), jnp.exp2(b - top)
+        total = shares[0] + shares[1]
+        joint.append(top + jnp.log2(total))
         for i, share in enumerate(shares):
-            share_ref[3 * h + i : 3 * h + i + 1, :] = share / total
+            share_ref[2 * h + i : 2 * h + i + 1, :] = share / total
     columns = share_ref[...].T
-    for h in range(heads):
-        mixed = 0.0
-        for i, (part, where) in enumerate(parts):
-            mixed = mixed + columns[:, 3 * h + i : 3 * h + i + 1] * part[where, of_head(h)].astype(jnp.float32)
-        whole_ref[:, of_head(h)] = mixed.astype(whole_ref.dtype)
-    block, x = rows // count, lax.axis_index("x")
+    rows = [
+        sum(columns[:, 2 * h + i : 2 * h + i + 1] * part[where, of_head(h)].astype(jnp.float32) for i, (part, where) in enumerate(parts))
+        for h in range(heads)
+    ]
+    return rows, joint
+
+
+def premerge_kernel(home0, home1, far_ref, *refs):
+    *tiles, share_ref, level_ref = refs
+    heads = far_ref.shape[1] // DH
     for k, tile in enumerate(tiles):
-        tile[...] = whole_ref[pl.ds(pl.multiple_of((x + k) % count * block, block), block), :]
-
-
-def merge(home, near, far, half):
-    def kernel(*refs):
-        merge_kernel(*refs, half=half)
-
-    rows, width = home.shape[0] - TAIL, home.shape[1]
+        rows = tile.shape[0] - TAIL
+        home = (home0, home1)[k // 2]
+        parts = [(home, pl.ds(k % 2 * rows, rows)), (far_ref, pl.ds(k * rows, rows))]
+        merged_rows, joint = merged(parts, heads, share_ref)
+        level_ref[...] = jnp.zeros(level_ref.shape, jnp.float32)
+        for h in range(heads):
+            tile[:rows, of_head(h)] = merged_rows[h].astype(jnp.bfloat16)
+            rest = joint[h]
+            for i in range(3):
+                term = rest.astype(jnp.bfloat16).astype(jnp.float32)
+                level_ref[3 * h + i : 3 * h + i + 1, :rows] = term
+                rest = rest - term
+        tile[rows:, :] = level_ref[...].astype(jnp.bfloat16)
+
+
+def premerge(home0, home1, far):
+    width = far.shape[1]
     count = lax.axis_size("x")
-    scratch = [pltpu.VMEM((DH, rows), jnp.float32), pltpu.VMEM((rows, width), jnp.bfloat16)]
-    return kernel_call(kernel, (), (home, near, far), [(rows // count, width)] * count, scratch)
-
-
-def project_kernel(*refs):
-    mine, below, opposite, above, own, near, near_other, far, far_other, out_ref = refs
-    half = far.shape[0]
-    core = lax.axis_index("core")
-
+    rows = (far.shape[0] - TAIL) // count
+    scratch = [pltpu.VMEM((DH, rows), jnp.float32), pltpu.VMEM((TAIL, width), jnp.float32)]
+    return kernel_call(premerge_kernel, (), (home0, home1, far), [(rows + TAIL, width)] * count, scratch)
+
+
+def project_kernel(*refs, part):
+    own, near, near_other, far, far_other, out_ref, share_ref, row_ref = refs[8:]
+    tiles = list(zip(refs[:4], refs[4:8]))
+    half, core, heads = far.shape[0], lax.axis_index("core"), own.shape[0] // DH
+    rows = out_ref.shape[0]
+    for n, pair in enumerate(tiles):
+        mixed, _ = merged([(ref, pl.ds(0, 2 * rows)) for ref in pair], heads, share_ref)
+        for h in range(heads):
+            row_ref[n, :, of_head(h)] = mixed[h][part * rows : (part + 1) * rows].astype(jnp.bfloat16)
+    below, above = row_ref[1], row_ref[3]
     pairs = [
-        (mine[...], own),
-        (jnp.where(core == 0, below[...], above[...]), near),
-        (jnp.where(core == 0, above[...], below[...]), near_other),
-        (jnp.where(core == 0, opposite[:, :half], opposite[:, half:]), far),
-        (jnp.where(core == 0, opposite[:, half:], opposite[:, :half]), far_other),
+        (row_ref[0], own),
+        (jnp.where(core == 0, below, above), near),
+        (jnp.where(core == 0, above, below), near_other),
+        (jnp.where(core == 0, row_ref[2, :, :half], row_ref[2, :, half:]), far),
+        (jnp.where(core == 0, row_ref[2, :, half:], row_ref[2, :, :half]), far_other),
     ]
     acc = sum(jnp.dot(a, w[...], preferred_element_type=jnp.float32) for a, w in pairs)
     out_ref[...] = acc.astype(out_ref.dtype)
 
 
-def project(tiles, weights):
-    out = (tiles[0].shape[0], weights[0].shape[1])
-    return kernel_call(project_kernel, (), (*tiles, *weights), [out], [])[0]
+def project(tiles, nears, weights, part):
+    def kernel(*refs):
+        project_kernel(*refs, part=part)
+
+    depth, width = weights[0].shape
+    rows = (tiles[0].shape[0] - TAIL) // 2
+    scratch = [pltpu.VMEM((DH, 2 * rows), jnp.float32), pltpu.VMEM((len(tiles), rows, depth), jnp.bfloat16)]
+    return kernel_call(kernel, (), (*tiles, *nears, *weights), [(rows, width)], scratch)[0]
 
 
 def after(value, *others):
@@ -282,39 +327,37 @@
     own_keys, own_values, own_weight, *local = load(mem_keys, mem_values, out_weight, queries, local_keys, local_values)
     memory = (own_keys, own_values, other_keys, other_values)
 
+    count = lax.axis_size("x")
+
     def at_home(local, half):
         def kernel(*refs):
-            home_kernel(*refs, half=half)
+            home_kernel(*refs, tiles=range(half * count // 2, (half + 1) * count // 2))
 
         return attention(kernel, (offsets, mem_lengths), (*local, *memory), rows // 2, width)[0]
 
-    def guest(load, table, back, parts=1):
+    def guest(load, table, back, parts):
         def kernel(*refs):
             guest_kernel(*refs, back=back)
 
         return attention(kernel, (table, mem_lengths), (load, *memory), rows, width, parts)
 
     home0 = at_home(local, 0)
-    (far,) = guest(after(query_far, home0), offsets_far, 4)
+    (far,) = guest(after(query_far, home0), offsets_far, 4, 1)
     from_far = moved(shift, far, DOC, 4)
-    near = guest(after(query_near, far), offsets_near, 2, 2)
-    from_near = [moved(shift, out, DOC, 2) for out in near]
-
-    near_weight = after(near_weight, *near)
+
+    near_weight = after(near_weight, far)
     passed_on = pass_on(near_weight)
-    home1 = at_home((after(local[0], *near, passed_on), *local[1:]), 1)
     far_weight = moved(part_ways, passed_on)
     weights = [own_weight, near_weight, moved(swap, near_weight, "core"), far_weight, moved(swap, far_weight, "core")]
 
-    def tiles_of(home, near, half):
-        mine, *tiles = merge(home, near, from_far, half)
-        return mine, *(moved(shift, tile, "x", k) for k, tile in enumerate(tiles, 1))
-
-    given = tiles_of(after(home0, home1), from_near[0], 0)
-    kept = tiles_of(home1, after(from_near[1], given[0]), 1)
-    given = project(given, weights)
+    near = guest(after(query_near, far, passed_on), offsets_near, 2, count)
+    nears = [moved(return_tile, tile, 2, k) for k, tile in enumerate(near)]
+    home1 = at_home((after(local[0], *near), *local[1:]), 1)
+    mine, *tiles = premerge(home0, home1, from_far)
+    tiles = mine, *(moved(shift, tile, "x", k) for k, tile in enumerate(tiles, 1))
+    given = project(tiles, nears, weights, 0)
     taken = swap(given, "yh")
-    kept = project(kept, weights)
+    kept = project(tiles, nears, weights, 1)
     return (kept.astype(jnp.float32) + taken.astype(jnp.float32)).astype(jnp.bfloat16)
 
 

time: 105 us -> 115 us (1.095)
  the two profiles are of different devices: /device:TPU:2 before, /device:TPU:1 now
where the time goes in v7:
time: 115 us
  waiting for transfers between devices  55.5 us (48%)
  starting transfers between devices  30.1 us (26%)
  Pallas kernels  28.2 us (25%)
    pallas_call x8, Pallas kernels, kernel_call(): pl.pallas_call(kernel, grid_spec=pltpu.PrefetchScalarGridSpec(num_scalar_...  25.5 us
    ppermute x8, waiting for transfers between devices, shift(): lax.ppermute(value, axis, [(i, (i + steps) % count) for i in range(count)])  20.8 us
    ppermute x2, waiting for transfers between devices, part_ways(): return lax.ppermute(value, ('core', 'x'), up + down)  15.1 us
    ppermute x4, waiting for transfers between devices, return_tile(): return lax.ppermute(value, (*DOC, 'x'), pairs)  14.7 us
    ppermute x8, starting transfers between devices, shift(): lax.ppermute(value, axis, [(i, (i + steps) % count) for i in range(count)])  14.1 us
    ppermute x5, starting transfers between devices, swap(): return lax.ppermute(value, axis, [(0, 1), (1, 0)])  8.01 us
    ppermute x2, starting transfers between devices, part_ways(): return lax.ppermute(value, ('core', 'x'), up + down)  6.38 us
    ppermute x5, waiting for transfers between devices, swap(): return lax.ppermute(value, axis, [(0, 1), (1, 0)])  4.89 us
  transfers between devices with their start and end apart: 19, of which 10 were waited for; matrix products, arithmetic and copies ran while one was open for 0% of the time, Pallas kernels for 23%

profile of v7, /device:TPU:1, one launch (start us, length us, event | category | flops | bytes accessed | tf_op | source)
XLA Modules:
  0.0 114.7 jit_solution(15386801697924337808)
XLA Ops:
  0.0 0.0 copy-start.1
  0.0 0.0 copy-start
  0.0 3.3 %collective-permute-start.6 = (bf16[512,2048]{1,0:T(8,128)(2,1)}, bf16[512,2048]{1,0:T(8,128)(2,1)S(1)}, u32[]{:S(2)}, u32[]{:S(2)}) collective-permute-start(bf16[512,2048]{1,0:T(8,128)(2,1)} %refs_2_.1), channel_id=1, source_target_pairs={{0,1},{1,2},{2,3},{3,0},{8,11},{9,8},{10,9},{11,10},{4,5},{5,6},{6... | collective-permute-start | bytes 6291464 | tf_op jit(solution)/shard_map/ppermute | solution.py:45
  3.3 0.0 collective-permute-start
  3.3 0.5 collective-permute-start.1
  3.8 5.6 %collective-permute-start.5 = (bf16[512,512]{1,0:T(8,128)(2,1)}, bf16[512,512]{1,0:T(8,128)(2,1)S(1)}, u32[]{:S(2)}, u32[]{:S(2)}) collective-permute-start(bf16[512,512]{1,0:T(8,128)(2,1)} %refs_3_.1), channel_id=1, source_target_pairs={{0,224},{8,232},{16,240},{24,248},{32,0},{40,8},{48,16},{56,24},{6... | collective-permute-start | bytes 1572872 | tf_op jit(solution)/shard_map/ppermute | solution.py:24
  9.4 0.7 collective-permute-start.4
  10.1 2.7 %load.1 = (bf16[1024,512]{1,0:T(8,128)(2,1)S(1)}, bf16[1024,512]{1,0:T(8,128)(2,1)S(1)}, bf16[512,2048]{1,0:T(8,128)(2,1)S(1)}, bf16[512,512]{1,0:T(8,128)(2,1)S...) custom-call(bf16[1024,512]{1,0:T(8,128)(2,1)} %refs_0_.3, bf16[1024,512]{1,0:T(8,128)(2,1)} %refs_1_.5, ...), custom_call_target="tpu_custom_call" | custom-call | tf_op jit(solution)/shard_map/load/pallas_call | solution.py:206
  12.8 0.0 collective-permute-done.refs_7_.refs_5_
  12.8 0.0 collective-permute-done.1.refs_8_.refs_6_
  12.8 0.0 copy-done.1
  12.8 0.0 copy-done
  12.8 5.9 %shard_map.82.home0 = bf16[272,512]{1,0:T(8,128)(2,1)S(1)} custom-call(s32[1,4]{1,0:T(1,128)S(1)} %copy-done.1, s32[32]{0:T(128)S(1)} %copy-done, bf16[512,512]{1,0:T(8,128)(2,1)S(1)} %get-tuple-element.35.refs_2_, bf16[512,512]{1,0:T(8,128)(2,1)S(1)} %get-tuple-element.24.refs_3_, bf16[512,512]{1,0:T(8,128)(2,1)S(1)} %get-tuple-element.25.refs_4_, ...), custom_call_target="tpu_custom_call" | custom-call | tf_op jit(solution)/shard_map/pallas_call | solution.py:170
  18.8 2.2 %collective-permute-done.5.refs_2_ = bf16[512,512]{1,0:T(8,128)(2,1)S(1)} collective-permute-done((bf16[512,512]{1,0:T(8,128)(2,1)}, bf16[512,512]{1,0:T(8,128)(2,1)S(1)}, u32[]{:S(2)}, u32[]{:S(2)}) %collective-permute-start.5) | collective-permute-done | bytes 524320 | tf_op jit(solution)/shard_map/ppermute | solution.py:24
  21.0 0.0 collective-permute-done.4.refs_0_
  21.0 1.1 shard_map.83
  22.1 0.0 copy-start.2
  22.1 4.5 %collective-permute-done.6.weights.refs_9_ = bf16[512,2048]{1,0:T(8,128)(2,1)S(1)} collective-permute-done((bf16[512,2048]{1,0:T(8,128)(2,1)}, bf16[512,2048]{1,0:T(8,128)(2,1)S(1)}, u32[]{:S(2)}, u32[]{:S(2)}) %collective-permute-start.6) | collective-permute-done | bytes 2097184 | tf_op jit(solution)/shard_map/ppermute | solution.py:45
  26.6 0.1 shard_map.84
  26.7 3.1 %collective-permute-start.16 = (bf16[256,2048]{1,0:T(8,128)(2,1)S(1)}, bf16[256,2048]{1,0:T(8,128)(2,1)S(1)}, u32[]{:S(2)}, u32[]{:S(2)}) collective-permute-start(bf16[256,2048]{1,0:T(8,128)(2,1)S(1)} %shard_map.84), channel_id=1, source_target_pairs={{0,1},{1,2},{2,3},{3,0},{8,11},{9,8},{10,9},{11,10},{4,5},{5,6},{6... | collective-permute-start | bytes 3145736 | tf_op jit(solution)/shard_map/ppermute | solution.py:45
  29.8 1.2 %collective-permute-start.15 = (bf16[512,2048]{1,0:T(8,128)(2,1)S(1)}, bf16[512,2048]{1,0:T(8,128)(2,1)S(1)}, u32[]{:S(2)}, u32[]{:S(2)}) collective-permute-start(bf16[512,2048]{1,0:T(8,128)(2,1)S(1)} %collective-permute-done.6.weights.refs_9_), channel_id=1, source_target_pairs={{0,8},{8,0},{1,9},{9,1},{2,10},{10,2},{3,11},{11,3},{4,12},{12,4},... | collective-permute-start | bytes 6291464 | tf_op jit(solution)/shard_map/ppermute | solution.py:38
  30.9 10.6 %collective-permute-done.16.refs_11_ = bf16[256,2048]{1,0:T(8,128)(2,1)S(1)} collective-permute-done((bf16[256,2048]{1,0:T(8,128)(2,1)S(1)}, bf16[256,2048]{1,0:T(8,128)(2,1)S(1)}, u32[]{:S(2)}, u32[]{:S(2)}) %collective-permute-start.16) | collective-permute-done | bytes 1048608 | tf_op jit(solution)/shard_map/ppermute | solution.py:45
  41.5 5.3 %collective-permute-start.17 = (bf16[256,2048]{1,0:T(8,128)(2,1)S(1)}, bf16[256,2048]{1,0:T(8,128)(2,1)S(1)}, u32[]{:S(2)}, u32[]{:S(2)}) collective-permute-start(bf16[256,2048]{1,0:T(8,128)(2,1)S(1)} %collective-permute-done.16.refs_11_), channel_id=1, source_target_pairs={{0,8},{8,0},{1,9},{9,1},{2,10},{10,2},{3,11},{11,3},{4,12},{12,4},... | collective-permute-start | bytes 3145736 | tf_op jit(solution)/shard_map/ppermute | solution.py:38
  46.8 0.0 collective-permute-start.7
  46.8 0.0 copy-done.2
  46.8 4.9 %collective-permute-start.3 = (bf16[512,512]{1,0:T(8,128)(2,1)S(1)}, bf16[512,512]{1,0:T(8,128)(2,1)S(1)}, u32[]{:S(2)}, u32[]{:S(2)}) collective-permute-start(bf16[512,512]{1,0:T(8,128)(2,1)S(1)} %copy-done.2), channel_id=1, source_target_pairs={{0,240},{8,248},{16,0},{24,8},{32,16},{40,24},{48,32},{56,40},{64,... | collective-permute-start | bytes 1572872 | tf_op jit(solution)/shard_map/ppermute | solution.py:24
  51.7 0.2 collective-permute-start.2
  51.9 11.0 %collective-permute-done.3.refs_2_ = bf16[512,512]{1,0:T(8,128)(2,1)S(1)} collective-permute-done((bf16[512,512]{1,0:T(8,128)(2,1)S(1)}, bf16[512,512]{1,0:T(8,128)(2,1)S(1)}, u32[]{:S(2)}, u32[]{:S(2)}) %collective-permute-start.3) | collective-permute-done | bytes 524320 | tf_op jit(solution)/shard_map/ppermute | solution.py:24
  62.9 0.0 collective-permute-done.2.refs_0_
  63.0 7.7 %shard_map.85 = (bf16[144,512]{1,0:T(8,128)(2,1)S(1)}, bf16[144,512]{1,0:T(8,128)(2,1)S(1)}, bf16[144,512]{1,0:T(8,128)(2,1)S(1)}, bf16[144,512]{1,0:T(8,128)(2,1)S(1)}) custom-call(s32[1,4]{1,0:T(1,128)S(1)} %collective-permute-done.2.refs_0_, s32[32]{0:T(128)S(1)} %copy-done, bf16[512,512]{1,0:T(8,128)(2,1)S(1)} %collective-permute-done.3.refs_2_, ...), custom_call_target="tpu_custom_call" | custom-call | tf_op jit(solution)/shard_map/pallas_call | solution.py:170
  70.7 5.9 %shard_map.86.home1 = bf16[272,512]{1,0:T(8,128)(2,1)S(1)} custom-call(s32[1,4]{1,0:T(1,128)S(1)} %copy-done.1, s32[32]{0:T(128)S(1)} %copy-done, bf16[512,512]{1,0:T(8,128)(2,1)S(1)} %get-tuple-element.35.refs_2_, bf16[512,512]{1,0:T(8,128)(2,1)S(1)} %get-tuple-element.24.refs_3_, bf16[512,512]{1,0:T(8,128)(2,1)S(1)} %get-tuple-element.25.refs_4_, ...), custom_call_target="tpu_custom_call" | custom-call | tf_op jit(solution)/shard_map/pallas_call | solution.py:170
  76.6 0.0 collective-permute-done.7.far_ref
  76.6 0.8 shard_map.87
  77.5 0.1 collective-permute-start.8
  77.6 1.2 %collective-permute-start.9 = (bf16[144,512]{1,0:T(8,128)(2,1)S(1)}, bf16[144,512]{1,0:T(8,128)(2,1)S(1)}, u32[]{:S(2)}, u32[]{:S(2)}) collective-permute-start(bf16[144,512]{1,0:T(8,128)(2,1)S(1)} %get-tuple-element.38), channel_id=1, source_target_pairs={{0,2},{1,3},{2,0},{3,1},{4,6},{5,7},{6,4},{7,5},{8,10},{9,11},{10,... | collective-permute-start | bytes 442376 | tf_op jit(solution)/shard_map/ppermute | solution.py:24
  78.8 1.4 %collective-permute-start.10 = (bf16[144,512]{1,0:T(8,128)(2,1)S(1)}, bf16[144,512]{1,0:T(8,128)(2,1)S(1)}, u32[]{:S(2)}, u32[]{:S(2)}) collective-permute-start(bf16[144,512]{1,0:T(8,128)(2,1)S(1)} %get-tuple-element.39), channel_id=1, source_target_pairs={{0,3},{1,0},{2,1},{3,2},{4,7},{5,4},{6,5},{7,6},{8,11},{9,8},{10,9... | collective-permute-start | bytes 442376 | tf_op jit(solution)/shard_map/ppermute | solution.py:24
  80.3 6.6 %collective-permute-done.8.refs_1_ = bf16[144,512]{1,0:T(8,128)(2,1)S(1)} collective-permute-done((bf16[144,512]{1,0:T(8,128)(2,1)S(1)}, bf16[144,512]{1,0:T(8,128)(2,1)S(1)}, u32[]{:S(2)}, u32[]{:S(2)}) %collective-permute-start.8) | collective-permute-done | bytes 147488 | tf_op jit(solution)/shard_map/ppermute | solution.py:24
  86.9 0.0 collective-permute-start.11
  86.9 0.0 collective-permute-done.9.refs_2_
  86.9 0.0 collective-permute-start.12
  86.9 0.9 collective-permute-done.10.refs_3_
  87.8 0.2 collective-permute-start.13
  88.0 8.5 %collective-permute-done.11.refs_4_ = bf16[144,512]{1,0:T(8,128)(2,1)S(1)} collective-permute-done((bf16[144,512]{1,0:T(8,128)(2,1)S(1)}, bf16[144,512]{1,0:T(8,128)(2,1)S(1)}, u32[]{:S(2)}, u32[]{:S(2)}) %collective-permute-start.11) | collective-permute-done | bytes 147488 | tf_op jit(solution)/shard_map/ppermute | solution.py:34
  96.5 1.4 %collective-permute-start.14 = (bf16[144,512]{1,0:T(8,128)(2,1)S(1)}, bf16[144,512]{1,0:T(8,128)(2,1)S(1)}, u32[]{:S(2)}, u32[]{:S(2)}) collective-permute-start(bf16[144,512]{1,0:T(8,128)(2,1)S(1)} %get-tuple-element.34), channel_id=1, source_target_pairs={{0,19},{1,16},{2,17},{3,18},{8,27},{9,24},{10,25},{11,26},{16,35},... | collective-permute-start | bytes 442376 | tf_op jit(solution)/shard_map/ppermute | solution.py:34
  97.9 0.0 collective-permute-done.12.refs_5_
  98.0 2.4 %collective-permute-done.13.refs_6_ = bf16[144,512]{1,0:T(8,128)(2,1)S(1)} collective-permute-done((bf16[144,512]{1,0:T(8,128)(2,1)S(1)}, bf16[144,512]{1,0:T(8,128)(2,1)S(1)}, u32[]{:S(2)}, u32[]{:S(2)}) %collective-permute-start.13) | collective-permute-done | bytes 147488 | tf_op jit(solution)/shard_map/ppermute | solution.py:34
  100.4 3.8 %collective-permute-done.14.refs_7_ = bf16[144,512]{1,0:T(8,128)(2,1)S(1)} collective-permute-done((bf16[144,512]{1,0:T(8,128)(2,1)S(1)}, bf16[144,512]{1,0:T(8,128)(2,1)S(1)}, u32[]{:S(2)}, u32[]{:S(2)}) %collective-permute-start.14) | collective-permute-done | bytes 147488 | tf_op jit(solution)/shard_map/ppermute | solution.py:34
  104.2 0.0 collective-permute-done.17.refs_12_
  104.2 0.0 collective-permute-done.15.refs_10_
  104.2 1.9 %shard_map.89 = bf16[64,2048]{1,0:T(8,128)(2,1)S(1)} custom-call(bf16[144,512]{1,0:T(8,128)(2,1)S(1)} %get-tuple-element.36.refs_0_, bf16[144,512]{1,0:T(8,128)(2,1)S(1)} %collective-permute-done.8.refs_1_, bf16[144,512]{1,0:T(8,128)(2,1)S(1)} %collective-permute-done.9.refs_2_, bf16[144,512]{1,0:T(8,128)(2,1)S(1)} %collective-permute-done.10.refs_3_, ...), custom_call_target="tpu_custom_call" | custom-call | tf_op jit(solution)/shard_map/pallas_call | solution.py:170
  106.1 1.0 collective-permute-start.18
  107.1 1.9 %shard_map.88 = bf16[64,2048]{1,0:T(8,128)(2,1)S(1)} custom-call(bf16[144,512]{1,0:T(8,128)(2,1)S(1)} %get-tuple-element.36.refs_0_, bf16[144,512]{1,0:T(8,128)(2,1)S(1)} %collective-permute-done.8.refs_1_, bf16[144,512]{1,0:T(8,128)(2,1)S(1)} %collective-permute-done.9.refs_2_, bf16[144,512]{1,0:T(8,128)(2,1)S(1)} %collective-permute-done.10.refs_3_, ...), custom_call_target="tpu_custom_call" | custom-call | tf_op jit(solution)/shard_map/pallas_call | solution.py:170
  109.0 4.9 %collective-permute-done.18 = bf16[64,2048]{1,0:T(8,128)(2,1)S(1)} collective-permute-done((bf16[64,2048]{1,0:T(8,128)(2,1)S(1)}, bf16[64,2048]{1,0:T(8,128)(2,1)S(1)}, u32[]{:S(2)}, u32[]{:S(2)}) %collective-permute-start.18) | collective-permute-done | bytes 262176 | tf_op jit(solution)/shard_map/ppermute | solution.py:38
  113.9 0.8 add_convert_fusion
Async XLA Ops:
  0.0 12.8 %copy-start.1 = (s32[1,4]{1,0:T(1,128)S(1)}, s32[1,4]{1,0:T(1,128)}, u32[]{:S(2)}) copy-start(s32[1,4]{1,0:T(1,128)} %refs_0_.5) | copy-start | bytes 52
  0.0 12.8 %copy-start = (s32[32]{0:T(128)S(1)}, s32[32]{0:T(128)}, u32[]{:S(2)}) copy-start(s32[32]{0:T(128)} %refs_1_.9) | copy-start | bytes 388
  0.0 26.6 %collective-permute-start.6 = (bf16[512,2048]{1,0:T(8,128)(2,1)}, bf16[512,2048]{1,0:T(8,128)(2,1)S(1)}, u32[]{:S(2)}, u32[]{:S(2)}) collective-permute-start(bf16[512,2048]{1,0:T(8,128)(2,1)} %refs_2_.1), channel_id=1, source_target_pairs={{0,1},{1,2},{2,3},{3,0},{8,11},{9,8},{10,9},{11,10},{4,5},{5,6},{6... | collective-permute-start | bytes 6291464 | tf_op jit(solution)/shard_map/ppermute | solution.py:45
  3.3 9.5 %collective-permute-start = (bf16[1024,512]{1,0:T(8,128)(2,1)}, bf16[1024,512]{1,0:T(8,128)(2,1)S(1)}, u32[]{:S(2)}, u32[]{:S(2)}) collective-permute-start(bf16[1024,512]{1,0:T(8,128)(2,1)} %refs_0_.3), channel_id=1, source_target_pairs={{0,8},{8,0},{1,9},{9,1},{2,10},{10,2},{3,11},{11,3},{4,12},{12,4},... | collective-permute-start | bytes 3145736 | tf_op jit(solution)/shard_map/ppermute | solution.py:38
  3.3 9.5 %collective-permute-start.1 = (bf16[1024,512]{1,0:T(8,128)(2,1)}, bf16[1024,512]{1,0:T(8,128)(2,1)S(1)}, u32[]{:S(2)}, u32[]{:S(2)}) collective-permute-start(bf16[1024,512]{1,0:T(8,128)(2,1)} %refs_1_.5), channel_id=1, source_target_pairs={{0,8},{8,0},{1,9},{9,1},{2,10},{10,2},{3,11},{11,3},{4,12},{12,4},... | collective-permute-start | bytes 3145736 | tf_op jit(solution)/shard_map/ppermute | solution.py:38
  3.8 17.2 %collective-permute-start.5 = (bf16[512,512]{1,0:T(8,128)(2,1)}, bf16[512,512]{1,0:T(8,128)(2,1)S(1)}, u32[]{:S(2)}, u32[]{:S(2)}) collective-permute-start(bf16[512,512]{1,0:T(8,128)(2,1)} %refs_3_.1), channel_id=1, source_target_pairs={{0,224},{8,232},{16,240},{24,248},{32,0},{40,8},{48,16},{56,24},{6... | collective-permute-start | bytes 1572872 | tf_op jit(solution)/shard_map/ppermute | solution.py:24
  9.4 11.6 %collective-permute-start.4 = (s32[1,4]{1,0:T(1,128)}, s32[1,4]{1,0:T(1,128)S(1)}, u32[]{:S(2)}, u32[]{:S(2)}) collective-permute-start(s32[1,4]{1,0:T(1,128)} %refs_0_.5), channel_id=1, source_target_pairs={{0,224},{8,232},{16,240},{24,248},{32,0},{40,8},{48,16},{56,24},{6... | collective-permute-start | bytes 56 | tf_op jit(solution)/shard_map/ppermute | solution.py:24
  22.1 24.7 %copy-start.2 = (bf16[512,512]{1,0:T(8,128)(2,1)S(1)}, bf16[512,512]{1,0:T(8,128)(2,1)}, u32[]{:S(2)}) copy-start(bf16[512,512]{1,0:T(8,128)(2,1)} %refs_3_.1) | copy-start | bytes 1572868
  26.7 14.8 %collective-permute-start.16 = (bf16[256,2048]{1,0:T(8,128)(2,1)S(1)}, bf16[256,2048]{1,0:T(8,128)(2,1)S(1)}, u32[]{:S(2)}, u32[]{:S(2)}) collective-permute-start(bf16[256,2048]{1,0:T(8,128)(2,1)S(1)} %shard_map.84), channel_id=1, source_target_pairs={{0,1},{1,2},{2,3},{3,0},{8,11},{9,8},{10,9},{11,10},{4,5},{5,6},{6... | collective-permute-start | bytes 3145736 | tf_op jit(solution)/shard_map/ppermute | solution.py:45
  29.8 74.4 %collective-permute-start.15 = (bf16[512,2048]{1,0:T(8,128)(2,1)S(1)}, bf16[512,2048]{1,0:T(8,128)(2,1)S(1)}, u32[]{:S(2)}, u32[]{:S(2)}) collective-permute-start(bf16[512,2048]{1,0:T(8,128)(2,1)S(1)} %collective-permute-done.6.weights.refs_9_), channel_id=1, source_target_pairs={{0,8},{8,0},{1,9},{9,1},{2,10},{10,2},{3,11},{11,3},{4,12},{12,4},... | collective-permute-start | bytes 6291464 | tf_op jit(solution)/shard_map/ppermute | solution.py:38
  41.5 62.7 %collective-permute-start.17 = (bf16[256,2048]{1,0:T(8,128)(2,1)S(1)}, bf16[256,2048]{1,0:T(8,128)(2,1)S(1)}, u32[]{:S(2)}, u32[]{:S(2)}) collective-permute-start(bf16[256,2048]{1,0:T(8,128)(2,1)S(1)} %collective-permute-done.16.refs_11_), channel_id=1, source_target_pairs={{0,8},{8,0},{1,9},{9,1},{2,10},{10,2},{3,11},{11,3},{4,12},{12,4},... | collective-permute-start | bytes 3145736 | tf_op jit(solution)/shard_map/ppermute | solution.py:38
  46.8 29.8 %collective-permute-start.7 = (bf16[528,512]{1,0:T(8,128)(2,1)S(1)}, bf16[528,512]{1,0:T(8,128)(2,1)S(1)}, u32[]{:S(2)}, u32[]{:S(2)}) collective-permute-start(bf16[528,512]{1,0:T(8,128)(2,1)S(1)} %shard_map.83), channel_id=1, source_target_pairs={{0,32},{8,40},{16,48},{24,56},{32,64},{40,72},{48,80},{56,88},{64,... | collective-permute-start | bytes 1622024 | tf_op jit(solution)/shard_map/ppermute | solution.py:24
  46.8 16.1 %collective-permute-start.3 = (bf16[512,512]{1,0:T(8,128)(2,1)S(1)}, bf16[512,512]{1,0:T(8,128)(2,1)S(1)}, u32[]{:S(2)}, u32[]{:S(2)}) collective-permute-start(bf16[512,512]{1,0:T(8,128)(2,1)S(1)} %copy-done.2), channel_id=1, source_target_pairs={{0,240},{8,248},{16,0},{24,8},{32,16},{40,24},{48,32},{56,40},{64,... | collective-permute-start | bytes 1572872 | tf_op jit(solution)/shard_map/ppermute | solution.py:24
  51.7 11.2 %collective-permute-start.2 = (s32[1,4]{1,0:T(1,128)S(1)}, s32[1,4]{1,0:T(1,128)S(1)}, u32[]{:S(2)}, u32[]{:S(2)}) collective-permute-start(s32[1,4]{1,0:T(1,128)S(1)} %copy-done.1), channel_id=1, source_target_pairs={{0,240},{8,248},{16,0},{24,8},{32,16},{40,24},{48,32},{56,40},{64,... | collective-permute-start | bytes 56 | tf_op jit(solution)/shard_map/ppermute | solution.py:24
  77.5 9.4 %collective-permute-start.8 = (bf16[144,512]{1,0:T(8,128)(2,1)S(1)}, bf16[144,512]{1,0:T(8,128)(2,1)S(1)}, u32[]{:S(2)}, u32[]{:S(2)}) collective-permute-start(bf16[144,512]{1,0:T(8,128)(2,1)S(1)} %get-tuple-element.37), channel_id=1, source_target_pairs={{0,1},{1,2},{2,3},{3,0},{4,5},{5,6},{6,7},{7,4},{8,9},{9,10},{10,1... | collective-permute-start | bytes 442376 | tf_op jit(solution)/shard_map/ppermute | solution.py:24
  77.6 9.3 %collective-permute-start.9 = (bf16[144,512]{1,0:T(8,128)(2,1)S(1)}, bf16[144,512]{1,0:T(8,128)(2,1)S(1)}, u32[]{:S(2)}, u32[]{:S(2)}) collective-permute-start(bf16[144,512]{1,0:T(8,128)(2,1)S(1)} %get-tuple-element.38), channel_id=1, source_target_pairs={{0,2},{1,3},{2,0},{3,1},{4,6},{5,7},{6,4},{7,5},{8,10},{9,11},{10,... | collective-permute-start | bytes 442376 | tf_op jit(solution)/shard_map/ppermute | solution.py:24
  78.8 9.0 %collective-permute-start.10 = (bf16[144,512]{1,0:T(8,128)(2,1)S(1)}, bf16[144,512]{1,0:T(8,128)(2,1)S(1)}, u32[]{:S(2)}, u32[]{:S(2)}) collective-permute-start(bf16[144,512]{1,0:T(8,128)(2,1)S(1)} %get-tuple-element.39), channel_id=1, source_target_pairs={{0,3},{1,0},{2,1},{3,2},{4,7},{5,4},{6,5},{7,6},{8,11},{9,8},{10,9... | collective-permute-start | bytes 442376 | tf_op jit(solution)/shard_map/ppermute | solution.py:24
  86.9 9.6 %collective-permute-start.11 = (bf16[144,512]{1,0:T(8,128)(2,1)S(1)}, bf16[144,512]{1,0:T(8,128)(2,1)S(1)}, u32[]{:S(2)}, u32[]{:S(2)}) collective-permute-start(bf16[144,512]{1,0:T(8,128)(2,1)S(1)} %get-tuple-element.31), channel_id=1, source_target_pairs={{0,16},{1,17},{2,18},{3,19},{8,24},{9,25},{10,26},{11,27},{16,32},... | collective-permute-start | bytes 442376 | tf_op jit(solution)/shard_map/ppermute | solution.py:34
  86.9 11.1 %collective-permute-start.12 = (bf16[144,512]{1,0:T(8,128)(2,1)S(1)}, bf16[144,512]{1,0:T(8,128)(2,1)S(1)}, u32[]{:S(2)}, u32[]{:S(2)}) collective-permute-start(bf16[144,512]{1,0:T(8,128)(2,1)S(1)} %get-tuple-element.32), channel_id=1, source_target_pairs={{0,17},{1,18},{2,19},{3,16},{8,25},{9,26},{10,27},{11,24},{16,33},... | collective-permute-start | bytes 442376 | tf_op jit(solution)/shard_map/ppermute | solution.py:34
  87.8 12.6 %collective-permute-start.13 = (bf16[144,512]{1,0:T(8,128)(2,1)S(1)}, bf16[144,512]{1,0:T(8,128)(2,1)S(1)}, u32[]{:S(2)}, u32[]{:S(2)}) collective-permute-start(bf16[144,512]{1,0:T(8,128)(2,1)S(1)} %get-tuple-element.33), channel_id=1, source_target_pairs={{0,18},{1,19},{2,16},{3,17},{8,26},{9,27},{10,24},{11,25},{16,34},... | collective-permute-start | bytes 442376 | tf_op jit(solution)/shard_map/ppermute | solution.py:34
  96.5 7.6 %collective-permute-start.14 = (bf16[144,512]{1,0:T(8,128)(2,1)S(1)}, bf16[144,512]{1,0:T(8,128)(2,1)S(1)}, u32[]{:S(2)}, u32[]{:S(2)}) collective-permute-start(bf16[144,512]{1,0:T(8,128)(2,1)S(1)} %get-tuple-element.34), channel_id=1, source_target_pairs={{0,19},{1,16},{2,17},{3,18},{8,27},{9,24},{10,25},{11,26},{16,35},... | collective-permute-start | bytes 442376 | tf_op jit(solution)/shard_map/ppermute | solution.py:34
  106.1 7.8 %collective-permute-start.18 = (bf16[64,2048]{1,0:T(8,128)(2,1)S(1)}, bf16[64,2048]{1,0:T(8,128)(2,1)S(1)}, u32[]{:S(2)}, u32[]{:S(2)}) collective-permute-start(bf16[64,2048]{1,0:T(8,128)(2,1)S(1)} %shard_map.89), channel_id=1, source_target_pairs={{0,4},{4,0},{1,5},{5,1},{2,6},{6,2},{3,7},{7,3},{8,12},{12,8},{9,1... | collective-permute-start | bytes 786440 | tf_op jit(solution)/shard_map/ppermute | solution.py:38

commit v8 on v4

--- a/solution.py
+++ b/solution.py
@@ -298,12 +298,14 @@
 
     home0 = at_home(local, 0)
     from_far, far = guest(after(query_far, home0), offsets_far, 4)
-    from_near, near = guest(after(query_near, far), offsets_near, 2)
-
-    near_weight = after(near_weight, near)
+
+    near_weight = after(near_weight, far)
     passed_on = pass_on(near_weight)
-    home1 = at_home((after(local[0], near, passed_on), *local[1:]), 1)
     far_weight = moved(part_ways, passed_on)
+
+    from_near, near = guest(after(query_near, far, passed_on), offsets_near, 2)
+    home1 = at_home((after(local[0], near), *local[1:]), 1)
+    far_weight = after(far_weight, home1)
     weights = [own_weight, near_weight, moved(swap, near_weight, "core"), far_weight, moved(swap, far_weight, "core")]
 
     mine, *tiles = merge(home0, home1, from_far, from_near)

time: 104 us -> 107 us (1.029)
  waiting for transfers between devices: 46.4 us -> 49.8 us
    ppermute x9, waiting for transfers between devices: 29.8 us -> 41.6 us  [shift(): lax.ppermute(value, axis, [(i, (i + steps) % count) for i in range(count)])]
    ppermute x2, waiting for transfers between devices: 13.3 us -> 4.52 us  [part_ways(): return lax.ppermute(value, ('core', 'x'), up + down)]
    ppermute x5, starting transfers between devices: 13.2 us -> 4.46 us  [swap(): return lax.ppermute(value, axis, [(0, 1), (1, 0)])]
    ppermute x9, starting transfers between devices: 11 us -> 16.4 us  [shift(): lax.ppermute(value, axis, [(i, (i + steps) % count) for i in range(count)])]
    ppermute x2, starting transfers between devices: 3.95 us -> 6.38 us  [part_ways(): return lax.ppermute(value, ('core', 'x'), up + down)]
  transfers between devices with their start and end apart: 16 -> 16, of which waited for: 8 -> 8; matrix products, arithmetic and copies ran while one was open for 0% -> 0% of each run, Pallas kernels for 25% -> 24%
where the time goes in v8:
time: 107 us; the launch traced here: 105 us
  waiting for transfers between devices  49.8 us (47%)
  starting transfers between devices  27.2 us (25%)
  Pallas kernels  27 us (25%)
    ppermute x9, waiting for transfers between devices, shift(): lax.ppermute(value, axis, [(i, (i + steps) % count) for i in range(count)])  41.6 us
    pallas_call x8, Pallas kernels, kernel_call(): pl.pallas_call(kernel, grid_spec=pltpu.PrefetchScalarGridSpec(num_scalar_...  24.3 us
    ppermute x9, starting transfers between devices, shift(): lax.ppermute(value, axis, [(i, (i + steps) % count) for i in range(count)])  16.4 us
    ppermute x2, starting transfers between devices, part_ways(): return lax.ppermute(value, ('core', 'x'), up + down)  6.38 us
    ppermute x2, waiting for transfers between devices, part_ways(): return lax.ppermute(value, ('core', 'x'), up + down)  4.52 us
    ppermute x5, starting transfers between devices, swap(): return lax.ppermute(value, axis, [(0, 1), (1, 0)])  4.46 us
    ppermute x5, waiting for transfers between devices, swap(): return lax.ppermute(value, axis, [(0, 1), (1, 0)])  3.67 us
    pallas_call x1, Pallas kernels, load(): pl.pallas_call(load_kernel, in_specs=[pl.BlockSpec(memory_space=pltpu.HBM...  2.67 us
  transfers between devices with their start and end apart: 16, of which 8 were waited for; matrix products, arithmetic and copies ran while one was open for 0% of the time, Pallas kernels for 24%

profile of v8, /device:TPU:1, one launch (start us, length us, event | category | flops | bytes accessed | tf_op | source)
XLA Modules:
  0.0 105.0 jit_solution(17221663912140729331)
XLA Ops:
  0.0 0.0 copy-start.1
  0.0 0.0 copy-start
  0.0 3.3 %collective-permute-start.6 = (bf16[512,2048]{1,0:T(8,128)(2,1)}, bf16[512,2048]{1,0:T(8,128)(2,1)S(1)}, u32[]{:S(2)}, u32[]{:S(2)}) collective-permute-start(bf16[512,2048]{1,0:T(8,128)(2,1)} %refs_2_.1), channel_id=1, source_target_pairs={{0,1},{1,2},{2,3},{3,0},{8,11},{9,8},{10,9},{11,10},{4,5},{5,6},{6... | collective-permute-start | bytes 6291464 | tf_op jit(solution)/shard_map/ppermute | solution.py:35
  3.3 0.0 collective-permute-start
  3.3 0.5 collective-permute-start.1
  3.8 5.6 %collective-permute-start.5 = (bf16[512,512]{1,0:T(8,128)(2,1)}, bf16[512,512]{1,0:T(8,128)(2,1)S(1)}, u32[]{:S(2)}, u32[]{:S(2)}) collective-permute-start(bf16[512,512]{1,0:T(8,128)(2,1)} %refs_3_.1), channel_id=1, source_target_pairs={{0,224},{8,232},{16,240},{24,248},{32,0},{40,8},{48,16},{56,24},{6... | collective-permute-start | bytes 1572872 | tf_op jit(solution)/shard_map/ppermute | solution.py:24
  9.4 0.7 collective-permute-start.4
  10.1 2.7 %load.1 = (bf16[1024,512]{1,0:T(8,128)(2,1)S(1)}, bf16[1024,512]{1,0:T(8,128)(2,1)S(1)}, bf16[512,2048]{1,0:T(8,128)(2,1)S(1)}, bf16[512,512]{1,0:T(8,128)(2,1)S...) custom-call(bf16[1024,512]{1,0:T(8,128)(2,1)} %refs_0_.3, bf16[1024,512]{1,0:T(8,128)(2,1)} %refs_1_.5, ...), custom_call_target="tpu_custom_call" | custom-call | tf_op jit(solution)/shard_map/load/pallas_call | solution.py:177
  12.8 0.0 collective-permute-done.refs_7_.refs_5_
  12.8 0.0 collective-permute-done.1.refs_8_.refs_6_
  12.8 0.0 copy-done.1
  12.8 0.0 copy-done
  12.8 5.4 %shard_map.82.refs_0_ = bf16[272,512]{1,0:T(8,128)(2,1)S(1)} custom-call(s32[1,4]{1,0:T(1,128)S(1)} %copy-done.1, s32[32]{0:T(128)S(1)} %copy-done, bf16[512,512]{1,0:T(8,128)(2,1)S(1)} %get-tuple-element.28.refs_2_, bf16[512,512]{1,0:T(8,128)(2,1)S(1)} %get-tuple-element.21.refs_3_, bf16[512,512]{1,0:T(8,128)(2,1)S(1)} %get-tuple-element.22.refs_4_, ...), custom_call_target="tpu_custom_call" | custom-call | tf_op jit(solution)/shard_map/pallas_call | solution.py:142
  18.3 2.7 %collective-permute-done.5.refs_2_ = bf16[512,512]{1,0:T(8,128)(2,1)S(1)} collective-permute-done((bf16[512,512]{1,0:T(8,128)(2,1)}, bf16[512,512]{1,0:T(8,128)(2,1)S(1)}, u32[]{:S(2)}, u32[]{:S(2)}) %collective-permute-start.5) | collective-permute-done | bytes 524320 | tf_op jit(solution)/shard_map/ppermute | solution.py:24
  21.0 0.0 collective-permute-done.4.refs_0_
  21.0 1.1 %shard_map.83 = bf16[528,512]{1,0:T(8,128)(2,1)S(1)} custom-call(s32[1,4]{1,0:T(1,128)S(1)} %collective-permute-done.4.refs_0_, s32[32]{0:T(128)S(1)} %copy-done, bf16[512,512]{1,0:T(8,128)(2,1)S(1)} %collective-permute-done.5.refs_2_, bf16[1024,512]{1,0:T(8,128)(2,1)S(1)} %get-tuple-element.23.refs_5_.refs_3_, ...), custom_call_target="tpu_custom_call" | custom-call | tf_op jit(solution)/shard_map/pallas_call | solution.py:142
  22.1 0.0 copy-start.2
  22.1 4.5 %collective-permute-done.6.weights.refs_5_ = bf16[512,2048]{1,0:T(8,128)(2,1)S(1)} collective-permute-done((bf16[512,2048]{1,0:T(8,128)(2,1)}, bf16[512,2048]{1,0:T(8,128)(2,1)S(1)}, u32[]{:S(2)}, u32[]{:S(2)}) %collective-permute-start.6) | collective-permute-done | bytes 2097184 | tf_op jit(solution)/shard_map/ppermute | solution.py:35
  26.6 0.1 shard_map.84
  26.7 3.1 %collective-permute-start.13 = (bf16[256,2048]{1,0:T(8,128)(2,1)S(1)}, bf16[256,2048]{1,0:T(8,128)(2,1)S(1)}, u32[]{:S(2)}, u32[]{:S(2)}) collective-permute-start(bf16[256,2048]{1,0:T(8,128)(2,1)S(1)} %shard_map.84), channel_id=1, source_target_pairs={{0,1},{1,2},{2,3},{3,0},{8,11},{9,8},{10,9},{11,10},{4,5},{5,6},{6... | collective-permute-start | bytes 3145736 | tf_op jit(solution)/shard_map/ppermute | solution.py:35
  29.8 1.2 %collective-permute-start.12 = (bf16[512,2048]{1,0:T(8,128)(2,1)S(1)}, bf16[512,2048]{1,0:T(8,128)(2,1)S(1)}, u32[]{:S(2)}, u32[]{:S(2)}) collective-permute-start(bf16[512,2048]{1,0:T(8,128)(2,1)S(1)} %collective-permute-done.6.weights.refs_5_), channel_id=1, source_target_pairs={{0,8},{8,0},{1,9},{9,1},{2,10},{10,2},{3,11},{11,3},{4,12},{12,4},... | collective-permute-start | bytes 6291464 | tf_op jit(solution)/shard_map/ppermute | solution.py:28
  30.9 0.0 copy-done.2
  30.9 5.4 %collective-permute-start.3 = (bf16[512,512]{1,0:T(8,128)(2,1)S(1)}, bf16[512,512]{1,0:T(8,128)(2,1)S(1)}, u32[]{:S(2)}, u32[]{:S(2)}) collective-permute-start(bf16[512,512]{1,0:T(8,128)(2,1)S(1)} %copy-done.2), channel_id=1, source_target_pairs={{0,240},{8,248},{16,0},{24,8},{32,16},{40,24},{48,32},{56,40},{64,... | collective-permute-start | bytes 1572872 | tf_op jit(solution)/shard_map/ppermute | solution.py:24
  36.4 0.3 collective-permute-start.2
  36.6 10.5 %collective-permute-done.3.refs_2_ = bf16[512,512]{1,0:T(8,128)(2,1)S(1)} collective-permute-done((bf16[512,512]{1,0:T(8,128)(2,1)S(1)}, bf16[512,512]{1,0:T(8,128)(2,1)S(1)}, u32[]{:S(2)}, u32[]{:S(2)}) %collective-permute-start.3) | collective-permute-done | bytes 524320 | tf_op jit(solution)/shard_map/ppermute | solution.py:24
  47.1 0.0 collective-permute-done.2.refs_0_
  47.2 7.7 %shard_map.85 = bf16[528,512]{1,0:T(8,128)(2,1)S(1)} custom-call(s32[1,4]{1,0:T(1,128)S(1)} %collective-permute-done.2.refs_0_, s32[32]{0:T(128)S(1)} %copy-done, bf16[512,512]{1,0:T(8,128)(2,1)S(1)} %collective-permute-done.3.refs_2_, bf16[1024,512]{1,0:T(8,128)(2,1)S(1)} %get-tuple-element.23.refs_5_.refs_3_, ...), custom_call_target="tpu_custom_call" | custom-call | tf_op jit(solution)/shard_map/pallas_call | solution.py:142
  54.9 5.8 %shard_map.86.refs_1_ = bf16[272,512]{1,0:T(8,128)(2,1)S(1)} custom-call(s32[1,4]{1,0:T(1,128)S(1)} %copy-done.1, s32[32]{0:T(128)S(1)} %copy-done, bf16[512,512]{1,0:T(8,128)(2,1)S(1)} %get-tuple-element.28.refs_2_, bf16[512,512]{1,0:T(8,128)(2,1)S(1)} %get-tuple-element.21.refs_3_, bf16[512,512]{1,0:T(8,128)(2,1)S(1)} %get-tuple-element.22.refs_4_, ...), custom_call_target="tpu_custom_call" | custom-call | tf_op jit(solution)/shard_map/pallas_call | solution.py:142
  60.7 0.0 collective-permute-done.13.refs_7_
  60.7 0.1 collective-permute-start.14
  60.8 0.1 collective-permute-start.7
  60.9 0.1 collective-permute-start.8
  61.0 14.5 %collective-permute-done.7.refs_2_ = bf16[528,512]{1,0:T(8,128)(2,1)S(1)} collective-permute-done((bf16[528,512]{1,0:T(8,128)(2,1)S(1)}, bf16[528,512]{1,0:T(8,128)(2,1)S(1)}, u32[]{:S(2)}, u32[]{:S(2)}) %collective-permute-start.7) | collective-permute-done | bytes 540704 | tf_op jit(solution)/shard_map/ppermute | solution.py:24
  75.5 8.8 %collective-permute-done.8.refs_3_ = bf16[528,512]{1,0:T(8,128)(2,1)S(1)} collective-permute-done((bf16[528,512]{1,0:T(8,128)(2,1)S(1)}, bf16[528,512]{1,0:T(8,128)(2,1)S(1)}, u32[]{:S(2)}, u32[]{:S(2)}) %collective-permute-start.8) | collective-permute-done | bytes 540704 | tf_op jit(solution)/shard_map/ppermute | solution.py:24
  84.3 1.1 %shard_map.87 = (bf16[128,512]{1,0:T(8,128)(2,1)S(1)}, bf16[128,512]{1,0:T(8,128)(2,1)S(1)}, bf16[128,512]{1,0:T(8,128)(2,1)S(1)}, bf16[128,512]{1,0:T(8,128)(2,1)S(1)}) custom-call(bf16[272,512]{1,0:T(8,128)(2,1)S(1)} %shard_map.82.refs_0_, bf16[272,512]{1,0:T(8,128)(2,1)S(1)} %shard_map.86.refs_1_, bf16[528,512]{1,0:T(8,128)(2,1)S(1)} %collective-permute-done.7.refs_2_, ...), custom_call_target="tpu_custom_call" | custom-call | tf_op jit(solution)/shard_map/pallas_call | solution.py:142
  85.4 0.9 collective-permute-start.9
  86.3 2.6 %collective-permute-start.10 = (bf16[128,512]{1,0:T(8,128)(2,1)S(1)}, bf16[128,512]{1,0:T(8,128)(2,1)S(1)}, u32[]{:S(2)}, u32[]{:S(2)}) collective-permute-start(bf16[128,512]{1,0:T(8,128)(2,1)S(1)} %get-tuple-element.31), channel_id=1, source_target_pairs={{0,2},{1,3},{2,0},{3,1},{4,6},{5,7},{6,4},{7,5},{8,10},{9,11},{10,... | collective-permute-start | bytes 393224 | tf_op jit(solution)/shard_map/ppermute | solution.py:24
  89.0 0.7 collective-permute-start.11
  89.6 1.5 %collective-permute-done.9.refs_1_ = bf16[128,512]{1,0:T(8,128)(2,1)S(1)} collective-permute-done((bf16[128,512]{1,0:T(8,128)(2,1)S(1)}, bf16[128,512]{1,0:T(8,128)(2,1)S(1)}, u32[]{:S(2)}, u32[]{:S(2)}) %collective-permute-start.9) | collective-permute-done | bytes 131104 | tf_op jit(solution)/shard_map/ppermute | solution.py:24
  91.1 3.6 %collective-permute-done.10.refs_2_ = bf16[128,512]{1,0:T(8,128)(2,1)S(1)} collective-permute-done((bf16[128,512]{1,0:T(8,128)(2,1)S(1)}, bf16[128,512]{1,0:T(8,128)(2,1)S(1)}, u32[]{:S(2)}, u32[]{:S(2)}) %collective-permute-start.10) | collective-permute-done | bytes 131104 | tf_op jit(solution)/shard_map/ppermute | solution.py:24
  94.7 0.0 collective-permute-done.11.refs_3_
  94.7 0.0 collective-permute-done.14.refs_8_
  94.7 0.0 collective-permute-done.12.refs_6_
  94.7 1.6 %shard_map.89 = bf16[64,2048]{1,0:T(8,128)(2,1)S(1)} custom-call(bf16[128,512]{1,0:T(8,128)(2,1)S(1)} %get-tuple-element.29.refs_0_, bf16[128,512]{1,0:T(8,128)(2,1)S(1)} %collective-permute-done.9.refs_1_, bf16[128,512]{1,0:T(8,128)(2,1)S(1)} %collective-permute-done.10.refs_2_, bf16[128,512]{1,0:T(8,128)(2,1)S(1)} %collective-permute-done.11.refs_3_, ...), custom_call_target="tpu_custom_call" | custom-call | tf_op jit(solution)/shard_map/pallas_call | solution.py:142
  96.3 2.7 %collective-permute-start.15 = (bf16[64,2048]{1,0:T(8,128)(2,1)S(1)}, bf16[64,2048]{1,0:T(8,128)(2,1)S(1)}, u32[]{:S(2)}, u32[]{:S(2)}) collective-permute-start(bf16[64,2048]{1,0:T(8,128)(2,1)S(1)} %shard_map.89), channel_id=1, source_target_pairs={{0,4},{4,0},{1,5},{5,1},{2,6},{6,2},{3,7},{7,3},{8,12},{12,8},{9,1... | collective-permute-start | bytes 786440 | tf_op jit(solution)/shard_map/ppermute | solution.py:28
  99.0 1.6 %shard_map.88 = bf16[64,2048]{1,0:T(8,128)(2,1)S(1)} custom-call(bf16[128,512]{1,0:T(8,128)(2,1)S(1)} %get-tuple-element.29.refs_0_, bf16[128,512]{1,0:T(8,128)(2,1)S(1)} %collective-permute-done.9.refs_1_, bf16[128,512]{1,0:T(8,128)(2,1)S(1)} %collective-permute-done.10.refs_2_, bf16[128,512]{1,0:T(8,128)(2,1)S(1)} %collective-permute-done.11.refs_3_, ...), custom_call_target="tpu_custom_call" | custom-call | tf_op jit(solution)/shard_map/pallas_call | solution.py:142
  100.5 3.7 %collective-permute-done.15 = bf16[64,2048]{1,0:T(8,128)(2,1)S(1)} collective-permute-done((bf16[64,2048]{1,0:T(8,128)(2,1)S(1)}, bf16[64,2048]{1,0:T(8,128)(2,1)S(1)}, u32[]{:S(2)}, u32[]{:S(2)}) %collective-permute-start.15) | collective-permute-done | bytes 262176 | tf_op jit(solution)/shard_map/ppermute | solution.py:28
  104.2 0.8 add_convert_fusion
Async XLA Ops:
  0.0 12.8 %copy-start.1 = (s32[1,4]{1,0:T(1,128)S(1)}, s32[1,4]{1,0:T(1,128)}, u32[]{:S(2)}) copy-start(s32[1,4]{1,0:T(1,128)} %refs_0_.5) | copy-start | bytes 52
  0.0 12.8 %copy-start = (s32[32]{0:T(128)S(1)}, s32[32]{0:T(128)}, u32[]{:S(2)}) copy-start(s32[32]{0:T(128)} %refs_1_.9) | copy-start | bytes 388
  0.0 26.6 %collective-permute-start.6 = (bf16[512,2048]{1,0:T(8,128)(2,1)}, bf16[512,2048]{1,0:T(8,128)(2,1)S(1)}, u32[]{:S(2)}, u32[]{:S(2)}) collective-permute-start(bf16[512,2048]{1,0:T(8,128)(2,1)} %refs_2_.1), channel_id=1, source_target_pairs={{0,1},{1,2},{2,3},{3,0},{8,11},{9,8},{10,9},{11,10},{4,5},{5,6},{6... | collective-permute-start | bytes 6291464 | tf_op jit(solution)/shard_map/ppermute | solution.py:35
  3.3 9.5 %collective-permute-start = (bf16[1024,512]{1,0:T(8,128)(2,1)}, bf16[1024,512]{1,0:T(8,128)(2,1)S(1)}, u32[]{:S(2)}, u32[]{:S(2)}) collective-permute-start(bf16[1024,512]{1,0:T(8,128)(2,1)} %refs_0_.3), channel_id=1, source_target_pairs={{0,8},{8,0},{1,9},{9,1},{2,10},{10,2},{3,11},{11,3},{4,12},{12,4},... | collective-permute-start | bytes 3145736 | tf_op jit(solution)/shard_map/ppermute | solution.py:28
  3.3 9.5 %collective-permute-start.1 = (bf16[1024,512]{1,0:T(8,128)(2,1)}, bf16[1024,512]{1,0:T(8,128)(2,1)S(1)}, u32[]{:S(2)}, u32[]{:S(2)}) collective-permute-start(bf16[1024,512]{1,0:T(8,128)(2,1)} %refs_1_.5), channel_id=1, source_target_pairs={{0,8},{8,0},{1,9},{9,1},{2,10},{10,2},{3,11},{11,3},{4,12},{12,4},... | collective-permute-start | bytes 3145736 | tf_op jit(solution)/shard_map/ppermute | solution.py:28
  3.8 17.2 %collective-permute-start.5 = (bf16[512,512]{1,0:T(8,128)(2,1)}, bf16[512,512]{1,0:T(8,128)(2,1)S(1)}, u32[]{:S(2)}, u32[]{:S(2)}) collective-permute-start(bf16[512,512]{1,0:T(8,128)(2,1)} %refs_3_.1), channel_id=1, source_target_pairs={{0,224},{8,232},{16,240},{24,248},{32,0},{40,8},{48,16},{56,24},{6... | collective-permute-start | bytes 1572872 | tf_op jit(solution)/shard_map/ppermute | solution.py:24
  9.4 11.6 %collective-permute-start.4 = (s32[1,4]{1,0:T(1,128)}, s32[1,4]{1,0:T(1,128)S(1)}, u32[]{:S(2)}, u32[]{:S(2)}) collective-permute-start(s32[1,4]{1,0:T(1,128)} %refs_0_.5), channel_id=1, source_target_pairs={{0,224},{8,232},{16,240},{24,248},{32,0},{40,8},{48,16},{56,24},{6... | collective-permute-start | bytes 56 | tf_op jit(solution)/shard_map/ppermute | solution.py:24
  22.1 8.8 %copy-start.2 = (bf16[512,512]{1,0:T(8,128)(2,1)S(1)}, bf16[512,512]{1,0:T(8,128)(2,1)}, u32[]{:S(2)}) copy-start(bf16[512,512]{1,0:T(8,128)(2,1)} %refs_3_.1) | copy-start | bytes 1572868
  26.7 34.0 %collective-permute-start.13 = (bf16[256,2048]{1,0:T(8,128)(2,1)S(1)}, bf16[256,2048]{1,0:T(8,128)(2,1)S(1)}, u32[]{:S(2)}, u32[]{:S(2)}) collective-permute-start(bf16[256,2048]{1,0:T(8,128)(2,1)S(1)} %shard_map.84), channel_id=1, source_target_pairs={{0,1},{1,2},{2,3},{3,0},{8,11},{9,8},{10,9},{11,10},{4,5},{5,6},{6... | collective-permute-start | bytes 3145736 | tf_op jit(solution)/shard_map/ppermute | solution.py:35
  29.8 65.0 %collective-permute-start.12 = (bf16[512,2048]{1,0:T(8,128)(2,1)S(1)}, bf16[512,2048]{1,0:T(8,128)(2,1)S(1)}, u32[]{:S(2)}, u32[]{:S(2)}) collective-permute-start(bf16[512,2048]{1,0:T(8,128)(2,1)S(1)} %collective-permute-done.6.weights.refs_5_), channel_id=1, source_target_pairs={{0,8},{8,0},{1,9},{9,1},{2,10},{10,2},{3,11},{11,3},{4,12},{12,4},... | collective-permute-start | bytes 6291464 | tf_op jit(solution)/shard_map/ppermute | solution.py:28
  30.9 16.2 %collective-permute-start.3 = (bf16[512,512]{1,0:T(8,128)(2,1)S(1)}, bf16[512,512]{1,0:T(8,128)(2,1)S(1)}, u32[]{:S(2)}, u32[]{:S(2)}) collective-permute-start(bf16[512,512]{1,0:T(8,128)(2,1)S(1)} %copy-done.2), channel_id=1, source_target_pairs={{0,240},{8,248},{16,0},{24,8},{32,16},{40,24},{48,32},{56,40},{64,... | collective-permute-start | bytes 1572872 | tf_op jit(solution)/shard_map/ppermute | solution.py:24
  36.4 10.8 %collective-permute-start.2 = (s32[1,4]{1,0:T(1,128)S(1)}, s32[1,4]{1,0:T(1,128)S(1)}, u32[]{:S(2)}, u32[]{:S(2)}) collective-permute-start(s32[1,4]{1,0:T(1,128)S(1)} %copy-done.1), channel_id=1, source_target_pairs={{0,240},{8,248},{16,0},{24,8},{32,16},{40,24},{48,32},{56,40},{64,... | collective-permute-start | bytes 56 | tf_op jit(solution)/shard_map/ppermute | solution.py:24
  60.7 34.0 %collective-permute-start.14 = (bf16[256,2048]{1,0:T(8,128)(2,1)S(1)}, bf16[256,2048]{1,0:T(8,128)(2,1)S(1)}, u32[]{:S(2)}, u32[]{:S(2)}) collective-permute-start(bf16[256,2048]{1,0:T(8,128)(2,1)S(1)} %collective-permute-done.13.refs_7_), channel_id=1, source_target_pairs={{0,8},{8,0},{1,9},{9,1},{2,10},{10,2},{3,11},{11,3},{4,12},{12,4},... | collective-permute-start | bytes 3145736 | tf_op jit(solution)/shard_map/ppermute | solution.py:28
  60.8 14.7 %collective-permute-start.7 = (bf16[528,512]{1,0:T(8,128)(2,1)S(1)}, bf16[528,512]{1,0:T(8,128)(2,1)S(1)}, u32[]{:S(2)}, u32[]{:S(2)}) collective-permute-start(bf16[528,512]{1,0:T(8,128)(2,1)S(1)} %shard_map.83), channel_id=1, source_target_pairs={{0,32},{8,40},{16,48},{24,56},{32,64},{40,72},{48,80},{56,88},{64,... | collective-permute-start | bytes 1622024 | tf_op jit(solution)/shard_map/ppermute | solution.py:24
  60.9 23.4 %collective-permute-start.8 = (bf16[528,512]{1,0:T(8,128)(2,1)S(1)}, bf16[528,512]{1,0:T(8,128)(2,1)S(1)}, u32[]{:S(2)}, u32[]{:S(2)}) collective-permute-start(bf16[528,512]{1,0:T(8,128)(2,1)S(1)} %shard_map.85), channel_id=1, source_target_pairs={{0,16},{8,24},{16,32},{24,40},{32,48},{40,56},{48,64},{56,72},{64,... | collective-permute-start | bytes 1622024 | tf_op jit(solution)/shard_map/ppermute | solution.py:24
  85.4 5.7 %collective-permute-start.9 = (bf16[128,512]{1,0:T(8,128)(2,1)S(1)}, bf16[128,512]{1,0:T(8,128)(2,1)S(1)}, u32[]{:S(2)}, u32[]{:S(2)}) collective-permute-start(bf16[128,512]{1,0:T(8,128)(2,1)S(1)} %get-tuple-element.30), channel_id=1, source_target_pairs={{0,1},{1,2},{2,3},{3,0},{4,5},{5,6},{6,7},{7,4},{8,9},{9,10},{10,1... | collective-permute-start | bytes 393224 | tf_op jit(solution)/shard_map/ppermute | solution.py:24
  86.3 8.4 %collective-permute-start.10 = (bf16[128,512]{1,0:T(8,128)(2,1)S(1)}, bf16[128,512]{1,0:T(8,128)(2,1)S(1)}, u32[]{:S(2)}, u32[]{:S(2)}) collective-permute-start(bf16[128,512]{1,0:T(8,128)(2,1)S(1)} %get-tuple-element.31), channel_id=1, source_target_pairs={{0,2},{1,3},{2,0},{3,1},{4,6},{5,7},{6,4},{7,5},{8,10},{9,11},{10,... | collective-permute-start | bytes 393224 | tf_op jit(solution)/shard_map/ppermute | solution.py:24
  89.0 5.7 %collective-permute-start.11 = (bf16[128,512]{1,0:T(8,128)(2,1)S(1)}, bf16[128,512]{1,0:T(8,128)(2,1)S(1)}, u32[]{:S(2)}, u32[]{:S(2)}) collective-permute-start(bf16[128,512]{1,0:T(8,128)(2,1)S(1)} %get-tuple-element.32), channel_id=1, source_target_pairs={{0,3},{1,0},{2,1},{3,2},{4,7},{5,4},{6,5},{7,6},{8,11},{9,8},{10,9... | collective-permute-start | bytes 393224 | tf_op jit(solution)/shard_map/ppermute | solution.py:24
  96.3 7.9 %collective-permute-start.15 = (bf16[64,2048]{1,0:T(8,128)(2,1)S(1)}, bf16[64,2048]{1,0:T(8,128)(2,1)S(1)}, u32[]{:S(2)}, u32[]{:S(2)}) collective-permute-start(bf16[64,2048]{1,0:T(8,128)(2,1)S(1)} %shard_map.89), channel_id=1, source_target_pairs={{0,4},{4,0},{1,5},{5,1},{2,6},{6,2},{3,7},{7,3},{8,12},{12,8},{9,1... | collective-permute-start | bytes 786440 | tf_op jit(solution)/shard_map/ppermute | solution.py:28
